TPU v7x, 32 devices: a whole 2x2x4 slice. The times are simulated.
32 devices in a mesh: dp: 16 (over z, x, core), pair: 2 (over y).
Axes of the slice: x: 2, y: 2, z: 4, core: 2. Of those that a mesh axis runs over, the one named last changes fastest.
Arguments:
- hidden: bfloat16 [64, 64, 768], P(('dp', 'pair')), may hold values from -12 to 12
- features: bfloat16 [64, 257, 1408], P(('dp', 'pair')), may hold values from -6 to 6
- text_lengths: int32 [64], P(('dp', 'pair')), may hold values from 1 to 32
- cotangent: bfloat16 [64, 64, 768], P(('dp', 'pair')), may hold values from -12 to 12
- self_project: bfloat16 [3, 768, 768], P(None, ('dp', 'pair')), may hold values from -0.21875 to 0.21875
- self_output: bfloat16 [768, 768], P(('dp', 'pair')), may hold values from -0.625 to 0.625
- self_bias: bfloat16 [3, 768], P(None, ('dp', 'pair')), may hold values from -3 to 3
- norm_gain: bfloat16 [4, 768], P(None, ('dp', 'pair')), may hold values from 0.25 to 1.75
- norm_bias: bfloat16 [4, 768], P(None, ('dp', 'pair')), may hold values from -3 to 3
- cross_query: bfloat16 [768, 768], P(('dp', 'pair')), may hold values from -0.21875 to 0.21875
- cross_output: bfloat16 [768, 768], P(('dp', 'pair')), may hold values from -0.75 to 0.75
- image_project: bfloat16 [2, 1408, 768], P(None, None, ('dp', 'pair')), may hold values from -0.15625 to 0.15625
- cross_bias: bfloat16 [3, 768], P(None, ('dp', 'pair')), may hold values from -3 to 3
- expand_weight: bfloat16 [2, 768, 3072], P(None, None, ('dp', 'pair')), may hold values from -0.21875 to 0.21875
- expand_bias: bfloat16 [2, 3072], P(None, ('dp', 'pair')), may hold values from -3 to 3
- reduce_weight: bfloat16 [2, 3072, 768], P(None, ('dp', 'pair')), may hold values from -0.109375 to 0.109375
- reduce_bias: bfloat16 [2, 768], P(None, ('dp', 'pair')), may hold values from -3 to 3
Outputs:
- layer_out: bfloat16 [64, 64, 768], P(('dp', 'pair'))
- hidden_grad: float32 [64, 64, 768], P(('dp', 'pair'))
- feature_grad: float32 [64, 257, 1408], P(('dp', 'pair'))
- grad_self_project: float32 [3, 768, 768], P(None, ('dp', 'pair'))
- grad_self_output: float32 [768, 768], P(('dp', 'pair'))
- grad_self_bias: float32 [3, 768], P(None, ('dp', 'pair'))
- grad_norm_gain: float32 [4, 768], P(None, ('dp', 'pair'))
- grad_norm_bias: float32 [4, 768], P(None, ('dp', 'pair'))
- grad_cross_query: float32 [768, 768], P(('dp', 'pair'))
- grad_cross_output: float32 [768, 768], P(('dp', 'pair'))
- grad_image_project: float32 [2, 1408, 768], P(None, None, ('dp', 'pair'))
- grad_cross_bias: float32 [3, 768], P(None, ('dp', 'pair'))
- grad_expand_weight: float32 [2, 768, 3072], P(None, None, ('dp', 'pair'))
- grad_expand_bias: float32 [2, 3072], P(None, ('dp', 'pair'))
- grad_reduce_weight: float32 [2, 3072, 768], P(None, ('dp', 'pair'))
- grad_reduce_bias: float32 [2, 768], P(None, ('dp', 'pair'))
Inputs may be any that keep to these rules, and one draw needn't show every extreme that they name: `text_lengths`: text rows at or beyond an item's length are padding that no row attends to.
All inputs are finite; a program needn't handle non-finite values.
Results may differ from a plain program's by a relative error of at most 0.02.
Values may be sent and summed in bfloat16 or wider, within the bound.
No kernel may reach another device: no remote copies, remote signals or barrier semaphores. Data moves between devices by JAX's collectives and lax.ppermute only.
A program may use at most 320 MiB of HBM per device.

v0:
```python
import functools

import jax
import jax.numpy as jnp
from jax import lax
from jax.experimental import pallas as pl
from jax.experimental.pallas import tpu as pltpu
from jax.sharding import Mesh, PartitionSpec as P

HEAD = 64
NQ = 32
GROUP = 256
PER = GROUP // HEAD
eps = 1e-06
masked_off = 1000000000.0
AXES = ("z", "x", "c", "y")
BF = jnp.bfloat16
F32 = jnp.float32


def coords(index):
    return (index // 8, index // 4 % 2, index // 2 % 2, index % 2)


def pairs(count, move):
    result = []
    for source in range(count):
        z, x, c, y = move(*coords(source))
        result.append((source, ((z * 2 + x) * 2 + c) * 2 + y))
    return result


def step_a(z, x, c, y):
    return (z, x ^ 1, c, y) if c == 0 else (z, x, c, y ^ 1)


def step_b(z, x, c, y):
    return (z, x, c, y ^ 1) if c == 0 else (z, x ^ 1, c, y)


def step_c(z, x, c, y):
    return (z, x, c ^ 1, y)


def swap(value, move):
    count = lax.axis_size(AXES)
    return lax.ppermute(value, AXES, pairs(count, move))


def swap_z(value, distance):
    return swap(value, lambda z, x, c, y: (z ^ distance, x, c, y))


def gather_z(unit, *gates):
    if lax.axis_size("z") == 4:
        near = jnp.concatenate([unit, swap_z(unit, 2)], axis=0)
        near = after(near, *gates)
        return near, jnp.concatenate([near, swap_z(near, 1)], axis=0)
    near = lax.all_gather(unit, "z", axis=0, tiled=True)
    return near, near


def gather_all(near):
    a, b = swap(near, step_a), swap(near, step_b)
    pieces = [near, a, b, swap(a, step_b)]
    return pieces + [swap(piece, step_c) for piece in pieces]


def gather_plane(rows):
    for move in (step_a, step_b):
        rows = jnp.concatenate([rows, swap(rows, move)], axis=0)
    return [rows, swap(rows, step_c)]


def after(value, *earlier):
    return lax.optimization_barrier((value,) + earlier)[0]


def add_low(left, right):
    return (left.astype(F32) + right.astype(F32)).astype(BF)


def halved(kept, got):
    half = got.shape[0] // 2
    return add_low(kept[:half], got[:half]), add_low(kept[half:], got[half:])


def scatter_plane(kept, sent):
    for move in (step_c, step_b):
        kept, sent = halved(kept, swap(sent, move))
    return kept, swap(sent, step_a)


def step_z1(z, x, c, y):
    return (z ^ 1, x, c, y)


def step_z2(z, x, c, y):
    return (z ^ 2, x, c, y)


def scatter_rest(kept, got):
    return lax.psum_scatter(add_low(kept, got), "z", scatter_dimension=0, tiled=True).astype(F32)


def slot_owner(count):
    z, x, c, y = (lax.axis_index(name) for name in AXES)
    planes = count // 8
    slot = jnp.arange(count)
    k = slot % planes
    alpha = slot // planes % 2
    beta = slot // (2 * planes) % 2
    core = c ^ (slot // (4 * planes))
    flip_x = jnp.where(core == 0, alpha, beta)
    flip_y = jnp.where(core == 0, beta, alpha)
    plane = z ^ (k % 2 * 2 + k // 2) if planes == 4 else k
    return ((plane * 2 + (x ^ flip_x)) * 2 + core) * 2 + (y ^ flip_y)


def place_of_slot(width):
    count = lax.axis_size(AXES)
    each = width // count
    source = (slot_owner(count)[:, None] * each + jnp.arange(each)[None, :]).reshape(-1)
    return (source[:, None] == jnp.arange(width)[None, :]).astype(BF)


def by_slot(values, order):
    return dot_t(values, order).astype(BF)


def by_slot_turned(values, order):
    return dot_t(order, values).astype(BF)


def by_place(values, order):
    return dot(values.astype(BF), order)


def dot(left, right):
    return lax.dot_general(
        left, right, (((left.ndim - 1,), (0,)), ((), ())), preferred_element_type=F32
    )


def dot_t(left, right):
    return lax.dot_general(
        left, right, (((left.ndim - 1,), (1,)), ((), ())), preferred_element_type=F32
    )


def outer(left, right):
    lead = tuple(range(left.ndim - 1))
    return lax.dot_general(left, right, ((lead, lead), ((), ())), preferred_element_type=F32)


def column_sum(values):
    return jnp.sum(values.astype(F32), axis=0, keepdims=True)


def layer_norm(values, scale, shift):
    center = values - jnp.mean(values, axis=-1, keepdims=True)
    spread = jnp.mean(center * center, axis=-1, keepdims=True)
    return center * lax.rsqrt(spread + eps) * scale + shift


def norm_back(values, scale, gradient):
    center = values - jnp.mean(values, axis=-1, keepdims=True)
    spread = jnp.mean(center * center, axis=-1, keepdims=True)
    inverse = lax.rsqrt(spread + eps)
    normal = center * inverse
    inner = gradient * scale
    result = inverse * (
        inner
        - jnp.mean(inner, axis=-1, keepdims=True)
        - normal * jnp.mean(inner * normal, axis=-1, keepdims=True)
    )
    return result, column_sum(gradient * normal), column_sum(gradient)


def gelu_parts(values):
    half = F32(0.5) + F32(0.5) * lax.erf(values * F32(0.5**0.5))
    return half


def gelu_slope(values):
    density = jnp.exp(values * values * F32(-0.5)) * F32((2.0 * 3.141592653589793) ** -0.5)
    return gelu_parts(values) + values * density


def head_masks():
    lane = lax.broadcasted_iota(jnp.int32, (1, GROUP), 1) // HEAD
    return [(lane == h).astype(F32).astype(BF) for h in range(PER)]


def spread_heads(rows, masks):
    return jnp.concatenate([rows * mask for mask in masks], axis=0)


def fold_heads(stacked, masks, count):
    total = None
    for h, mask in enumerate(masks):
        part = stacked[h * count : (h + 1) * count] * mask.astype(F32)
        total = part if total is None else total + part
    return total


def softmax_rows(scores):
    shifted = jnp.exp(scores - jnp.max(scores, axis=-1, keepdims=True))
    return shifted / jnp.sum(shifted, axis=-1, keepdims=True)


def self_mask(length, rows):
    shape = (PER * rows, rows)
    row = lax.broadcasted_iota(jnp.int32, shape, 0) % rows
    col = lax.broadcasted_iota(jnp.int32, shape, 1)
    allowed = (col < NQ) | ((row >= NQ) & (col <= row) & (col - NQ < length))
    return jnp.where(allowed, F32(0.0), F32(-masked_off))


def attend_group_back(q, k, v, mask_add, grad, masks, count):
    q = spread_heads(q, masks)
    grad = spread_heads(grad, masks)
    weights = softmax_rows(dot_t(q, k) * HEAD ** (-0.5) + mask_add)
    grad_value = outer(weights.astype(BF), grad).astype(BF)
    grad_weight = dot_t(grad, v)
    grad_score = (
        weights * (grad_weight - jnp.sum(grad_weight * weights, axis=-1, keepdims=True))
    ).astype(BF)
    grad_query = fold_heads(dot(grad_score, k), masks, count) * HEAD ** (-0.5)
    grad_key = outer(grad_score, q) * HEAD ** (-0.5)
    return grad_query.astype(BF), grad_key.astype(BF), grad_value


def fetch(pieces, start, target, sems):
    width = target.shape[1]
    copies = []
    row = 0
    for n, piece in enumerate(pieces):
        count = piece.shape[0]
        source = piece.at[:, pl.ds(start, width)]
        copies.append(
            pltpu.make_async_copy(source, target.at[pl.ds(row, count)], sems.at[n])
        )
        row += count
    for copy in copies:
        copy.start()
    return copies


def finish(copies):
    for copy in copies:
        copy.wait()


def turned_rows(rows):
    rows = list(rows)
    each = rows[0].shape[1]
    rows.append(jnp.zeros((128 - sum(row.shape[0] for row in rows), each), F32))
    return jnp.concatenate(rows, axis=0).T.astype(BF)


def pack_kernel(refs):
    project_ref, output_ref, up_ref, down_ref, bias_ref = refs[:5]
    vector_refs, self_ref, ff_ref = refs[5:-2], refs[-2], refs[-1]
    width = output_ref.shape[1]
    for n in range(3):
        self_ref[:, pl.ds(n * width, width)] = project_ref[n]
    self_ref[:, pl.ds(3 * width, width)] = output_ref[...]
    vectors = turned_rows(ref[...].astype(F32) for ref in vector_refs)
    self_ref[:, pl.ds(4 * width, 128)] = vectors
    for n in range(2):
        start = n * (2 * width + 128)
        ff_ref[:, pl.ds(start, width)] = up_ref[n]
        ff_ref[:, pl.ds(start + width, width)] = down_ref[n]
        bias = bias_ref[n : n + 1, :].astype(F32)
        ff_ref[:, pl.ds(start + 2 * width, 128)] = turned_rows([bias])


def self_forward_kernel(items, n_pieces, refs):
    length_ref, hidden_ref, order_ref = refs[:3]
    pieces = refs[3 : 3 + n_pieces]
    qkv_ref, mix_ref, pre_ref, query_ref, text_ref, low_ref, vec_ref, w_ref, sems = refs[
        3 + n_pieces :
    ]
    rows_all, width = hidden_ref.shape
    copies = fetch(pieces, 0, w_ref, sems)
    order = order_ref[...]
    hidden_slot = by_slot(hidden_ref[...], order)
    finish(copies)
    vec = outer(w_ref[:, pl.ds(4 * width, 128)], order)[: vec_ref.shape[0]]
    vec_ref[...] = vec
    bias = [vec[0:1], F32(0.0), vec[1:2]]
    for n in range(3):
        cols = pl.ds(n * width, width)
        qkv_ref[:, cols] = (dot(hidden_slot, w_ref[:, cols]) + bias[n]).astype(BF)
    masks = head_masks()
    count = rows_all // items
    for i in range(items):
        rows = pl.ds(i * count, count)
        mask_add = self_mask(length_ref[i], count)
        for g in range(width // GROUP):
            cols = [pl.ds(n * width + g * GROUP, GROUP) for n in range(3)]
            q = spread_heads(qkv_ref[rows, cols[0]], masks)
            scores = dot_t(q, qkv_ref[rows, cols[1]]) * HEAD ** (-0.5) + mask_add
            weights = softmax_rows(scores).astype(BF)
            mixed = dot(weights, qkv_ref[rows, cols[2]])
            mix_ref[rows, cols[0]] = fold_heads(mixed, masks, count).astype(BF)
    mixture_slot = by_slot(mix_ref[...], order)
    pre = dot(mixture_slot, w_ref[:, pl.ds(3 * width, width)])
    pre = pre + vec[2:3] + hidden_ref[...].astype(F32)
    pre_ref[...] = pre
    first = layer_norm(pre, vec[3:4], vec[7:8])
    text = count - NQ
    for i in range(items):
        query_ref[pl.ds(i * NQ, NQ), :] = first[i * count : i * count + NQ]
        part = first[i * count + NQ : (i + 1) * count]
        text_ref[pl.ds(i * text, text), :] = part
        low_ref[pl.ds(i * text, text), :] = part.astype(BF)


def image_kernel(n_pieces, refs):
    feature_ref, order_ref, vec_ref = refs[:3]
    pieces = refs[3 : 3 + n_pieces]
    key_ref, value_ref, w_ref, sems = refs[3 + n_pieces :]
    items, _, image_width = feature_ref.shape
    copies = fetch(pieces, 0, w_ref, sems)
    order = order_ref[...]
    bias_slot = dot_t(vec_ref[...].astype(BF), order)[12:13]
    finish(copies)
    for i in range(items):
        rows = feature_ref[i]
        keys = dot_t(rows, w_ref[:, pl.ds(0, image_width)])
        key_ref[i] = by_place(keys, order).astype(BF)
        values = dot_t(rows, w_ref[:, pl.ds(image_width, image_width)]) + bias_slot
        value_ref[i] = by_place(values, order).astype(BF)


def cross_forward_kernel(start, n_pieces, refs):
    first_ref, key_ref, value_ref, order_ref, vec_ref = refs[:5]
    pieces = refs[5 : 5 + n_pieces]
    rows_ref, look_ref, pre_ref, second_ref, low_ref, w_ref, sems = refs[5 + n_pieces :]
    copies = fetch(pieces, start, w_ref, sems)
    items = key_ref.shape[0]
    width = first_ref.shape[1]
    count = first_ref.shape[0] // items
    order = order_ref[...]
    vec = vec_ref[...]
    masks = head_masks()
    first_slot = by_slot(first_ref[...].astype(BF), order)
    finish(copies)
    rows_ref[...] = (dot(first_slot, w_ref[:, pl.ds(0, width)]) + vec[11:12]).astype(BF)
    for i in range(items):
        rows = pl.ds(i * count, count)
        for g in range(width // GROUP):
            cols = pl.ds(g * GROUP, GROUP)
            q = spread_heads(rows_ref[rows, cols], masks)
            scores = dot_t(q, key_ref[i, :, cols]) * HEAD ** (-0.5)
            mixed = dot(softmax_rows(scores).astype(BF), value_ref[i, :, cols])
            look_ref[rows, cols] = fold_heads(mixed, masks, count).astype(BF)
    pre = dot(by_slot(look_ref[...], order), w_ref[:, pl.ds(width, width)])
    pre = pre + vec[13:14] + first_ref[...]
    pre_ref[...] = pre
    second = layer_norm(pre, vec[4:5], vec[8:9])
    second_ref[...] = second
    low_ref[...] = second.astype(BF)


def branch_up_kernel(branch, n_pieces, refs):
    low_refs = refs[:2]
    pieces = refs[2 : 2 + n_pieces]
    pre_ref, act_ref, kept_ref, sent_ref, w_ref, sems = refs[2 + n_pieces :]
    half, width = low_refs[0].shape
    copies = fetch(pieces, branch * (2 * width + 128), w_ref, sems)
    finish(copies)
    first_lane = (lax.broadcasted_iota(jnp.int32, (8, 128), 1) == 0).astype(F32).astype(BF)
    bias = dot_t(first_lane, w_ref[:, pl.ds(2 * width, 128)])[0:1]
    for n, (low_ref, out_ref) in enumerate(zip(low_refs, (kept_ref, sent_ref))):
        rows = pl.ds(n * half, half)
        pre = dot_t(low_ref[...], w_ref[:, pl.ds(0, width)]) + bias
        pre_ref[rows, :] = pre
        active = (pre * gelu_parts(pre)).astype(BF)
        act_ref[rows, :] = active
        out_ref[...] = dot(active, w_ref[:, pl.ds(width, width)]).astype(out_ref.dtype)


def branch_end_kernel(branch, refs):
    kept_ref, got_ref, value_ref, cot_ref, vec_ref = refs[:5]
    out_ref, grad_ref, low_ref, sum_ref = refs[5:]
    items, count, _ = cot_ref.shape
    vec = vec_ref[...]
    gain, shift = vec[5 + branch : 6 + branch], vec[9 + branch : 10 + branch]
    total = kept_ref[...].astype(F32) + got_ref[...].astype(F32)
    total = total + vec[14 + branch : 15 + branch] + value_ref[...]
    start, size = (NQ, count - NQ) if branch else (0, NQ)
    cot = jnp.concatenate([cot_ref[i, start : start + size, :] for i in range(items)], axis=0)
    out_ref[...] = layer_norm(total, gain, shift).astype(BF)
    grad, gain_grad, shift_grad = norm_back(total, gain, cot.astype(F32))
    grad_ref[...] = grad
    low = grad.astype(BF)
    low_ref[...] = low
    sum_ref[0:1, :] = gain_grad
    sum_ref[1:2, :] = shift_grad
    sum_ref[2:3, :] = column_sum(low)


def branch_down_kernel(branch, n_pieces, refs):
    grad_refs, low_refs, (pre_ref, act_ref) = refs[:2], refs[2:4], refs[4:6]
    pieces = refs[6 : 6 + n_pieces]
    rest = refs[6 + n_pieces :]
    kept_ref, sent_ref, own_ref, w_ref, sems = rest
    half, width = low_refs[0].shape
    copies = fetch(pieces, branch * (2 * width + 128), w_ref, sems)
    finish(copies)
    grads = []
    for n, out_ref in enumerate((kept_ref, sent_ref)):
        rows = pl.ds(n * half, half)
        back = dot_t(grad_refs[n][...], w_ref[:, pl.ds(width, width)])
        grad_pre = (gelu_slope(pre_ref[rows, :]) * back).astype(BF)
        grads.append(grad_pre)
        out_ref[...] = dot(grad_pre, w_ref[:, pl.ds(0, width)]).astype(out_ref.dtype)
    grad_pre = jnp.concatenate(grads, axis=0)
    low = jnp.concatenate([ref[...] for ref in low_refs], axis=0)
    grad_low = jnp.concatenate([ref[...] for ref in grad_refs], axis=0)
    own_ref[:, pl.ds(0, width)] = outer(grad_pre, low).astype(BF)
    own_ref[:, pl.ds(width, width)] = outer(act_ref[...], grad_low).astype(BF)
    sums = outer(grad_pre, jnp.ones((2 * half, 128), BF)).astype(BF)
    own_ref[:, pl.ds(2 * width, 128)] = sums


def cross_backward_kernel(start, n_pieces, refs):
    kept_ref, got_ref, sum_ref, pre_ref, q_ref, k_ref, v_ref, order_ref, vec_ref = refs[:9]
    pieces = refs[9 : 9 + n_pieces]
    dq_ref, dk_ref, dv_ref, low_ref, first_ref, row_ref, w_ref, sems = refs[9 + n_pieces :]
    copies = fetch(pieces, start, w_ref, sems)
    items = k_ref.shape[0]
    width = q_ref.shape[1]
    count = q_ref.shape[0] // items
    order = order_ref[...]
    vec = vec_ref[...]
    masks = head_masks()
    gradient = kept_ref[...].astype(F32) + got_ref[...].astype(F32) + sum_ref[...]
    grad_two, gain_grad, shift_grad = norm_back(pre_ref[...], vec[4:5], gradient)
    low = grad_two.astype(BF)
    low_ref[...] = low
    finish(copies)
    looked = by_place(dot_t(low, w_ref[:, pl.ds(width, width)]), order).astype(BF)
    value_sum = []
    for g in range(width // GROUP):
        cols = pl.ds(g * GROUP, GROUP)
        total = None
        for i in range(items):
            rows = pl.ds(i * count, count)
            dq, dk, dv = attend_group_back(
                q_ref[rows, cols],
                k_ref[i, :, cols],
                v_ref[i, :, cols],
                F32(0.0),
                looked[i * count : (i + 1) * count, g * GROUP : (g + 1) * GROUP],
                masks,
                count,
            )
            dq_ref[rows, cols] = dq
            dk_ref[i, :, cols] = dk
            dv_ref[i, :, cols] = dv
            part = column_sum(dv)
            total = part if total is None else total + part
        value_sum.append(total)
    grad_cross = dq_ref[...]
    back = dot_t(grad_cross, w_ref[:, pl.ds(0, width)])
    first_ref[...] = grad_two + by_place(back, order)
    row_ref[0:1, :] = gain_grad
    row_ref[1:2, :] = shift_grad
    row_ref[2:3, :] = column_sum(grad_cross)
    row_ref[3:4, :] = jnp.concatenate(value_sum, axis=1)
    row_ref[4:5, :] = column_sum(low)


def cross_weights_kernel(refs):
    dq_ref, dk_ref, dv_ref, low_ref, first_ref, look_ref, feature_ref, order_ref = refs[:8]
    kept_ref, sent_ref = refs[8:]
    items, _, image_width = feature_ref.shape
    half, width = order_ref.shape[0] // 2, order_ref.shape[1]
    for part, out_ref in enumerate((kept_ref, sent_ref)):
        order = order_ref[pl.ds(part * half, half), :]
        for n, grad_ref in enumerate((dk_ref, dv_ref)):
            total = None
            for i in range(items):
                turned = by_slot_turned(grad_ref[i], order)
                product = dot(turned, feature_ref[i])
                total = product if total is None else total + product
            out_ref[:, pl.ds(n * image_width, image_width)] = total.astype(BF)
        start = 2 * image_width
        turned = by_slot_turned(first_ref[...].astype(BF), order)
        out_ref[:, pl.ds(start, width)] = dot(turned, dq_ref[...]).astype(BF)
        turned = by_slot_turned(look_ref[...], order)
        out_ref[:, pl.ds(start + width, width)] = dot(turned, low_ref[...]).astype(BF)


def feature_kernel(n_pieces, refs):
    dk_ref, dv_ref, order_ref = refs[:3]
    pieces = refs[3 : 3 + n_pieces]
    out_ref, w_ref, sems = refs[3 + n_pieces :]
    items, _, image_width = out_ref.shape
    copies = fetch(pieces, 0, w_ref, sems)
    order = order_ref[...]
    slots = [[by_slot(ref[i], order) for ref in (dk_ref, dv_ref)] for i in range(items)]
    finish(copies)
    for i in range(items):
        total = dot(slots[i][0], w_ref[:, pl.ds(0, image_width)])
        out_ref[i] = total + dot(slots[i][1], w_ref[:, pl.ds(image_width, image_width)])


def self_backward_kernel(items, n_pieces, refs):
    length_ref, query_ref, kept_ref, got_ref, text_ref, pre_ref, qkv_ref = refs[:7]
    mix_ref, hidden_ref, order_ref, vec_ref = refs[7:11]
    row_refs = refs[11:14]
    pieces = refs[14 : 14 + n_pieces]
    grad_ref, one_ref, g_kept_ref, g_sent_ref, w_ref, sum_ref, sems = refs[14 + n_pieces :]
    copies = fetch(pieces, 3 * pre_ref.shape[1], w_ref, sems)
    rows_all, width = pre_ref.shape
    count = rows_all // items
    text = count - NQ
    order = order_ref[...]
    vec = vec_ref[...]
    masks = head_masks()
    text_grad = kept_ref[...].astype(F32) + got_ref[...].astype(F32) + text_ref[...]
    query_grad = query_ref[...]
    gradient = []
    for i in range(items):
        gradient.append(query_grad[i * NQ : (i + 1) * NQ])
        gradient.append(text_grad[i * text : (i + 1) * text])
    gradient = jnp.concatenate(gradient, axis=0)
    grad_one, gain_grad, shift_grad = norm_back(pre_ref[...], vec[3:4], gradient)
    one_ref[...] = grad_one
    low = grad_one.astype(BF)
    finish(copies)
    grad_mix = by_place(dot_t(low, w_ref[...]), order).astype(BF)
    sums = [None, None, None]
    for i in range(items):
        rows = pl.ds(i * count, count)
        mask_add = self_mask(length_ref[i], count)
        for g in range(width // GROUP):
            cols = [pl.ds(n * width + g * GROUP, GROUP) for n in range(3)]
            results = attend_group_back(
                *[qkv_ref[rows, col] for col in cols],
                mask_add,
                grad_mix[i * count : (i + 1) * count, g * GROUP : (g + 1) * GROUP],
                masks,
                count,
            )
            for col, value in zip(cols, results):
                grad_ref[rows, col] = value
    query_rows, query_ends, text_ends = row_refs
    sum_ref[...] = jnp.zeros(sum_ref.shape, F32)
    total = column_sum(grad_ref[...])
    listed = [
        total[:, :width],
        total[:, 2 * width :],
        column_sum(low),
        gain_grad,
        query_rows[0:1, :],
        query_ends[0:1, :],
        text_ends[0:1, :],
        shift_grad,
        query_rows[1:2, :],
        query_ends[1:2, :],
        text_ends[1:2, :],
        query_rows[2:3, :],
        query_rows[3:4, :],
        query_rows[4:5, :],
        query_ends[2:3, :],
        text_ends[2:3, :],
    ]
    for n, value in enumerate(listed):
        sum_ref[n : n + 1, :] = value
    sums = sum_ref[...].astype(BF)
    half = width // 2
    for part, out_ref in enumerate((g_kept_ref, g_sent_ref)):
        block = order_ref[pl.ds(part * half, half), :]
        turned = by_slot_turned(hidden_ref[...], block)
        for n in range(3):
            cols = pl.ds(n * width, width)
            out_ref[:, cols] = dot(turned, grad_ref[:, cols]).astype(BF)
        turned = by_slot_turned(mix_ref[...], block)
        out_ref[:, pl.ds(3 * width, width)] = dot(turned, low).astype(BF)
        out_ref[:, pl.ds(4 * width, 128)] = dot_t(block, sums).astype(BF)


def hidden_kernel(n_pieces, refs):
    grad_ref, one_ref, order_ref = refs[:3]
    pieces = refs[3 : 3 + n_pieces]
    out_ref, w_ref, sems = refs[3 + n_pieces :]
    copies = fetch(pieces, 0, w_ref, sems)
    finish(copies)
    back = dot_t(grad_ref[...], w_ref[...])
    out_ref[...] = one_ref[...] + by_place(back, order_ref[...])


def shaped(*dims, kind=F32):
    return jax.ShapeDtypeStruct(dims, kind)


def kernel_call(
    body, name, outs, inputs, pieces=(), loaded=None, lengths=None, extra=(), cost=8
):
    vmem = pl.BlockSpec(memory_space=pltpu.VMEM)
    specs = [vmem] * len(inputs) + [pl.BlockSpec(memory_space=pl.ANY)] * len(pieces)
    arrays = tuple(inputs) + tuple(pieces)
    if lengths is not None:
        specs = [pl.BlockSpec(memory_space=pltpu.SMEM)] + specs
        arrays = (lengths,) + arrays
    scratch = []
    if loaded is not None:
        rows = sum(piece.shape[0] for piece in pieces)
        scratch = [pltpu.VMEM((rows, loaded), BF)] + list(extra)
        scratch.append(pltpu.SemaphoreType.DMA((len(pieces),)))
    return pl.pallas_call(
        lambda *refs: body(refs),
        name=name,
        out_shape=outs,
        in_specs=specs,
        out_specs=jax.tree.map(lambda _: vmem, outs),
        scratch_shapes=scratch,
        cost_estimate=pl.CostEstimate(
            flops=cost * 900_000_000, bytes_accessed=cost * 3_000_000, transcendentals=0
        ),
    )(*arrays)


def shards(
    hidden,
    features,
    text_lengths,
    cotangent,
    self_project,
    self_output,
    self_bias,
    norm_gain,
    norm_bias,
    cross_query,
    cross_output,
    image_project,
    cross_bias,
    expand_weight,
    expand_bias,
    reduce_weight,
    reduce_bias,
):
    part = functools.partial
    items, item_rows, width = hidden.shape
    each = self_output.shape[0]
    image_rows, image_width = features.shape[1:]
    ff_each = reduce_weight.shape[1]
    planes = lax.axis_size("z")
    rows = items * item_rows
    query_rows, text_rows = items * NQ, items * (item_rows - NQ)
    ff = planes * ff_each
    order = place_of_slot(width)
    flat = hidden.reshape(rows, width)

    vectors = (self_bias, norm_gain, norm_bias, cross_bias, reduce_bias)
    n_vectors = sum(v.shape[0] for v in vectors)
    ff_width = 2 * width + 128
    up_turned = jnp.swapaxes(expand_weight, 1, 2)
    unit_self, unit_ff = kernel_call(
        pack_kernel,
        "pack",
        (shaped(each, 4 * width + 128, kind=BF), shaped(ff_each, 2 * ff_width, kind=BF)),
        (self_project, self_output, up_turned, reduce_weight, expand_bias, *vectors),
        cost=1,
    )
    image_turned = jnp.swapaxes(image_project, 1, 2)
    unit_cross = jnp.concatenate(
        [image_turned[0], image_turned[1], cross_query, cross_output], axis=1
    )
    w_ff = [lax.all_gather(unit_ff, "z", axis=0, tiled=True)]
    half_self, near_self = gather_z(unit_self)
    w_self = gather_all(near_self)
    near_cross = gather_z(after(unit_cross, half_self), near_self)[1]
    w_cross = gather_all(after(near_cross, w_self[1]))
    cross_start = 2 * image_width

    qkv, mixture, pre_one, first_query, first_text, text_low, vec = kernel_call(
        part(self_forward_kernel, items, len(w_self)),
        "self_forward",
        (
            shaped(rows, 3 * width, kind=BF),
            shaped(rows, width, kind=BF),
            shaped(rows, width),
            shaped(query_rows, width),
            shaped(text_rows, width),
            shaped(text_rows, width, kind=BF),
            shaped(n_vectors, width),
        ),
        (flat, order),
        w_self,
        4 * width + 128,
        text_lengths,
    )

    wide = shaped(items, image_rows, width, kind=BF)
    image_keys, image_values = kernel_call(
        part(image_kernel, len(w_cross)),
        "image_rows",
        (wide, wide),
        (features, order, vec),
        w_cross,
        cross_start,
    )
    cross_rows, looked, pre_two, second, second_low = kernel_call(
        part(cross_forward_kernel, cross_start, len(w_cross)),
        "cross_forward",
        (
            shaped(query_rows, width, kind=BF),
            shaped(query_rows, width, kind=BF),
            shaped(query_rows, width),
            shaped(query_rows, width),
            shaped(query_rows, width, kind=BF),
        ),
        (first_query, image_keys, image_values, order, vec),
        w_cross,
        2 * width,
    )

    branches = [None, None]
    for j, values, low in ((1, first_text, text_low), (0, second, second_low)):
        count = values.shape[0]
        low_all = gather_plane(low)
        half = 4 * count
        pre_act, active, kept, sent = kernel_call(
            part(branch_up_kernel, j, len(w_ff)),
            "branch_up_%d" % j,
            (
                shaped(2 * half, ff),
                shaped(2 * half, ff, kind=BF),
                shaped(half, width),
                shaped(half, width, kind=BF),
            ),
            low_all,
            w_ff,
            ff_width,
        )
        out, grad_sum, grad_low, ends = kernel_call(
            part(branch_end_kernel, j),
            "branch_end_%d" % j,
            (
                shaped(count, width, kind=BF),
                shaped(count, width),
                shaped(count, width, kind=BF),
                shaped(8, width),
            ),
            (*scatter_plane(kept, sent), values, cotangent, vec),
        )
        kept, sent, grads = kernel_call(
            part(branch_down_kernel, j, len(w_ff)),
            "branch_down_%d" % j,
            (
                shaped(half, width),
                shaped(half, width, kind=BF),
                shaped(ff, ff_width, kind=BF),
            ),
            (*gather_plane(grad_low), *low_all, pre_act, active),
            w_ff,
            2 * width,
        )
        own = lax.psum_scatter(grads, "z", scatter_dimension=0, tiled=True)
        branches[j] = (out, grad_sum, ends, scatter_plane(kept, sent), own)
    query, text = branches
    layer_out = jnp.concatenate(
        [query[0].reshape(items, NQ, width), text[0].reshape(items, item_rows - NQ, width)],
        axis=1,
    )

    query_got = after(query[3][1], text[3][1])
    grad_cross, grad_ikey, grad_ivalue, two_low, grad_first, cross_ends = kernel_call(
        part(cross_backward_kernel, cross_start, len(w_cross)),
        "cross_backward",
        (
            shaped(query_rows, width, kind=BF),
            wide,
            wide,
            shaped(query_rows, width, kind=BF),
            shaped(query_rows, width),
            shaped(8, width),
        ),
        (query[3][0], query_got, query[1], pre_two, cross_rows, image_keys, image_values, order, vec),
        w_cross,
        2 * width,
    )
    packed = shaped(width // 2, cross_start + 2 * width, kind=BF)
    cross_kept, cross_sent = kernel_call(
        cross_weights_kernel,
        "cross_weights",
        (packed, packed),
        (grad_cross, grad_ikey, grad_ivalue, two_low, first_query, looked, features, order),
        cost=13,
    )
    grad_first = after(grad_first, cross_sent)
    cross_kept, cross_sent = halved(cross_kept, swap(cross_sent, step_c))

    packed = shaped(width // 2, 4 * width + 128, kind=BF)
    grad_qkv, grad_one, kept, sent = kernel_call(
        part(self_backward_kernel, items, len(w_self)),
        "self_backward",
        (shaped(rows, 3 * width, kind=BF), shaped(rows, width), packed, packed),
        (
            grad_first,
            *text[3],
            text[1],
            pre_one,
            qkv,
            mixture,
            flat,
            order,
            vec,
            cross_ends,
            query[2],
            text[2],
        ),
        w_self,
        width,
        text_lengths,
        (pltpu.VMEM((128, width), F32),),
    )
    sent = after(sent, cross_sent)
    cross_got = swap(cross_sent, step_b)
    kept, sent = halved(kept, swap(sent, step_c))
    feature_order = after(order, sent)
    cross_got = after(cross_got, sent)
    cross_kept, cross_sent = halved(cross_kept, cross_got)
    hidden_order = after(order, cross_sent)
    got = after(swap(sent, step_b), cross_sent)
    kept, sent = halved(kept, got)
    cross_got = after(swap(cross_sent, step_a), sent)
    got = swap(sent, step_a)
    if planes == 4:
        cross_kept, cross_sent = halved(cross_kept, cross_got)
        got = after(got, cross_sent)
        kept, sent = halved(kept, got)
        cross_got = after(swap(cross_sent, step_z1), sent)
        cross_kept, cross_sent = halved(cross_kept, cross_got)
        got = after(swap(sent, step_z1), cross_sent)
        kept, sent = halved(kept, got)
        own_cross = cross_kept.astype(F32) + swap(cross_sent, step_z2).astype(F32)
        own_self = kept.astype(F32) + swap(sent, step_z2).astype(F32)
    else:
        own_cross = scatter_rest(cross_kept, cross_got)
        own_self = scatter_rest(kept, got)
    own_ff = [after(branch[4], sent).astype(F32) for branch in branches]
    feature_grad = kernel_call(
        part(feature_kernel, len(w_cross)),
        "feature_grad",
        shaped(items, image_rows, image_width),
        (grad_ikey, grad_ivalue, feature_order),
        w_cross,
        cross_start,
    )
    hidden_grad = kernel_call(
        part(hidden_kernel, len(w_self)),
        "hidden_grad",
        shaped(rows, width),
        (grad_qkv, grad_one, hidden_order),
        w_self,
        3 * width,
    )

    own_sums = own_self[:, 4 * width : 4 * width + n_vectors].T
    own_up = [own[:, :width].T for own in own_ff]
    own_down = [own[:, width : 2 * width] for own in own_ff]
    own_up_bias = [own[:, 2 * width] for own in own_ff]
    return (
        layer_out,
        hidden_grad.reshape(items, item_rows, width),
        feature_grad,
        jnp.stack([own_self[:, n * width : (n + 1) * width] for n in range(3)]),
        own_self[:, 3 * width : 4 * width],
        own_sums[0:3],
        own_sums[3:7],
        own_sums[7:11],
        own_cross[:, cross_start : cross_start + width],
        own_cross[:, cross_start + width :],
        jnp.stack([own_cross[:, n * image_width : (n + 1) * image_width].T for n in range(2)]),
        own_sums[11:14],
        jnp.stack(own_up),
        jnp.stack(own_up_bias),
        jnp.stack(own_down),
        own_sums[14:16],
    )


def solution(mesh):
    dp, pair = mesh.devices.shape
    fine = Mesh(mesh.devices.reshape(dp // 4, 2, 2, pair), AXES)
    first, second, third = P(AXES), P(None, AXES), P(None, None, AXES)
    in_specs = (
        first, first, first, first,
        second, first, second, second, second, first, first,
        third, second, third, second, second, second,
    )
    out_specs = (
        first, first, first,
        second, first, second, second, second, first, first,
        third, second, third, second, second, second,
    )
    return jax.shard_map(shards, mesh=fine, in_specs=in_specs, out_specs=out_specs, check_vma=False)
```

profile of v0, /device:TPU:0, one launch (start us, length us, event | category | flops | bytes accessed | tf_op | source)
XLA Modules:
  0.0 364.5 jit_solution(10023160279217234900)
XLA Ops:
  7.3 2.2 pack.1
  9.4 4.1 %collective-permute-start = (bf16[24,3200]{1,0:T(8,128)(2,1)}, bf16[24,3200]{1,0:T(8,128)(2,1)S(1)}, u32[]{:S(2)}, u32[]{:S(2)}) collective-permute-start(bf16[24,3200]{1,0:T(8,128)(2,1)} %get-tuple-element.82), channel_id=1, source_target_pairs={{0,16},{1,17},{2,18},{3,19},{4,20},{5,21},{6,22},{7,23},{8,24},{9,... | collective-permute-start | bytes 460808 | tf_op jit(solution)/shard_map/ppermute | solution.py:47
  13.5 7.4 %collective-permute-done = bf16[24,3200]{1,0:T(8,128)(2,1)S(1)} collective-permute-done((bf16[24,3200]{1,0:T(8,128)(2,1)}, bf16[24,3200]{1,0:T(8,128)(2,1)S(1)}, u32[]{:S(2)}, u32[]{:S(2)}) %collective-permute-start) | collective-permute-done | bytes 153632 | tf_op jit(solution)/shard_map/ppermute | solution.py:47
  22.0 4.1 %collective-permute-start.1 = (bf16[48,3200]{1,0:T(8,128)(2,1)S(1)}, bf16[48,3200]{1,0:T(8,128)(2,1)S(1)}, u32[]{:S(2)}, u32[]{:S(2)}) collective-permute-start(bf16[48,3200]{1,0:T(8,128)(2,1)S(1)} %pad_maximum_fusion.5), channel_id=1, source_target_pairs={{0,8},{1,9},{2,10},{3,11},{4,12},{5,13},{6,14},{7,15},{8,0},{9,1},... | collective-permute-start | bytes 921608 | tf_op jit(solution)/shard_map/ppermute | solution.py:47
  26.1 7.7 %collective-permute-done.9 = bf16[24,4352]{1,0:T(8,128)(2,1)S(1)} collective-permute-done((bf16[24,4352]{1,0:T(8,128)(2,1)S(1)}, bf16[24,4352]{1,0:T(8,128)(2,1)S(1)}, u32[]{:S(2)}, u32[]{:S(2)}) %collective-permute-start.9) | collective-permute-done | bytes 208928 | tf_op jit(solution)/shard_map/ppermute | solution.py:47
  33.8 2.1 collective-permute-done.1
  37.5 9.3 %collective-permute-done.10 = bf16[48,4352]{1,0:T(8,128)(2,1)S(1)} collective-permute-done((bf16[48,4352]{1,0:T(8,128)(2,1)S(1)}, bf16[48,4352]{1,0:T(8,128)(2,1)S(1)}, u32[]{:S(2)}, u32[]{:S(2)}) %collective-permute-start.10) | collective-permute-done | bytes 417824 | tf_op jit(solution)/shard_map/ppermute | solution.py:47
  51.8 16.7 %collective-permute-done.11.refs_4_.refs_6_.refs_10_ = bf16[96,4352]{1,0:T(8,128)(2,1)} collective-permute-done((bf16[96,4352]{1,0:T(8,128)(2,1)S(1)}, bf16[96,4352]{1,0:T(8,128)(2,1)}, u32[]{:S(2)}, u32[]{:S(2)}) %collective-permute-start.11) | collective-permute-done | bytes 835616 | tf_op jit(solution)/shard_map/ppermute | solution.py:47
  73.2 5.8 %collective-permute-done.12.refs_5_.refs_7_.refs_11_ = bf16[96,4352]{1,0:T(8,128)(2,1)} collective-permute-done((bf16[96,4352]{1,0:T(8,128)(2,1)S(1)}, bf16[96,4352]{1,0:T(8,128)(2,1)}, u32[]{:S(2)}, u32[]{:S(2)}) %collective-permute-start.12) | collective-permute-done | bytes 835616 | tf_op jit(solution)/shard_map/ppermute | solution.py:47
  80.2 7.8 %collective-permute-done.13.refs_6_.refs_8_.refs_12_ = bf16[96,4352]{1,0:T(8,128)(2,1)} collective-permute-done((bf16[96,4352]{1,0:T(8,128)(2,1)}, bf16[96,4352]{1,0:T(8,128)(2,1)}, u32[]{:S(2)}, u32[]{:S(2)}) %collective-permute-start.13) | collective-permute-done | bytes 835616 | tf_op jit(solution)/shard_map/ppermute | solution.py:47
  89.2 7.3 %self_forward.1 = (bf16[128,2304]{1,0:T(8,128)(2,1)}, bf16[128,768]{1,0:T(8,128)(2,1)}, f32[128,768]{1,0:T(8,128)}, f32[64,768]{1,0:T(8,128)}, f32[64,768]{1,0:T...) custom-call(s32[2]{0:T(128)} %refs_0_.6, bf16[128,768]{1,0:T(8,128)(2,1)} %bitcast.46, ...), custom_call_target="tpu_custom_call" | custom-call | flops 7200000000 | bytes 24000000 | tf_op jit(solution)/shard_map/self_forward/pallas_call | solution.py:617
  99.3 2.1 collective-permute-done.24
  102.2 4.9 %collective-permute-done.25 = bf16[128,768]{1,0:T(8,128)(2,1)S(1)} collective-permute-done((bf16[128,768]{1,0:T(8,128)(2,1)S(1)}, bf16[128,768]{1,0:T(8,128)(2,1)S(1)}, u32[]{:S(2)}, u32[]{:S(2)}) %collective-permute-start.25) | collective-permute-done | bytes 196640 | tf_op jit(solution)/shard_map/ppermute | solution.py:47
  108.2 10.0 %image_rows.1 = (bf16[2,257,768]{2,1,0:T(8,128)(2,1)}, bf16[2,257,768]{2,1,0:T(8,128)(2,1)}) custom-call(bf16[2,257,1408]{2,1,0:T(8,128)(2,1)} %copy.41.refs_0_.refs_6_, bf16[768,768]{1,0:T(8,128)(2,1)} %fusion.refs_2_.refs_1_.refs_3_.refs_7_.refs_9_, f32[16,768]{1,0:T(8,128)} %get-tuple-element.84.refs_2_.refs_4_.refs_8_.refs_10_, ...), custom_call_target="tpu_custom_call" | custom-call | flops 7200000000 | bytes 24000000 | tf_op jit(solution)/shard_map/image_rows/pallas_call | solution.py:617
  119.0 4.9 %branch_up_1.1 = (f32[512,384]{1,0:T(8,128)}, bf16[512,384]{1,0:T(8,128)(2,1)}, f32[256,768]{1,0:T(8,128)}, bf16[256,768]{1,0:T(8,128)(2,1)}) custom-call(bf16[256,768]{1,0:T(8,128)(2,1)} %copy-done.23, bf16[256,768]{1,0:T(8,128)(2,1)} %copy-done.29, bf16[384,3328]{1,0:T(8,128)(2,1)} %all-gather.2.cloned.1.call-done.refs_2_.refs_6_), custom_call_target="tpu_custom_call" | custom-call | flops 7200000000 | bytes 24000000 | tf_op jit(solution)/shard_map/branch_up_1/pallas_call | solution.py:617
  124.5 7.7 %cross_forward.1 = (bf16[64,768]{1,0:T(8,128)(2,1)}, bf16[64,768]{1,0:T(8,128)(2,1)}, f32[64,768]{1,0:T(8,128)}, f32[64,768]{1,0:T(8,128)}, bf16[64,768]{1,0:T(8,128)(2,1)}) custom-call(f32[64,768]{1,0:T(8,128)} %get-tuple-element.83.refs_0_.refs_4_, bf16[2,257,768]{2,1,0:T(8,128)(2,1)} %get-tuple-element.88.refs_1_.refs_5_, ...), custom_call_target="tpu_custom_call" | custom-call | flops 7200000000 | bytes 24000000 | tf_op jit(solution)/shard_map/cross_forward/pallas_call | solution.py:617
  134.6 2.4 collective-permute-done.18
  140.2 3.5 collective-permute-done.19
  144.0 1.7 collective-permute-done.28
  148.7 4.9 %branch_up_0.1 = (f32[512,384]{1,0:T(8,128)}, bf16[512,384]{1,0:T(8,128)(2,1)}, f32[256,768]{1,0:T(8,128)}, bf16[256,768]{1,0:T(8,128)(2,1)}) custom-call(bf16[256,768]{1,0:T(8,128)(2,1)} %copy-done.22, bf16[256,768]{1,0:T(8,128)(2,1)} %copy-done.30, bf16[384,3328]{1,0:T(8,128)(2,1)} %all-gather.2.cloned.1.call-done.refs_2_.refs_6_), custom_call_target="tpu_custom_call" | custom-call | flops 7200000000 | bytes 24000000 | tf_op jit(solution)/shard_map/branch_up_0/pallas_call | solution.py:617
  154.3 2.2 branch_end_1.1
  158.9 3.6 collective-permute-done.36
  165.1 3.2 collective-permute-done.23.refs_1_
  169.0 2.1 branch_end_0.1
  172.6 3.3 collective-permute-done.30
  179.4 3.2 collective-permute-done.31
  183.6 6.0 %branch_down_1.1 = (f32[256,768]{1,0:T(8,128)}, bf16[256,768]{1,0:T(8,128)(2,1)}, bf16[384,1664]{1,0:T(8,128)(2,1)}) custom-call(bf16[256,768]{1,0:T(8,128)(2,1)} %copy-done.21, bf16[256,768]{1,0:T(8,128)(2,1)} %copy-done.31, bf16[256,768]{1,0:T(8,128)(2,1)} %copy-done.23, bf16[256,768]{1,0:T(8,128)(2,1)} %copy-done.29, ...), custom_call_target="tpu_custom_call" | custom-call | flops 7200000000 | bytes 24000000 | tf_op jit(solution)/shard_map/branch_down_1/pallas_call | solution.py:617
  190.8 6.0 %branch_down_0.1 = (f32[256,768]{1,0:T(8,128)}, bf16[256,768]{1,0:T(8,128)(2,1)}, bf16[384,1664]{1,0:T(8,128)(2,1)}) custom-call(bf16[256,768]{1,0:T(8,128)(2,1)} %copy-done.24, bf16[256,768]{1,0:T(8,128)(2,1)} %copy-done.32, bf16[256,768]{1,0:T(8,128)(2,1)} %copy-done.22, bf16[256,768]{1,0:T(8,128)(2,1)} %copy-done.30, ...), custom_call_target="tpu_custom_call" | custom-call | flops 7200000000 | bytes 24000000 | tf_op jit(solution)/shard_map/branch_down_0/pallas_call | solution.py:617
  200.6 2.3 collective-permute-done.40
  208.2 2.1 collective-permute-done.35.refs_1_
  210.9 10.6 %cross_backward.1 = (bf16[64,768]{1,0:T(8,128)(2,1)}, bf16[2,257,768]{2,1,0:T(8,128)(2,1)}, bf16[2,257,768]{2,1,0:T(8,128)(2,1)}, bf16[64,768]{1,0:T(8,128)(2,1)}, f32[64,768]{1,0:T(8,128)}, /*index=5*/f32[8,768]{1,0:T(8,128)}) custom-call(bf16[64,768]{1,0:T(8,128)(2,1)} %get-tuple-element.211.refs_0_, bf16[64,768]{1,0:T(8,128)(2,1)} %copy-done.35, ...), custom_call_target="tpu_custom_call" | custom-call | flops 7200000000 | bytes 24000000 | tf_op jit(solution)/shard_map/cross_backward/pallas_call | solution.py:617
  221.5 25.9 %cross_weights.1 = (bf16[384,4352]{1,0:T(8,128)(2,1)}, bf16[384,4352]{1,0:T(8,128)(2,1)}) custom-call(bf16[64,768]{1,0:T(8,128)(2,1)} %get-tuple-element.116.refs_0_, bf16[2,257,768]{2,1,0:T(8,128)(2,1)} %get-tuple-element.117.refs_1_.refs_0_, bf16[2,257,768]{2,1,0:T(8,128)(2,1)} %get-tuple-element.118.refs_2_.refs_1_, ...), custom_call_target="tpu_custom_call" | custom-call | flops 11699999744 | bytes 39000000 | tf_op jit(solution)/shard_map/cross_weights/pallas_call | solution.py:617
  247.5 13.0 %self_backward.1 = (bf16[128,2304]{1,0:T(8,128)(2,1)}, f32[128,768]{1,0:T(8,128)}, bf16[384,3200]{1,0:T(8,128)(2,1)}, bf16[384,3200]{1,0:T(8,128)(2,1)}) custom-call(s32[2]{0:T(128)} %refs_0_.6, f32[64,768]{1,0:T(8,128)} %get-tuple-element.122.refs_1_, bf16[64,768]{1,0:T(8,128)(2,1)} %get-tuple-element.208.refs_2_, bf16[64,768]{1,0:T(8,128)(2,1)} %copy-done.33, ...), custom_call_target="tpu_custom_call" | custom-call | flops 7200000000 | bytes 24000000 | tf_op jit(solution)/shard_map/self_backward/pallas_call | solution.py:617
  260.5 1.7 copy-done.1
  262.2 5.0 %add_convert_fusion = (bf16[192,4352]{1,0:T(8,128)(2,1)}, bf16[192,4352]{1,0:T(8,128)(2,1)S(1)}) fusion(bf16[384,4352]{1,0:T(8,128)(2,1)} %copy-done.1, bf16[384,4352]{1,0:T(8,128)(2,1)} %get-tuple-element.132), kind=kLoop, calls=%fused_computation | loop fusion | flops 6684672 | bytes 10027008 | tf_op jit(solution)/shard_map/convert_element_type | solution.py:80
  269.9 2.4 collective-permute-done.44
  272.3 4.1 %add_convert_fusion.2 = (bf16[192,3200]{1,0:T(8,128)(2,1)S(1)}, bf16[192,3200]{1,0:T(8,128)(2,1)}) fusion(bf16[384,3200]{1,0:T(8,128)(2,1)} %collective-permute-done.44, bf16[384,3200]{1,0:T(8,128)(2,1)} %get-tuple-element.133), kind=kLoop, calls=%fused_computation.2 | loop fusion | flops 4915200 | bytes 7372800 | tf_op jit(solution)/shard_map/convert_element_type | solution.py:80
  277.9 11.5 %collective-permute-done.43 = bf16[192,4352]{1,0:T(8,128)(2,1)} collective-permute-done((bf16[192,4352]{1,0:T(8,128)(2,1)}, bf16[192,4352]{1,0:T(8,128)(2,1)}, u32[]{:S(2)}, u32[]{:S(2)}) %collective-permute-start.43) | collective-permute-done | bytes 1671200 | tf_op jit(solution)/shard_map/ppermute | solution.py:47
  289.4 3.0 add_convert_fusion.4
  293.9 8.4 %feature_grad.1 = f32[2,257,1408]{2,1,0:T(8,128)} custom-call(bf16[2,257,768]{2,1,0:T(8,128)(2,1)} %get-tuple-element.117.refs_1_.refs_0_, bf16[2,257,768]{2,1,0:T(8,128)(2,1)} %get-tuple-element.118.refs_2_.refs_1_, bf16[768,768]{1,0:T(8,128)(2,1)} %fusion.refs_2_.refs_1_.refs_3_.refs_7_.refs_9_, bf16[96,4352]{1,0:T(8,128)(2,1)} %copy-done.5, ...), custom_call_target="tpu_custom_call" | custom-call | flops 7200000000 | bytes 24000000 | tf_op jit(solution)/shard_map/feature_grad/pallas_call | solution.py:617
  302.3 8.4 %collective-permute-done.45 = bf16[192,3200]{1,0:T(8,128)(2,1)} collective-permute-done((bf16[192,3200]{1,0:T(8,128)(2,1)}, bf16[192,3200]{1,0:T(8,128)(2,1)}, u32[]{:S(2)}, u32[]{:S(2)}) %collective-permute-start.45) | collective-permute-done | bytes 1228832 | tf_op jit(solution)/shard_map/ppermute | solution.py:47
  310.7 1.6 add_convert_fusion.6
  315.3 7.2 %collective-permute-done.46 = bf16[96,3200]{1,0:T(8,128)(2,1)S(1)} collective-permute-done((bf16[96,3200]{1,0:T(8,128)(2,1)S(1)}, bf16[96,3200]{1,0:T(8,128)(2,1)S(1)}, u32[]{:S(2)}, u32[]{:S(2)}) %collective-permute-start.46) | collective-permute-done | bytes 614432 | tf_op jit(solution)/shard_map/ppermute | solution.py:47
  324.3 3.3 collective-permute-start.51
  327.6 6.2 %hidden_grad.1 = f32[128,768]{1,0:T(8,128)} custom-call(bf16[128,2304]{1,0:T(8,128)(2,1)} %get-tuple-element.130.refs_0_, f32[128,768]{1,0:T(8,128)} %get-tuple-element.131.refs_1_, bf16[768,768]{1,0:T(8,128)(2,1)} %fusion.refs_2_.refs_1_.refs_3_.refs_7_.refs_9_, bf16[96,3200]{1,0:T(8,128)(2,1)} %copy-done.10, bf16[96,3200]{1,0:T(8,128)(2,1)} %copy-done.26, ...), custom_call_target="tpu_custom_call" | custom-call | flops 7200000000 | bytes 24000000 | tf_op jit(solution)/shard_map/hidden_grad/pallas_call | solution.py:617
  333.9 3.1 copy.43
  340.1 4.9 %collective-permute-done.48 = bf16[48,3200]{1,0:T(8,128)(2,1)S(1)} collective-permute-done((bf16[48,3200]{1,0:T(8,128)(2,1)S(1)}, bf16[48,3200]{1,0:T(8,128)(2,1)S(1)}, u32[]{:S(2)}, u32[]{:S(2)}) %collective-permute-start.48) | collective-permute-done | bytes 307232 | tf_op jit(solution)/shard_map/ppermute | solution.py:47
  349.8 3.0 collective-permute-done.50
  (223 shorter events, 75.7 us)
Async XLA Ops:
  7.2 111.1 %all-gather.2.cloned.1.call-start = ((), (), s32[]{:S(2)}) async-start(), calls=%async_computation.2 | async-start | bytes 3194880 | tf_op jit(solution)/shard_map/all_gather | solution.py:676
  9.4 11.5 %collective-permute-start = (bf16[24,3200]{1,0:T(8,128)(2,1)}, bf16[24,3200]{1,0:T(8,128)(2,1)S(1)}, u32[]{:S(2)}, u32[]{:S(2)}) collective-permute-start(bf16[24,3200]{1,0:T(8,128)(2,1)} %get-tuple-element.82), channel_id=1, source_target_pairs={{0,16},{1,17},{2,18},{3,19},{4,20},{5,21},{6,22},{7,23},{8,24},{9,... | collective-permute-start | bytes 460808 | tf_op jit(solution)/shard_map/ppermute | solution.py:47
  21.9 11.9 %collective-permute-start.9 = (bf16[24,4352]{1,0:T(8,128)(2,1)S(1)}, bf16[24,4352]{1,0:T(8,128)(2,1)S(1)}, u32[]{:S(2)}, u32[]{:S(2)}) collective-permute-start(bf16[24,4352]{1,0:T(8,128)(2,1)S(1)} %pad_maximum_fusion.8), channel_id=1, source_target_pairs={{0,16},{1,17},{2,18},{3,19},{4,20},{5,21},{6,22},{7,23},{8,24},{9,... | collective-permute-start | bytes 626696 | tf_op jit(solution)/shard_map/ppermute | solution.py:47
  22.0 14.0 %collective-permute-start.1 = (bf16[48,3200]{1,0:T(8,128)(2,1)S(1)}, bf16[48,3200]{1,0:T(8,128)(2,1)S(1)}, u32[]{:S(2)}, u32[]{:S(2)}) collective-permute-start(bf16[48,3200]{1,0:T(8,128)(2,1)S(1)} %pad_maximum_fusion.5), channel_id=1, source_target_pairs={{0,8},{1,9},{2,10},{3,11},{4,12},{5,13},{6,14},{7,15},{8,0},{9,1},... | collective-permute-start | bytes 921608 | tf_op jit(solution)/shard_map/ppermute | solution.py:47
  36.0 10.8 %collective-permute-start.10 = (bf16[48,4352]{1,0:T(8,128)(2,1)S(1)}, bf16[48,4352]{1,0:T(8,128)(2,1)S(1)}, u32[]{:S(2)}, u32[]{:S(2)}) collective-permute-start(bf16[48,4352]{1,0:T(8,128)(2,1)S(1)} %pad_maximum_fusion.4), channel_id=1, source_target_pairs={{0,8},{1,9},{2,10},{3,11},{4,12},{5,13},{6,14},{7,15},{8,0},{9,1},... | collective-permute-start | bytes 1253384 | tf_op jit(solution)/shard_map/ppermute | solution.py:47
  36.1 10.8 %collective-permute-start.2 = (bf16[96,3200]{1,0:T(8,128)(2,1)S(1)}, bf16[96,3200]{1,0:T(8,128)(2,1)S(1)}, u32[]{:S(2)}, u32[]{:S(2)}) collective-permute-start(bf16[96,3200]{1,0:T(8,128)(2,1)S(1)} %pad_maximum_fusion.1.refs_3_.refs_14_), channel_id=1, source_target_pairs={{0,4},{1,5},{2,3},{3,2},{4,0},{5,1},{6,7},{7,6},{8,12},{9,13},{10,... | collective-permute-start | bytes 1843208 | tf_op jit(solution)/shard_map/ppermute | solution.py:47
  37.5 307.7 %reduce-scatter.5.cloned.1.call-start = ((), (), s32[]{:S(2)}) async-start(), calls=%async_computation.4 | async-start | bytes 1597440 | tf_op jit(solution)/shard_map/reduce_scatter | solution.py:766
  46.9 21.6 %collective-permute-start.11 = (bf16[96,4352]{1,0:T(8,128)(2,1)S(1)}, bf16[96,4352]{1,0:T(8,128)(2,1)}, u32[]{:S(2)}, u32[]{:S(2)}) collective-permute-start(bf16[96,4352]{1,0:T(8,128)(2,1)S(1)} %pad_maximum_fusion.refs_3_.refs_5_.refs_9_), channel_id=1, source_target_pairs={{0,4},{1,5},{2,3},{3,2},{4,0},{5,1},{6,7},{7,6},{8,12},{9,13},{10,... | collective-permute-start | bytes 2506760 | tf_op jit(solution)/shard_map/ppermute | solution.py:47
  48.2 21.6 %collective-permute-start.3 = (bf16[96,3200]{1,0:T(8,128)(2,1)S(1)}, bf16[96,3200]{1,0:T(8,128)(2,1)S(1)}, u32[]{:S(2)}, u32[]{:S(2)}) collective-permute-start(bf16[96,3200]{1,0:T(8,128)(2,1)S(1)} %pad_maximum_fusion.1.refs_3_.refs_14_), channel_id=1, source_target_pairs={{0,1},{1,0},{2,6},{3,7},{4,5},{5,4},{6,2},{7,3},{8,9},{9,8},{10,14... | collective-permute-start | bytes 1843208 | tf_op jit(solution)/shard_map/ppermute | solution.py:47
  49.8 20.1 %collective-permute-start.5 = (bf16[96,3200]{1,0:T(8,128)(2,1)S(1)}, bf16[96,3200]{1,0:T(8,128)(2,1)S(1)}, u32[]{:S(2)}, u32[]{:S(2)}) collective-permute-start(bf16[96,3200]{1,0:T(8,128)(2,1)S(1)} %pad_maximum_fusion.1.refs_3_.refs_14_), channel_id=1, source_target_pairs={{0,2},{1,3},{2,0},{3,1},{4,6},{5,7},{6,4},{7,5},{8,10},{9,11},{10,... | collective-permute-start | bytes 1843208 | tf_op jit(solution)/shard_map/ppermute | solution.py:47
  49.8 20.6 %collective-permute-start.4 = (bf16[96,3200]{1,0:T(8,128)(2,1)S(1)}, bf16[96,3200]{1,0:T(8,128)(2,1)}, u32[]{:S(2)}, u32[]{:S(2)}) collective-permute-start(bf16[96,3200]{1,0:T(8,128)(2,1)S(1)} %collective-permute-done.2.refs_4_.refs_15_), channel_id=1, source_target_pairs={{0,1},{1,0},{2,6},{3,7},{4,5},{5,4},{6,2},{7,3},{8,9},{9,8},{10,14... | collective-permute-start | bytes 1843208 | tf_op jit(solution)/shard_map/ppermute | solution.py:47
  50.3 28.8 %collective-permute-start.12 = (bf16[96,4352]{1,0:T(8,128)(2,1)S(1)}, bf16[96,4352]{1,0:T(8,128)(2,1)}, u32[]{:S(2)}, u32[]{:S(2)}) collective-permute-start(bf16[96,4352]{1,0:T(8,128)(2,1)S(1)} %pad_maximum_fusion.refs_3_.refs_5_.refs_9_), channel_id=1, source_target_pairs={{0,1},{1,0},{2,6},{3,7},{4,5},{5,4},{6,2},{7,3},{8,9},{9,8},{10,14... | collective-permute-start | bytes 2506760 | tf_op jit(solution)/shard_map/ppermute | solution.py:47
  68.5 19.5 %collective-permute-start.13 = (bf16[96,4352]{1,0:T(8,128)(2,1)}, bf16[96,4352]{1,0:T(8,128)(2,1)}, u32[]{:S(2)}, u32[]{:S(2)}) collective-permute-start(bf16[96,4352]{1,0:T(8,128)(2,1)} %collective-permute-done.11.refs_4_.refs_6_.refs_10_), channel_id=1, source_target_pairs={{0,1},{1,0},{2,6},{3,7},{4,5},{5,4},{6,2},{7,3},{8,9},{9,8},{10,14... | collective-permute-start | bytes 2506760 | tf_op jit(solution)/shard_map/ppermute | solution.py:47
  70.7 18.4 %collective-permute-start.8 = (bf16[96,3200]{1,0:T(8,128)(2,1)}, bf16[96,3200]{1,0:T(8,128)(2,1)}, u32[]{:S(2)}, u32[]{:S(2)}) collective-permute-start(bf16[96,3200]{1,0:T(8,128)(2,1)} %collective-permute-done.4.refs_6_.refs_17_), channel_id=1, source_target_pairs={{0,2},{1,3},{2,0},{3,1},{4,6},{5,7},{6,4},{7,5},{8,10},{9,11},{10,... | collective-permute-start | bytes 1843208 | tf_op jit(solution)/shard_map/ppermute | solution.py:47
  72.7 34.5 %collective-permute-start.14 = (bf16[96,4352]{1,0:T(8,128)(2,1)S(1)}, bf16[96,4352]{1,0:T(8,128)(2,1)S(1)}, u32[]{:S(2)}, u32[]{:S(2)}) collective-permute-start(bf16[96,4352]{1,0:T(8,128)(2,1)S(1)} %pad_maximum_fusion.refs_3_.refs_5_.refs_9_), channel_id=1, source_target_pairs={{0,2},{1,3},{2,0},{3,1},{4,6},{5,7},{6,4},{7,5},{8,10},{9,11},{10,... | collective-permute-start | bytes 2506760 | tf_op jit(solution)/shard_map/ppermute | solution.py:47
  72.9 34.4 %collective-permute-start.15 = (bf16[96,4352]{1,0:T(8,128)(2,1)}, bf16[96,4352]{1,0:T(8,128)(2,1)}, u32[]{:S(2)}, u32[]{:S(2)}) collective-permute-start(bf16[96,4352]{1,0:T(8,128)(2,1)} %collective-permute-done.11.refs_4_.refs_6_.refs_10_), channel_id=1, source_target_pairs={{0,2},{1,3},{2,0},{3,1},{4,6},{5,7},{6,4},{7,5},{8,10},{9,11},{10,... | collective-permute-start | bytes 2506760 | tf_op jit(solution)/shard_map/ppermute | solution.py:47
  79.0 28.2 %collective-permute-start.16 = (bf16[96,4352]{1,0:T(8,128)(2,1)}, bf16[96,4352]{1,0:T(8,128)(2,1)}, u32[]{:S(2)}, u32[]{:S(2)}) collective-permute-start(bf16[96,4352]{1,0:T(8,128)(2,1)} %collective-permute-done.12.refs_5_.refs_7_.refs_11_), channel_id=1, source_target_pairs={{0,2},{1,3},{2,0},{3,1},{4,6},{5,7},{6,4},{7,5},{8,10},{9,11},{10,... | collective-permute-start | bytes 2506760 | tf_op jit(solution)/shard_map/ppermute | solution.py:47
  88.0 19.3 %collective-permute-start.17 = (bf16[96,4352]{1,0:T(8,128)(2,1)}, bf16[96,4352]{1,0:T(8,128)(2,1)}, u32[]{:S(2)}, u32[]{:S(2)}) collective-permute-start(bf16[96,4352]{1,0:T(8,128)(2,1)} %collective-permute-done.13.refs_6_.refs_8_.refs_12_), channel_id=1, source_target_pairs={{0,2},{1,3},{2,0},{3,1},{4,6},{5,7},{6,4},{7,5},{8,10},{9,11},{10,... | collective-permute-start | bytes 2506760 | tf_op jit(solution)/shard_map/ppermute | solution.py:47
  96.5 4.9 %collective-permute-start.24 = (bf16[64,768]{1,0:T(8,128)(2,1)}, bf16[64,768]{1,0:T(8,128)(2,1)S(1)}, u32[]{:S(2)}, u32[]{:S(2)}) collective-permute-start(bf16[64,768]{1,0:T(8,128)(2,1)} %get-tuple-element.96), channel_id=1, source_target_pairs={{0,4},{1,5},{2,3},{3,2},{4,0},{5,1},{6,7},{7,6},{8,12},{9,13},{10,... | collective-permute-start | bytes 294920 | tf_op jit(solution)/shard_map/ppermute | solution.py:47
  101.4 5.7 %collective-permute-start.25 = (bf16[128,768]{1,0:T(8,128)(2,1)S(1)}, bf16[128,768]{1,0:T(8,128)(2,1)S(1)}, u32[]{:S(2)}, u32[]{:S(2)}) collective-permute-start(bf16[128,768]{1,0:T(8,128)(2,1)S(1)} %pad_maximum_fusion.10), channel_id=1, source_target_pairs={{0,1},{1,0},{2,6},{3,7},{4,5},{5,4},{6,2},{7,3},{8,9},{9,8},{10,14... | collective-permute-start | bytes 589832 | tf_op jit(solution)/shard_map/ppermute | solution.py:47
  107.2 11.1 %collective-permute-start.26 = (bf16[256,768]{1,0:T(8,128)(2,1)S(1)}, bf16[256,768]{1,0:T(8,128)(2,1)S(1)}, u32[]{:S(2)}, u32[]{:S(2)}) collective-permute-start(bf16[256,768]{1,0:T(8,128)(2,1)S(1)} %constant_dynamic-update-slice_fusion.3.refs_0_.refs_2_), channel_id=1, source_target_pairs={{0,2},{1,3},{2,0},{3,1},{4,6},{5,7},{6,4},{7,5},{8,10},{9,11},{10,... | collective-permute-start | bytes 1179656 | tf_op jit(solution)/shard_map/ppermute | solution.py:47
  123.9 14.8 %collective-permute-start.27 = (bf16[256,768]{1,0:T(8,128)(2,1)}, bf16[256,768]{1,0:T(8,128)(2,1)S(1)}, u32[]{:S(2)}, u32[]{:S(2)}) collective-permute-start(bf16[256,768]{1,0:T(8,128)(2,1)} %get-tuple-element.98), channel_id=1, source_target_pairs={{0,2},{1,3},{2,0},{3,1},{4,6},{5,7},{6,4},{7,5},{8,10},{9,11},{10,... | collective-permute-start | bytes 1179656 | tf_op jit(solution)/shard_map/ppermute | solution.py:47
  132.1 4.9 %collective-permute-start.18 = (bf16[64,768]{1,0:T(8,128)(2,1)}, bf16[64,768]{1,0:T(8,128)(2,1)S(1)}, u32[]{:S(2)}, u32[]{:S(2)}) collective-permute-start(bf16[64,768]{1,0:T(8,128)(2,1)} %get-tuple-element.90), channel_id=1, source_target_pairs={{0,4},{1,5},{2,3},{3,2},{4,0},{5,1},{6,7},{7,6},{8,12},{9,13},{10,... | collective-permute-start | bytes 294920 | tf_op jit(solution)/shard_map/ppermute | solution.py:47
  137.9 5.7 %collective-permute-start.19 = (bf16[128,768]{1,0:T(8,128)(2,1)S(1)}, bf16[128,768]{1,0:T(8,128)(2,1)S(1)}, u32[]{:S(2)}, u32[]{:S(2)}) collective-permute-start(bf16[128,768]{1,0:T(8,128)(2,1)S(1)} %pad_maximum_fusion.9), channel_id=1, source_target_pairs={{0,1},{1,0},{2,6},{3,7},{4,5},{5,4},{6,2},{7,3},{8,9},{9,8},{10,14... | collective-permute-start | bytes 589832 | tf_op jit(solution)/shard_map/ppermute | solution.py:47
  138.8 7.0 %collective-permute-start.28 = (bf16[128,768]{1,0:T(8,128)(2,1)S(1)}, bf16[128,768]{1,0:T(8,128)(2,1)S(1)}, u32[]{:S(2)}, u32[]{:S(2)}) collective-permute-start(bf16[128,768]{1,0:T(8,128)(2,1)S(1)} %get-tuple-element.199), channel_id=1, source_target_pairs={{0,1},{1,0},{2,6},{3,7},{4,5},{5,4},{6,2},{7,3},{8,9},{9,8},{10,14... | collective-permute-start | bytes 589832 | tf_op jit(solution)/shard_map/ppermute | solution.py:47
  146.5 7.2 %collective-permute-start.29 = (bf16[64,768]{1,0:T(8,128)(2,1)S(1)}, bf16[64,768]{1,0:T(8,128)(2,1)S(1)}, u32[]{:S(2)}, u32[]{:S(2)}) collective-permute-start(bf16[64,768]{1,0:T(8,128)(2,1)S(1)} %get-tuple-element.214), channel_id=1, source_target_pairs={{0,4},{1,5},{2,3},{3,2},{4,0},{5,1},{6,7},{7,6},{8,12},{9,13},{10,... | collective-permute-start | bytes 294920 | tf_op jit(solution)/shard_map/ppermute | solution.py:47
  156.6 5.9 %collective-permute-start.36 = (bf16[64,768]{1,0:T(8,128)(2,1)}, bf16[64,768]{1,0:T(8,128)(2,1)S(1)}, u32[]{:S(2)}, u32[]{:S(2)}) collective-permute-start(bf16[64,768]{1,0:T(8,128)(2,1)} %get-tuple-element.106), channel_id=1, source_target_pairs={{0,4},{1,5},{2,3},{3,2},{4,0},{5,1},{6,7},{7,6},{8,12},{9,13},{10,... | collective-permute-start | bytes 294920 | tf_op jit(solution)/shard_map/ppermute | solution.py:47
  157.2 5.8 %collective-permute-start.22 = (bf16[128,768]{1,0:T(8,128)(2,1)S(1)}, bf16[128,768]{1,0:T(8,128)(2,1)S(1)}, u32[]{:S(2)}, u32[]{:S(2)}) collective-permute-start(bf16[128,768]{1,0:T(8,128)(2,1)S(1)} %get-tuple-element.197), channel_id=1, source_target_pairs={{0,1},{1,0},{2,6},{3,7},{4,5},{5,4},{6,2},{7,3},{8,9},{9,8},{10,14... | collective-permute-start | bytes 589832 | tf_op jit(solution)/shard_map/ppermute | solution.py:47
  162.5 10.0 %collective-permute-start.37 = (bf16[128,768]{1,0:T(8,128)(2,1)S(1)}, bf16[128,768]{1,0:T(8,128)(2,1)S(1)}, u32[]{:S(2)}, u32[]{:S(2)}) collective-permute-start(bf16[128,768]{1,0:T(8,128)(2,1)S(1)} %pad_maximum_fusion.13), channel_id=1, source_target_pairs={{0,1},{1,0},{2,6},{3,7},{4,5},{5,4},{6,2},{7,3},{8,9},{9,8},{10,14... | collective-permute-start | bytes 589832 | tf_op jit(solution)/shard_map/ppermute | solution.py:47
  163.7 4.6 %collective-permute-start.23 = (bf16[64,768]{1,0:T(8,128)(2,1)S(1)}, bf16[64,768]{1,0:T(8,128)(2,1)S(1)}, u32[]{:S(2)}, u32[]{:S(2)}) collective-permute-start(bf16[64,768]{1,0:T(8,128)(2,1)S(1)} %get-tuple-element.212), channel_id=1, source_target_pairs={{0,4},{1,5},{2,3},{3,2},{4,0},{5,1},{6,7},{7,6},{8,12},{9,13},{10,... | collective-permute-start | bytes 294920 | tf_op jit(solution)/shard_map/ppermute | solution.py:47
  171.1 4.8 %collective-permute-start.30 = (bf16[64,768]{1,0:T(8,128)(2,1)}, bf16[64,768]{1,0:T(8,128)(2,1)S(1)}, u32[]{:S(2)}, u32[]{:S(2)}) collective-permute-start(bf16[64,768]{1,0:T(8,128)(2,1)} %get-tuple-element.101), channel_id=1, source_target_pairs={{0,4},{1,5},{2,3},{3,2},{4,0},{5,1},{6,7},{7,6},{8,12},{9,13},{10,... | collective-permute-start | bytes 294920 | tf_op jit(solution)/shard_map/ppermute | solution.py:47
  172.5 10.2 %collective-permute-start.38 = (bf16[256,768]{1,0:T(8,128)(2,1)S(1)}, bf16[256,768]{1,0:T(8,128)(2,1)S(1)}, u32[]{:S(2)}, u32[]{:S(2)}) collective-permute-start(bf16[256,768]{1,0:T(8,128)(2,1)S(1)} %constant_dynamic-update-slice_fusion.9.refs_0_), channel_id=1, source_target_pairs={{0,2},{1,3},{2,0},{3,1},{4,6},{5,7},{6,4},{7,5},{8,10},{9,11},{10,... | collective-permute-start | bytes 1179656 | tf_op jit(solution)/shard_map/ppermute | solution.py:47
  176.9 5.7 %collective-permute-start.31 = (bf16[128,768]{1,0:T(8,128)(2,1)S(1)}, bf16[128,768]{1,0:T(8,128)(2,1)S(1)}, u32[]{:S(2)}, u32[]{:S(2)}) collective-permute-start(bf16[128,768]{1,0:T(8,128)(2,1)S(1)} %pad_maximum_fusion.12), channel_id=1, source_target_pairs={{0,1},{1,0},{2,6},{3,7},{4,5},{5,4},{6,2},{7,3},{8,9},{9,8},{10,14... | collective-permute-start | bytes 589832 | tf_op jit(solution)/shard_map/ppermute | solution.py:47
  182.6 7.5 %collective-permute-start.32 = (bf16[256,768]{1,0:T(8,128)(2,1)S(1)}, bf16[256,768]{1,0:T(8,128)(2,1)S(1)}, u32[]{:S(2)}, u32[]{:S(2)}) collective-permute-start(bf16[256,768]{1,0:T(8,128)(2,1)S(1)} %constant_dynamic-update-slice_fusion.6.refs_0_), channel_id=1, source_target_pairs={{0,2},{1,3},{2,0},{3,1},{4,6},{5,7},{6,4},{7,5},{8,10},{9,11},{10,... | collective-permute-start | bytes 1179656 | tf_op jit(solution)/shard_map/ppermute | solution.py:47
  189.6 7.5 %collective-permute-start.39 = (bf16[256,768]{1,0:T(8,128)(2,1)}, bf16[256,768]{1,0:T(8,128)(2,1)S(1)}, u32[]{:S(2)}, u32[]{:S(2)}) collective-permute-start(bf16[256,768]{1,0:T(8,128)(2,1)} %get-tuple-element.110), channel_id=1, source_target_pairs={{0,2},{1,3},{2,0},{3,1},{4,6},{5,7},{6,4},{7,5},{8,10},{9,11},{10,... | collective-permute-start | bytes 1179656 | tf_op jit(solution)/shard_map/ppermute | solution.py:47
  197.1 5.7 %collective-permute-start.40 = (bf16[128,768]{1,0:T(8,128)(2,1)S(1)}, bf16[128,768]{1,0:T(8,128)(2,1)S(1)}, u32[]{:S(2)}, u32[]{:S(2)}) collective-permute-start(bf16[128,768]{1,0:T(8,128)(2,1)S(1)} %get-tuple-element.193), channel_id=1, source_target_pairs={{0,1},{1,0},{2,6},{3,7},{4,5},{5,4},{6,2},{7,3},{8,9},{9,8},{10,14... | collective-permute-start | bytes 589832 | tf_op jit(solution)/shard_map/ppermute | solution.py:47
  199.0 6.0 %collective-permute-start.34 = (bf16[128,768]{1,0:T(8,128)(2,1)S(1)}, bf16[128,768]{1,0:T(8,128)(2,1)S(1)}, u32[]{:S(2)}, u32[]{:S(2)}) collective-permute-start(bf16[128,768]{1,0:T(8,128)(2,1)S(1)} %get-tuple-element.195), channel_id=1, source_target_pairs={{0,1},{1,0},{2,6},{3,7},{4,5},{5,4},{6,2},{7,3},{8,9},{9,8},{10,14... | collective-permute-start | bytes 589832 | tf_op jit(solution)/shard_map/ppermute | solution.py:47
  247.4 13.1 %collective-permute-start.42 = (bf16[384,4352]{1,0:T(8,128)(2,1)}, bf16[384,4352]{1,0:T(8,128)(2,1)S(1)}, u32[]{:S(2)}, u32[]{:S(2)}) collective-permute-start(bf16[384,4352]{1,0:T(8,128)(2,1)} %get-tuple-element.121), channel_id=1, source_target_pairs={{0,2},{1,3},{2,0},{3,1},{4,6},{5,7},{6,4},{7,5},{8,10},{9,11},{10,... | collective-permute-start | bytes 10027016 | tf_op jit(solution)/shard_map/ppermute | solution.py:47
  247.4 97.7 %reduce-scatter.3.cloned.1.call-start = ((), (), s32[]{:S(2)}) async-start(), calls=%async_computation.3 | async-start | bytes 1597440 | tf_op jit(solution)/shard_map/reduce_scatter | solution.py:766
  267.1 5.1 %collective-permute-start.44 = (bf16[384,3200]{1,0:T(8,128)(2,1)}, bf16[384,3200]{1,0:T(8,128)(2,1)}, u32[]{:S(2)}, u32[]{:S(2)}) collective-permute-start(bf16[384,3200]{1,0:T(8,128)(2,1)} %get-tuple-element.135), channel_id=1, source_target_pairs={{0,2},{1,3},{2,0},{3,1},{4,6},{5,7},{6,4},{7,5},{8,10},{9,11},{10,... | collective-permute-start | bytes 7372808 | tf_op jit(solution)/shard_map/ppermute | solution.py:47
  267.6 21.8 %collective-permute-start.43 = (bf16[192,4352]{1,0:T(8,128)(2,1)}, bf16[192,4352]{1,0:T(8,128)(2,1)}, u32[]{:S(2)}, u32[]{:S(2)}) collective-permute-start(bf16[192,4352]{1,0:T(8,128)(2,1)} %get-tuple-element.180), channel_id=1, source_target_pairs={{0,1},{1,0},{2,6},{3,7},{4,5},{5,4},{6,2},{7,3},{8,9},{9,8},{10,14... | collective-permute-start | bytes 5013512 | tf_op jit(solution)/shard_map/ppermute | solution.py:47
  276.4 34.3 %collective-permute-start.45 = (bf16[192,3200]{1,0:T(8,128)(2,1)}, bf16[192,3200]{1,0:T(8,128)(2,1)}, u32[]{:S(2)}, u32[]{:S(2)}) collective-permute-start(bf16[192,3200]{1,0:T(8,128)(2,1)} %get-tuple-element.183), channel_id=1, source_target_pairs={{0,1},{1,0},{2,6},{3,7},{4,5},{5,4},{6,2},{7,3},{8,9},{9,8},{10,14... | collective-permute-start | bytes 3686408 | tf_op jit(solution)/shard_map/ppermute | solution.py:47
  292.5 21.3 %collective-permute-start.47 = (bf16[96,4352]{1,0:T(8,128)(2,1)}, bf16[96,4352]{1,0:T(8,128)(2,1)S(1)}, u32[]{:S(2)}, u32[]{:S(2)}) collective-permute-start(bf16[96,4352]{1,0:T(8,128)(2,1)} %get-tuple-element.185), channel_id=1, source_target_pairs={{0,4},{1,5},{2,3},{3,2},{4,0},{5,1},{6,7},{7,6},{8,12},{9,13},{10,... | collective-permute-start | bytes 2506760 | tf_op jit(solution)/shard_map/ppermute | solution.py:47
  312.3 10.2 %collective-permute-start.46 = (bf16[96,3200]{1,0:T(8,128)(2,1)S(1)}, bf16[96,3200]{1,0:T(8,128)(2,1)S(1)}, u32[]{:S(2)}, u32[]{:S(2)}) collective-permute-start(bf16[96,3200]{1,0:T(8,128)(2,1)S(1)} %get-tuple-element.186), channel_id=1, source_target_pairs={{0,4},{1,5},{2,3},{3,2},{4,0},{5,1},{6,7},{7,6},{8,12},{9,13},{10,... | collective-permute-start | bytes 1843208 | tf_op jit(solution)/shard_map/ppermute | solution.py:47
  314.0 9.5 %collective-permute-start.49 = (bf16[48,4352]{1,0:T(8,128)(2,1)S(1)}, bf16[48,4352]{1,0:T(8,128)(2,1)S(1)}, u32[]{:S(2)}, u32[]{:S(2)}) collective-permute-start(bf16[48,4352]{1,0:T(8,128)(2,1)S(1)} %get-tuple-element.189), channel_id=1, source_target_pairs={{0,8},{1,9},{2,10},{3,11},{4,12},{5,13},{6,14},{7,15},{8,0},{9,1},... | collective-permute-start | bytes 1253384 | tf_op jit(solution)/shard_map/ppermute | solution.py:47
  324.3 13.4 %collective-permute-start.51 = (bf16[24,4352]{1,0:T(8,128)(2,1)}, bf16[24,4352]{1,0:T(8,128)(2,1)}, u32[]{:S(2)}, u32[]{:S(2)}) collective-permute-start(bf16[24,4352]{1,0:T(8,128)(2,1)} %add_convert_fusion.13), channel_id=1, source_target_pairs={{0,16},{1,17},{2,18},{3,19},{4,20},{5,21},{6,22},{7,23},{8,24},{9,... | collective-permute-start | bytes 626696 | tf_op jit(solution)/shard_map/ppermute | solution.py:47
  337.0 8.0 %collective-permute-start.48 = (bf16[48,3200]{1,0:T(8,128)(2,1)S(1)}, bf16[48,3200]{1,0:T(8,128)(2,1)S(1)}, u32[]{:S(2)}, u32[]{:S(2)}) collective-permute-start(bf16[48,3200]{1,0:T(8,128)(2,1)S(1)} %copy-done.15), channel_id=1, source_target_pairs={{0,8},{1,9},{2,10},{3,11},{4,12},{5,13},{6,14},{7,15},{8,0},{9,1},... | collective-permute-start | bytes 921608 | tf_op jit(solution)/shard_map/ppermute | solution.py:47
  345.0 7.8 %collective-permute-start.50 = (bf16[24,3200]{1,0:T(8,128)(2,1)S(1)}, bf16[24,3200]{1,0:T(8,128)(2,1)S(1)}, u32[]{:S(2)}, u32[]{:S(2)}) collective-permute-start(bf16[24,3200]{1,0:T(8,128)(2,1)S(1)} %add_convert_fusion.22), channel_id=1, source_target_pairs={{0,16},{1,17},{2,18},{3,19},{4,20},{5,21},{6,22},{7,23},{8,24},{9,... | collective-permute-start | bytes 460808 | tf_op jit(solution)/shard_map/ppermute | solution.py:47
  (44 other events, 333.1 us)
Sparse Core Ops, SparseCore 0:
  37.6 54.3 all-gather.1
  247.5 31.3 reduce-scatter.4
  281.2 29.5 reduce-scatter.2
where the time goes:
time: 368 us; the launch traced here: 365 us
  waiting for transfers between devices  129 us (35%)
  Pallas kernels  117 us (32%)
  starting transfers between devices  52.2 us (14%)
  other arithmetic  30.6 us (8%)
  local copies, waits for them, and re-layouts  20.7 us (6%)
  between operations  14.7 us (4%)
    ppermute x52, waiting for transfers between devices, swap(): return lax.ppermute(value, AXES, pairs(count, move))  129 us
    pallas_call x15, Pallas kernels, kernel_call(): pl.pallas_call(lambda *refs: body(refs), name=name, out_shape=outs, in_sp...  117 us
    ppermute x52, starting transfers between devices, swap(): return lax.ppermute(value, AXES, pairs(count, move))  52.1 us
    convert_element_type x16, other arithmetic, add_low(): return (left.astype(F32) + right.astype(F32)).astype(BF)  18.7 us
    unnamed x89, local copies, waits for them, and re-layouts  18.7 us
  transfers between devices with their start and end apart: 55, of which 28 were waited for; matrix products, arithmetic and copies ran while one was open for 10% of the time, Pallas kernels for 20%

commit v1 on v0

--- a/solution.py
+++ b/solution.py
@@ -13,6 +13,7 @@
 PER = GROUP // HEAD
 eps = 1e-06
 masked_off = 1000000000.0
+LATE = 4
 AXES = ("z", "x", "c", "y")
 BF = jnp.bfloat16
 F32 = jnp.float32
@@ -51,24 +52,35 @@
     return swap(value, lambda z, x, c, y: (z ^ distance, x, c, y))
 
 
-def gather_z(unit, *gates):
+def gather_z(unit):
     if lax.axis_size("z") == 4:
         near = jnp.concatenate([unit, swap_z(unit, 2)], axis=0)
-        near = after(near, *gates)
-        return near, jnp.concatenate([near, swap_z(near, 1)], axis=0)
-    near = lax.all_gather(unit, "z", axis=0, tiled=True)
-    return near, near
-
-
-def gather_all(near):
-    a, b = swap(near, step_a), swap(near, step_b)
+        return jnp.concatenate([near, swap_z(near, 1)], axis=0)
+    return lax.all_gather(unit, "z", axis=0, tiled=True)
+
+
+def gather_z_direct(unit):
+    if lax.axis_size("z") == 4:
+        one, two, three = (swap_z(unit, k) for k in (1, 2, 3))
+        return jnp.concatenate([unit, two, one, three], axis=0)
+    return lax.all_gather(unit, "z", axis=0, tiled=True)
+
+
+def gather_all(near, first=(), last=()):
+    a = swap(after(near, *first), step_a)
+    b = swap(after(near, *last), step_b)
     pieces = [near, a, b, swap(a, step_b)]
-    return pieces + [swap(piece, step_c) for piece in pieces]
-
-
-def gather_plane(rows):
-    for move in (step_a, step_b):
-        rows = jnp.concatenate([rows, swap(rows, move)], axis=0)
+    pieces.append(swap(after(near, *last), step_c))
+    return pieces + [swap(piece, step_c) for piece in pieces[1:3]]
+
+
+def finish_all(pieces, *gates):
+    return pieces + [swap(after(pieces[3], *gates), step_c)]
+
+
+def gather_plane(rows, first=(), second=()):
+    rows = jnp.concatenate([rows, after(swap(rows, step_a), *first)], axis=0)
+    rows = jnp.concatenate([rows, after(swap(rows, step_b), *second)], axis=0)
     return [rows, swap(rows, step_c)]
 
 
@@ -229,6 +241,18 @@
     grad_query = fold_heads(dot(grad_score, k), masks, count) * HEAD ** (-0.5)
     grad_key = outer(grad_score, q) * HEAD ** (-0.5)
     return grad_query.astype(BF), grad_key.astype(BF), grad_value
+
+
+def repeat(count, body):
+    def step(i, carry):
+        body(i)
+        return carry
+
+    lax.fori_loop(0, count, step, 0)
+
+
+def stretch(i, count):
+    return pl.ds(pl.multiple_of(i * count, count), count)
 
 
 def fetch(pieces, start, target, sems):
@@ -295,8 +319,9 @@
         qkv_ref[:, cols] = (dot(hidden_slot, w_ref[:, cols]) + bias[n]).astype(BF)
     masks = head_masks()
     count = rows_all // items
-    for i in range(items):
-        rows = pl.ds(i * count, count)
+
+    def attend(i):
+        rows = stretch(i, count)
         mask_add = self_mask(length_ref[i], count)
         for g in range(width // GROUP):
             cols = [pl.ds(n * width + g * GROUP, GROUP) for n in range(3)]
@@ -305,6 +330,8 @@
             weights = softmax_rows(scores).astype(BF)
             mixed = dot(weights, qkv_ref[rows, cols[2]])
             mix_ref[rows, cols[0]] = fold_heads(mixed, masks, count).astype(BF)
+
+    repeat(items, attend)
     mixture_slot = by_slot(mix_ref[...], order)
     pre = dot(mixture_slot, w_ref[:, pl.ds(3 * width, width)])
     pre = pre + vec[2:3] + hidden_ref[...].astype(F32)
@@ -327,12 +354,15 @@
     order = order_ref[...]
     bias_slot = dot_t(vec_ref[...].astype(BF), order)[12:13]
     finish(copies)
-    for i in range(items):
+
+    def project(i):
         rows = feature_ref[i]
         keys = dot_t(rows, w_ref[:, pl.ds(0, image_width)])
-        key_ref[i] = by_place(keys, order).astype(BF)
+        key_ref[i] = by_place(keys, order_ref[...]).astype(BF)
         values = dot_t(rows, w_ref[:, pl.ds(image_width, image_width)]) + bias_slot
-        value_ref[i] = by_place(values, order).astype(BF)
+        value_ref[i] = by_place(values, order_ref[...]).astype(BF)
+
+    repeat(items, project)
 
 
 def cross_forward_kernel(start, n_pieces, refs):
@@ -349,14 +379,17 @@
     first_slot = by_slot(first_ref[...].astype(BF), order)
     finish(copies)
     rows_ref[...] = (dot(first_slot, w_ref[:, pl.ds(0, width)]) + vec[11:12]).astype(BF)
-    for i in range(items):
-        rows = pl.ds(i * count, count)
+
+    def attend(i):
+        rows = stretch(i, count)
         for g in range(width // GROUP):
             cols = pl.ds(g * GROUP, GROUP)
             q = spread_heads(rows_ref[rows, cols], masks)
             scores = dot_t(q, key_ref[i, :, cols]) * HEAD ** (-0.5)
             mixed = dot(softmax_rows(scores).astype(BF), value_ref[i, :, cols])
             look_ref[rows, cols] = fold_heads(mixed, masks, count).astype(BF)
+
+    repeat(items, attend)
     pre = dot(by_slot(look_ref[...], order), w_ref[:, pl.ds(width, width)])
     pre = pre + vec[13:14] + first_ref[...]
     pre_ref[...] = pre
@@ -430,7 +463,9 @@
 def cross_backward_kernel(start, n_pieces, refs):
     kept_ref, got_ref, sum_ref, pre_ref, q_ref, k_ref, v_ref, order_ref, vec_ref = refs[:9]
     pieces = refs[9 : 9 + n_pieces]
-    dq_ref, dk_ref, dv_ref, low_ref, first_ref, row_ref, w_ref, sems = refs[9 + n_pieces :]
+    dq_ref, dk_ref, dv_ref, low_ref, first_ref, row_ref, w_ref, look_ref, sems = refs[
+        9 + n_pieces :
+    ]
     copies = fetch(pieces, start, w_ref, sems)
     items = k_ref.shape[0]
     width = q_ref.shape[1]
@@ -443,35 +478,34 @@
     low = grad_two.astype(BF)
     low_ref[...] = low
     finish(copies)
-    looked = by_place(dot_t(low, w_ref[:, pl.ds(width, width)]), order).astype(BF)
-    value_sum = []
-    for g in range(width // GROUP):
-        cols = pl.ds(g * GROUP, GROUP)
-        total = None
-        for i in range(items):
-            rows = pl.ds(i * count, count)
+    look_ref[...] = by_place(dot_t(low, w_ref[:, pl.ds(width, width)]), order).astype(BF)
+
+    def attend(i):
+        rows = stretch(i, count)
+        for g in range(width // GROUP):
+            cols = pl.ds(g * GROUP, GROUP)
             dq, dk, dv = attend_group_back(
                 q_ref[rows, cols],
                 k_ref[i, :, cols],
                 v_ref[i, :, cols],
                 F32(0.0),
-                looked[i * count : (i + 1) * count, g * GROUP : (g + 1) * GROUP],
+                look_ref[rows, cols],
                 masks,
                 count,
             )
             dq_ref[rows, cols] = dq
             dk_ref[i, :, cols] = dk
             dv_ref[i, :, cols] = dv
-            part = column_sum(dv)
-            total = part if total is None else total + part
-        value_sum.append(total)
+            row_ref[3:4, cols] = row_ref[3:4, cols] + column_sum(dv)
+
+    row_ref[3:4, :] = jnp.zeros((1, width), F32)
+    repeat(items, attend)
     grad_cross = dq_ref[...]
     back = dot_t(grad_cross, w_ref[:, pl.ds(0, width)])
     first_ref[...] = grad_two + by_place(back, order)
     row_ref[0:1, :] = gain_grad
     row_ref[1:2, :] = shift_grad
     row_ref[2:3, :] = column_sum(grad_cross)
-    row_ref[3:4, :] = jnp.concatenate(value_sum, axis=1)
     row_ref[4:5, :] = column_sum(low)
 
 
@@ -502,12 +536,14 @@
     out_ref, w_ref, sems = refs[3 + n_pieces :]
     items, _, image_width = out_ref.shape
     copies = fetch(pieces, 0, w_ref, sems)
-    order = order_ref[...]
-    slots = [[by_slot(ref[i], order) for ref in (dk_ref, dv_ref)] for i in range(items)]
     finish(copies)
-    for i in range(items):
-        total = dot(slots[i][0], w_ref[:, pl.ds(0, image_width)])
-        out_ref[i] = total + dot(slots[i][1], w_ref[:, pl.ds(image_width, image_width)])
+
+    def back(i):
+        keys, values = (by_slot(ref[i], order_ref[...]) for ref in (dk_ref, dv_ref))
+        total = dot(keys, w_ref[:, pl.ds(0, image_width)])
+        out_ref[i] = total + dot(values, w_ref[:, pl.ds(image_width, image_width)])
+
+    repeat(items, back)
 
 
 def self_backward_kernel(items, n_pieces, refs):
@@ -515,7 +551,9 @@
     mix_ref, hidden_ref, order_ref, vec_ref = refs[7:11]
     row_refs = refs[11:14]
     pieces = refs[14 : 14 + n_pieces]
-    grad_ref, one_ref, g_kept_ref, g_sent_ref, w_ref, sum_ref, sems = refs[14 + n_pieces :]
+    grad_ref, one_ref, g_kept_ref, g_sent_ref, w_ref, sum_ref, mixed_ref, sems = refs[
+        14 + n_pieces :
+    ]
     copies = fetch(pieces, 3 * pre_ref.shape[1], w_ref, sems)
     rows_all, width = pre_ref.shape
     count = rows_all // items
@@ -534,22 +572,24 @@
     one_ref[...] = grad_one
     low = grad_one.astype(BF)
     finish(copies)
-    grad_mix = by_place(dot_t(low, w_ref[...]), order).astype(BF)
-    sums = [None, None, None]
-    for i in range(items):
-        rows = pl.ds(i * count, count)
+    mixed_ref[...] = by_place(dot_t(low, w_ref[...]), order).astype(BF)
+
+    def attend(i):
+        rows = stretch(i, count)
         mask_add = self_mask(length_ref[i], count)
         for g in range(width // GROUP):
             cols = [pl.ds(n * width + g * GROUP, GROUP) for n in range(3)]
             results = attend_group_back(
                 *[qkv_ref[rows, col] for col in cols],
                 mask_add,
-                grad_mix[i * count : (i + 1) * count, g * GROUP : (g + 1) * GROUP],
+                mixed_ref[rows, cols[0]],
                 masks,
                 count,
             )
             for col, value in zip(cols, results):
                 grad_ref[rows, col] = value
+
+    repeat(items, attend)
     query_rows, query_ends, text_ends = row_refs
     sum_ref[...] = jnp.zeros(sum_ref.shape, F32)
     total = column_sum(grad_ref[...])
@@ -578,9 +618,12 @@
     for part, out_ref in enumerate((g_kept_ref, g_sent_ref)):
         block = order_ref[pl.ds(part * half, half), :]
         turned = by_slot_turned(hidden_ref[...], block)
-        for n in range(3):
-            cols = pl.ds(n * width, width)
+
+        def weigh(n):
+            cols = stretch(n, width)
             out_ref[:, cols] = dot(turned, grad_ref[:, cols]).astype(BF)
+
+        repeat(3, weigh)
         turned = by_slot_turned(mix_ref[...], block)
         out_ref[:, pl.ds(3 * width, width)] = dot(turned, low).astype(BF)
         out_ref[:, pl.ds(4 * width, 128)] = dot_t(block, sums).astype(BF)
@@ -592,7 +635,13 @@
     out_ref, w_ref, sems = refs[3 + n_pieces :]
     copies = fetch(pieces, 0, w_ref, sems)
     finish(copies)
-    back = dot_t(grad_ref[...], w_ref[...])
+    width = one_ref.shape[1]
+
+    def part(n, total):
+        cols = stretch(n, width)
+        return total + dot_t(grad_ref[:, cols], w_ref[:, cols])
+
+    back = lax.fori_loop(0, 3, part, jnp.zeros(one_ref.shape, F32))
     out_ref[...] = one_ref[...] + by_place(back, order_ref[...])
 
 
@@ -674,10 +723,10 @@
         [image_turned[0], image_turned[1], cross_query, cross_output], axis=1
     )
     w_ff = [lax.all_gather(unit_ff, "z", axis=0, tiled=True)]
-    half_self, near_self = gather_z(unit_self)
-    w_self = gather_all(near_self)
-    near_cross = gather_z(after(unit_cross, half_self), near_self)[1]
-    w_cross = gather_all(after(near_cross, w_self[1]))
+    near_self = gather_z_direct(unit_self)
+    w_self = finish_all(gather_all(near_self))
+    near_cross = gather_z(after(unit_cross, near_self))
+    w_cross = gather_all(near_cross, w_self[1:3], w_self[3:4])
     cross_start = 2 * image_width
 
     qkv, mixture, pre_one, first_query, first_text, text_low, vec = kernel_call(
@@ -698,6 +747,7 @@
         text_lengths,
     )
 
+    w_cross = finish_all(w_cross, first_query)
     wide = shaped(items, image_rows, width, kind=BF)
     image_keys, image_values = kernel_call(
         part(image_kernel, len(w_cross)),
@@ -725,7 +775,10 @@
     branches = [None, None]
     for j, values, low in ((1, first_text, text_low), (0, second, second_low)):
         count = values.shape[0]
-        low_all = gather_plane(low)
+        if j:
+            low_all = gather_plane(low, (image_keys,), (second_low,))
+        else:
+            low_all = gather_plane(low)
         half = 4 * count
         pre_act, active, kept, sent = kernel_call(
             part(branch_up_kernel, j, len(w_ff)),
@@ -786,18 +839,10 @@
         (query[3][0], query_got, query[1], pre_two, cross_rows, image_keys, image_values, order, vec),
         w_cross,
         2 * width,
-    )
-    packed = shaped(width // 2, cross_start + 2 * width, kind=BF)
-    cross_kept, cross_sent = kernel_call(
-        cross_weights_kernel,
-        "cross_weights",
-        (packed, packed),
-        (grad_cross, grad_ikey, grad_ivalue, two_low, first_query, looked, features, order),
-        cost=13,
-    )
-    grad_first = after(grad_first, cross_sent)
-    cross_kept, cross_sent = halved(cross_kept, swap(cross_sent, step_c))
-
+        extra=(pltpu.VMEM((query_rows, width), BF),),
+        cost=LATE,
+    )
+    grad_first = after(grad_first, branches[1][4])
     packed = shaped(width // 2, 4 * width + 128, kind=BF)
     grad_qkv, grad_one, kept, sent = kernel_call(
         part(self_backward_kernel, items, len(w_self)),
@@ -820,33 +865,11 @@
         w_self,
         width,
         text_lengths,
-        (pltpu.VMEM((128, width), F32),),
-    )
-    sent = after(sent, cross_sent)
-    cross_got = swap(cross_sent, step_b)
-    kept, sent = halved(kept, swap(sent, step_c))
+        (pltpu.VMEM((128, width), F32), pltpu.VMEM((rows, width), BF)),
+        LATE,
+    )
+
     feature_order = after(order, sent)
-    cross_got = after(cross_got, sent)
-    cross_kept, cross_sent = halved(cross_kept, cross_got)
-    hidden_order = after(order, cross_sent)
-    got = after(swap(sent, step_b), cross_sent)
-    kept, sent = halved(kept, got)
-    cross_got = after(swap(cross_sent, step_a), sent)
-    got = swap(sent, step_a)
-    if planes == 4:
-        cross_kept, cross_sent = halved(cross_kept, cross_got)
-        got = after(got, cross_sent)
-        kept, sent = halved(kept, got)
-        cross_got = after(swap(cross_sent, step_z1), sent)
-        cross_kept, cross_sent = halved(cross_kept, cross_got)
-        got = after(swap(sent, step_z1), cross_sent)
-        kept, sent = halved(kept, got)
-        own_cross = cross_kept.astype(F32) + swap(cross_sent, step_z2).astype(F32)
-        own_self = kept.astype(F32) + swap(sent, step_z2).astype(F32)
-    else:
-        own_cross = scatter_rest(cross_kept, cross_got)
-        own_self = scatter_rest(kept, got)
-    own_ff = [after(branch[4], sent).astype(F32) for branch in branches]
     feature_grad = kernel_call(
         part(feature_kernel, len(w_cross)),
         "feature_grad",
@@ -854,7 +877,22 @@
         (grad_ikey, grad_ivalue, feature_order),
         w_cross,
         cross_start,
-    )
+        cost=LATE,
+    )
+    kept, sent = halved(kept, after(swap(sent, step_c), feature_grad))
+    packed = shaped(width // 2, cross_start + 2 * width, kind=BF)
+    grad_cross = after(grad_cross, sent)
+    cross_kept, cross_sent = kernel_call(
+        cross_weights_kernel,
+        "cross_weights",
+        (packed, packed),
+        (grad_cross, grad_ikey, grad_ivalue, two_low, first_query, looked, features, order),
+        cost=LATE,
+    )
+    got = swap(sent, step_b)
+    cross_sent = after(cross_sent, got)
+    kept, sent = halved(kept, got)
+    hidden_order = after(order, cross_sent, sent)
     hidden_grad = kernel_call(
         part(hidden_kernel, len(w_self)),
         "hidden_grad",
@@ -862,8 +900,26 @@
         (grad_qkv, grad_one, hidden_order),
         w_self,
         3 * width,
-    )
-
+        cost=LATE,
+    )
+    got = swap(sent, step_a)
+    cross_got = after(swap(cross_sent, step_c), hidden_grad, got)
+    cross_kept, cross_sent = halved(cross_kept, cross_got)
+    if planes == 4:
+        kept, sent = halved(kept, got)
+        cross_got = after(swap(cross_sent, step_b), sent, branches[0][4])
+        cross_kept, cross_sent = halved(cross_kept, cross_got)
+        kept, sent = halved(kept, after(swap(sent, step_z1), cross_sent))
+        cross_got = after(swap(cross_sent, step_a), sent)
+        cross_kept, cross_sent = halved(cross_kept, cross_got)
+        own_self = kept.astype(F32) + swap(sent, step_z2).astype(F32)
+        cross_kept, cross_sent = halved(cross_kept, swap(cross_sent, step_z1))
+        own_cross = cross_kept.astype(F32) + swap(cross_sent, step_z2).astype(F32)
+    else:
+        own_self = scatter_rest(kept, got)
+        cross_kept, cross_sent = halved(cross_kept, swap(cross_sent, step_b))
+        own_cross = scatter_rest(cross_kept, swap(cross_sent, step_a))
+    own_ff = [after(branch[4], cross_sent).astype(F32) for branch in branches]
     own_sums = own_self[:, 4 * width : 4 * width + n_vectors].T
     own_up = [own[:, :width].T for own in own_ff]
     own_down = [own[:, width : 2 * width] for own in own_ff]

time: 368 us -> 337 us (0.916)
  starting transfers between devices: 52.2 us -> 40.6 us
  Pallas kernels: 117 us -> 111 us
  waiting for transfers between devices: 129 us -> 123 us
    ppermute x52 -> x53, waiting for transfers between devices: 129 us -> 103 us  [swap(): return lax.ppermute(value, AXES, pairs(count, move))]
    reduce_scatter x2, waiting for transfers between devices: 0.04 us -> 20.2 us  [shards(): own = lax.psum_scatter(grads, 'z', scatter_dimension=0, tiled=True)]
    ppermute x52 -> x53, starting transfers between devices: 52.1 us -> 40.3 us  [swap(): return lax.ppermute(value, AXES, pairs(count, move))]
    pallas_call x15, Pallas kernels: 117 us -> 111 us  [kernel_call(): pl.pallas_call(lambda *refs: body(refs), name=name, out_shape=outs, in_sp...]
    unnamed x89 -> x76, local copies, waits for them, and re-layouts: 18.7 us -> 15.1 us
  transfers between devices with their start and end apart: 55 -> 56, of which waited for: 28 -> 29; matrix products, arithmetic and copies ran while one was open for 10% -> 10% of each run, Pallas kernels for 20% -> 28%
where the time goes in v1:
time: 337 us; the launch traced here: 333 us
  waiting for transfers between devices  123 us (36%)
  Pallas kernels  111 us (33%)
  starting transfers between devices  40.6 us (12%)
  other arithmetic  27 us (8%)
  local copies, waits for them, and re-layouts  17.1 us (5%)
  between operations  14.8 us (4%)
    pallas_call x15, Pallas kernels, kernel_call(): pl.pallas_call(lambda *refs: body(refs), name=name, out_shape=outs, in_sp...  111 us
    ppermute x53, waiting for transfers between devices, swap(): return lax.ppermute(value, AXES, pairs(count, move))  103 us
    ppermute x53, starting transfers between devices, swap(): return lax.ppermute(value, AXES, pairs(count, move))  40.3 us
    reduce_scatter x2, waiting for transfers between devices, shards(): own = lax.psum_scatter(grads, 'z', scatter_dimension=0, tiled=True)  20.2 us
    convert_element_type x16, other arithmetic, add_low(): return (left.astype(F32) + right.astype(F32)).astype(BF)  17.2 us
    unnamed x76, local copies, waits for them, and re-layouts  15.1 us
  transfers between devices with their start and end apart: 56, of which 29 were waited for; matrix products, arithmetic and copies ran while one was open for 10% of the time, Pallas kernels for 28%

profile of v1, /device:TPU:0, one launch (start us, length us, event | category | flops | bytes accessed | tf_op | source)
XLA Modules:
  0.0 333.4 jit_solution(4268586014701733599)
XLA Ops:
  7.3 2.2 pack.1
  9.4 5.1 %collective-permute-start.2 = (bf16[24,3200]{1,0:T(8,128)(2,1)}, bf16[24,3200]{1,0:T(8,128)(2,1)S(1)}, u32[]{:S(2)}, u32[]{:S(2)}) collective-permute-start(bf16[24,3200]{1,0:T(8,128)(2,1)} %get-tuple-element.85), channel_id=1, source_target_pairs={{0,24},{1,25},{2,26},{3,27},{4,28},{5,29},{6,30},{7,31},{8,16},{9,... | collective-permute-start | bytes 460808 | tf_op jit(solution)/shard_map/ppermute | solution.py:48
  16.1 11.6 %collective-permute-done = bf16[24,3200]{1,0:T(8,128)(2,1)S(1)} collective-permute-done((bf16[24,3200]{1,0:T(8,128)(2,1)}, bf16[24,3200]{1,0:T(8,128)(2,1)S(1)}, u32[]{:S(2)}, u32[]{:S(2)}) %collective-permute-start) | collective-permute-done | bytes 153632 | tf_op jit(solution)/shard_map/ppermute | solution.py:48
  27.8 1.6 collective-permute-start.4
  29.4 1.5 collective-permute-start.3
  31.2 10.3 %collective-permute-done.10 = bf16[24,4352]{1,0:T(8,128)(2,1)S(1)} collective-permute-done((bf16[24,4352]{1,0:T(8,128)(2,1)S(1)}, bf16[24,4352]{1,0:T(8,128)(2,1)S(1)}, u32[]{:S(2)}, u32[]{:S(2)}) %collective-permute-start.10) | collective-permute-done | bytes 208928 | tf_op jit(solution)/shard_map/ppermute | solution.py:48
  42.8 1.5 collective-permute-start.5
  44.3 8.9 %collective-permute-done.11 = bf16[48,4352]{1,0:T(8,128)(2,1)S(1)} collective-permute-done((bf16[48,4352]{1,0:T(8,128)(2,1)S(1)}, bf16[48,4352]{1,0:T(8,128)(2,1)S(1)}, u32[]{:S(2)}, u32[]{:S(2)}) %collective-permute-start.11) | collective-permute-done | bytes 417824 | tf_op jit(solution)/shard_map/ppermute | solution.py:48
  56.6 16.5 %collective-permute-done.12.refs_4_.refs_6_.refs_10_ = bf16[96,4352]{1,0:T(8,128)(2,1)} collective-permute-done((bf16[96,4352]{1,0:T(8,128)(2,1)S(1)}, bf16[96,4352]{1,0:T(8,128)(2,1)}, u32[]{:S(2)}, u32[]{:S(2)}) %collective-permute-start.12) | collective-permute-done | bytes 835616 | tf_op jit(solution)/shard_map/ppermute | solution.py:48
  75.4 9.1 %self_forward.1 = (bf16[128,2304]{1,0:T(8,128)(2,1)}, bf16[128,768]{1,0:T(8,128)(2,1)}, f32[128,768]{1,0:T(8,128)}, f32[64,768]{1,0:T(8,128)}, f32[64,768]{1,0:T...) custom-call(s32[2]{0:T(128)} %refs_0_.6, bf16[128,768]{1,0:T(8,128)(2,1)} %bitcast.46, ...), custom_call_target="tpu_custom_call" | custom-call | flops 7200000000 | bytes 24000000 | tf_op jit(solution)/shard_map/self_forward/pallas_call | solution.py:666
  88.6 10.2 %image_rows.1 = (bf16[2,257,768]{2,1,0:T(8,128)(2,1)}, bf16[2,257,768]{2,1,0:T(8,128)(2,1)}) custom-call(bf16[2,257,1408]{2,1,0:T(8,128)(2,1)} %copy.41.refs_0_.refs_6_, bf16[768,768]{1,0:T(8,128)(2,1)} %fusion.refs_2_.refs_1_.refs_3_.refs_7_.refs_9_, f32[16,768]{1,0:T(8,128)} %get-tuple-element.87.refs_2_.refs_4_.refs_8_.refs_10_, ...), custom_call_target="tpu_custom_call" | custom-call | flops 7200000000 | bytes 24000000 | tf_op jit(solution)/shard_map/image_rows/pallas_call | solution.py:666
  98.9 1.5 collective-permute-start.26
  100.4 8.0 %cross_forward.1 = (bf16[64,768]{1,0:T(8,128)(2,1)}, bf16[64,768]{1,0:T(8,128)(2,1)}, f32[64,768]{1,0:T(8,128)}, f32[64,768]{1,0:T(8,128)}, bf16[64,768]{1,0:T(8,128)(2,1)}) custom-call(f32[64,768]{1,0:T(8,128)} %get-tuple-element.86.refs_0_.refs_4_, bf16[2,257,768]{2,1,0:T(8,128)(2,1)} %get-tuple-element.92.refs_1_.refs_5_, ...), custom_call_target="tpu_custom_call" | custom-call | flops 7200000000 | bytes 24000000 | tf_op jit(solution)/shard_map/cross_forward/pallas_call | solution.py:666
  108.9 4.5 %collective-permute-done.19 = bf16[64,768]{1,0:T(8,128)(2,1)S(1)} collective-permute-done((bf16[64,768]{1,0:T(8,128)(2,1)}, bf16[64,768]{1,0:T(8,128)(2,1)S(1)}, u32[]{:S(2)}, u32[]{:S(2)}) %collective-permute-start.19) | collective-permute-done | bytes 98336 | tf_op jit(solution)/shard_map/ppermute | solution.py:48
  115.7 4.8 %branch_up_1.1 = (f32[512,384]{1,0:T(8,128)}, bf16[512,384]{1,0:T(8,128)(2,1)}, f32[256,768]{1,0:T(8,128)}, bf16[256,768]{1,0:T(8,128)(2,1)}) custom-call(bf16[256,768]{1,0:T(8,128)(2,1)} %copy-done.20, bf16[256,768]{1,0:T(8,128)(2,1)} %copy-done.23, bf16[384,3328]{1,0:T(8,128)(2,1)} %all-gather.2.cloned.1.call-done.refs_2_.refs_6_), custom_call_target="tpu_custom_call" | custom-call | flops 7200000000 | bytes 24000000 | tf_op jit(solution)/shard_map/branch_up_1/pallas_call | solution.py:666
  123.8 1.5 collective-permute-start.29
  126.1 4.8 %branch_up_0.1 = (f32[512,384]{1,0:T(8,128)}, bf16[512,384]{1,0:T(8,128)(2,1)}, f32[256,768]{1,0:T(8,128)}, bf16[256,768]{1,0:T(8,128)(2,1)}) custom-call(bf16[256,768]{1,0:T(8,128)(2,1)} %copy-done.5, bf16[256,768]{1,0:T(8,128)(2,1)} %copy-done.24, bf16[384,3328]{1,0:T(8,128)(2,1)} %all-gather.2.cloned.1.call-done.refs_2_.refs_6_), custom_call_target="tpu_custom_call" | custom-call | flops 7200000000 | bytes 24000000 | tf_op jit(solution)/shard_map/branch_up_0/pallas_call | solution.py:666
  134.8 1.5 collective-permute-done.30.refs_1_
  136.9 2.1 branch_end_1.1
  141.8 2.1 collective-permute-done.37
  146.1 2.2 branch_end_0.1
  149.6 3.5 %collective-permute-done.31 = bf16[64,768]{1,0:T(8,128)(2,1)S(1)} collective-permute-done((bf16[64,768]{1,0:T(8,128)(2,1)}, bf16[64,768]{1,0:T(8,128)(2,1)S(1)}, u32[]{:S(2)}, u32[]{:S(2)}) %collective-permute-start.31) | collective-permute-done | bytes 98336 | tf_op jit(solution)/shard_map/ppermute | solution.py:48
  154.2 1.5 collective-permute-start.32
  155.7 4.2 %collective-permute-done.32 = bf16[128,768]{1,0:T(8,128)(2,1)S(1)} collective-permute-done((bf16[128,768]{1,0:T(8,128)(2,1)S(1)}, bf16[128,768]{1,0:T(8,128)(2,1)S(1)}, u32[]{:S(2)}, u32[]{:S(2)}) %collective-permute-start.32) | collective-permute-done | bytes 196640 | tf_op jit(solution)/shard_map/ppermute | solution.py:48
  161.7 5.9 %branch_down_1.1 = (f32[256,768]{1,0:T(8,128)}, bf16[256,768]{1,0:T(8,128)(2,1)}, bf16[384,1664]{1,0:T(8,128)(2,1)}) custom-call(bf16[256,768]{1,0:T(8,128)(2,1)} %copy-done.7, bf16[256,768]{1,0:T(8,128)(2,1)} %copy-done.26, bf16[256,768]{1,0:T(8,128)(2,1)} %copy-done.20, bf16[256,768]{1,0:T(8,128)(2,1)} %copy-done.23, ...), custom_call_target="tpu_custom_call" | custom-call | flops 7200000000 | bytes 24000000 | tf_op jit(solution)/shard_map/branch_down_1/pallas_call | solution.py:666
  169.2 6.2 %branch_down_0.1 = (f32[256,768]{1,0:T(8,128)}, bf16[256,768]{1,0:T(8,128)(2,1)}, bf16[384,1664]{1,0:T(8,128)(2,1)}) custom-call(bf16[256,768]{1,0:T(8,128)(2,1)} %copy-done.6, bf16[256,768]{1,0:T(8,128)(2,1)} %copy-done.25, bf16[256,768]{1,0:T(8,128)(2,1)} %copy-done.5, bf16[256,768]{1,0:T(8,128)(2,1)} %copy-done.24, ...), custom_call_target="tpu_custom_call" | custom-call | flops 7200000000 | bytes 24000000 | tf_op jit(solution)/shard_map/branch_down_0/pallas_call | solution.py:666
  175.6 1.4 collective-permute-start.41
  178.9 2.4 collective-permute-done.41
  186.6 2.1 collective-permute-done.36.refs_1_
  189.4 10.9 %cross_backward.1 = (bf16[64,768]{1,0:T(8,128)(2,1)}, bf16[2,257,768]{2,1,0:T(8,128)(2,1)}, bf16[2,257,768]{2,1,0:T(8,128)(2,1)}, bf16[64,768]{1,0:T(8,128)(2,1)}, f32[64,768]{1,0:T(8,128)}, /*index=5*/f32[8,768]{1,0:T(8,128)}) custom-call(bf16[64,768]{1,0:T(8,128)(2,1)} %get-tuple-element.217.refs_0_, bf16[64,768]{1,0:T(8,128)(2,1)} %copy-done.29, ...), custom_call_target="tpu_custom_call" | custom-call | flops 3600000000 | bytes 12000000 | tf_op jit(solution)/shard_map/cross_backward/pallas_call | solution.py:666
  200.4 14.5 %self_backward.1 = (bf16[128,2304]{1,0:T(8,128)(2,1)}, f32[128,768]{1,0:T(8,128)}, bf16[384,3200]{1,0:T(8,128)(2,1)}, bf16[384,3200]{1,0:T(8,128)(2,1)}) custom-call(s32[2]{0:T(128)} %refs_0_.6, f32[64,768]{1,0:T(8,128)} %get-tuple-element.123.refs_1_, bf16[64,768]{1,0:T(8,128)(2,1)} %get-tuple-element.214.refs_2_, bf16[64,768]{1,0:T(8,128)(2,1)} %copy-done.27, ...), custom_call_target="tpu_custom_call" | custom-call | flops 3600000000 | bytes 12000000 | tf_op jit(solution)/shard_map/self_backward/pallas_call | solution.py:666
  215.0 9.9 %feature_grad.1 = f32[2,257,1408]{2,1,0:T(8,128)} custom-call(bf16[2,257,768]{2,1,0:T(8,128)(2,1)} %get-tuple-element.136.refs_0_.refs_1_, bf16[2,257,768]{2,1,0:T(8,128)(2,1)} %get-tuple-element.137.refs_1_.refs_2_, bf16[768,768]{1,0:T(8,128)(2,1)} %fusion.refs_2_.refs_1_.refs_3_.refs_7_.refs_9_, bf16[96,4352]{1,0:T(8,128)(2,1)} %copy-done.16, ...), custom_call_target="tpu_custom_call" | custom-call | flops 3600000000 | bytes 12000000 | tf_op jit(solution)/shard_map/feature_grad/pallas_call | solution.py:666
  226.4 3.0 add_convert_fusion.2
  230.8 13.2 %cross_weights.1 = (bf16[384,4352]{1,0:T(8,128)(2,1)}, bf16[384,4352]{1,0:T(8,128)(2,1)}) custom-call(bf16[64,768]{1,0:T(8,128)(2,1)} %get-tuple-element.140.refs_0_, bf16[2,257,768]{2,1,0:T(8,128)(2,1)} %get-tuple-element.136.refs_0_.refs_1_, bf16[2,257,768]{2,1,0:T(8,128)(2,1)} %get-tuple-element.137.refs_1_.refs_2_, ...), custom_call_target="tpu_custom_call" | custom-call | flops 3600000000 | bytes 12000000 | tf_op jit(solution)/shard_map/cross_weights/pallas_call | solution.py:666
  244.0 2.2 collective-permute-done.44
  246.2 1.6 add_convert_fusion.6
  249.2 6.7 %hidden_grad.1 = f32[128,768]{1,0:T(8,128)} custom-call(bf16[128,2304]{1,0:T(8,128)(2,1)} %get-tuple-element.131.refs_0_, f32[128,768]{1,0:T(8,128)} %get-tuple-element.132.refs_1_, bf16[768,768]{1,0:T(8,128)(2,1)} %fusion.refs_2_.refs_1_.refs_3_.refs_7_.refs_9_, bf16[96,3200]{1,0:T(8,128)(2,1)} %copy-done.17, bf16[96,3200]{1,0:T(8,128)(2,1)} %copy-done.22, ...), custom_call_target="tpu_custom_call" | custom-call | flops 3600000000 | bytes 12000000 | tf_op jit(solution)/shard_map/hidden_grad/pallas_call | solution.py:666
  255.8 2.3 collective-permute-done.45
  258.1 4.9 %add_convert_fusion = (bf16[192,4352]{1,0:T(8,128)(2,1)}, bf16[192,4352]{1,0:T(8,128)(2,1)S(1)}) fusion(bf16[384,4352]{1,0:T(8,128)(2,1)} %collective-permute-done.47, bf16[384,4352]{1,0:T(8,128)(2,1)} %get-tuple-element.146), kind=kLoop, calls=%fused_computation | loop fusion | flops 6684672 | bytes 10027008 | tf_op jit(solution)/shard_map/convert_element_type | solution.py:92
  264.8 20.2 %reduce-scatter.5.cloned.1.call-done = bf16[96,1664]{1,0:T(8,128)(2,1)} async-done(((bf16[384,1664]{1,0:T(8,128)(2,1)}), bf16[96,1664]{1,0:T(8,128)(2,1)}) %reduce-scatter.5.cloned.1.call-update) | async-done | bytes 319504 | tf_op jit(solution)/shard_map/reduce_scatter | solution.py:819
  285.0 2.0 add_convert_fusion.4
  288.9 3.1 copy.43
  291.9 1.5 collective-permute-start.50
  293.4 2.1 collective-permute-done.49
  295.6 8.8 %collective-permute-done.50 = bf16[96,4352]{1,0:T(8,128)(2,1)S(1)} collective-permute-done((bf16[96,4352]{1,0:T(8,128)(2,1)S(1)}, bf16[96,4352]{1,0:T(8,128)(2,1)S(1)}, u32[]{:S(2)}, u32[]{:S(2)}) %collective-permute-start.50) | collective-permute-done | bytes 835616 | tf_op jit(solution)/shard_map/ppermute | solution.py:48
  310.1 4.8 %collective-permute-done.51 = bf16[48,4352]{1,0:T(8,128)(2,1)S(1)} collective-permute-done((bf16[48,4352]{1,0:T(8,128)(2,1)S(1)}, bf16[48,4352]{1,0:T(8,128)(2,1)S(1)}, u32[]{:S(2)}, u32[]{:S(2)}) %collective-permute-start.51) | collective-permute-done | bytes 417824 | tf_op jit(solution)/shard_map/ppermute | solution.py:48
  315.0 1.6 collective-permute-start.52
  319.3 5.8 %collective-permute-done.52 = bf16[24,4352]{1,0:T(8,128)(2,1)S(1)} collective-permute-done((bf16[24,4352]{1,0:T(8,128)(2,1)S(1)}, bf16[24,4352]{1,0:T(8,128)(2,1)S(1)}, u32[]{:S(2)}, u32[]{:S(2)}) %collective-permute-start.52) | collective-permute-done | bytes 208928 | tf_op jit(solution)/shard_map/ppermute | solution.py:48
  (211 shorter events, 60.5 us)
Async XLA Ops:
  7.2 107.8 %all-gather.2.cloned.1.call-start = ((), (), s32[]{:S(2)}) async-start(), calls=%async_computation.2 | async-start | bytes 3194880 | tf_op jit(solution)/shard_map/all_gather | solution.py:725
  9.4 18.3 %collective-permute-start.2 = (bf16[24,3200]{1,0:T(8,128)(2,1)}, bf16[24,3200]{1,0:T(8,128)(2,1)S(1)}, u32[]{:S(2)}, u32[]{:S(2)}) collective-permute-start(bf16[24,3200]{1,0:T(8,128)(2,1)} %get-tuple-element.85), channel_id=1, source_target_pairs={{0,24},{1,25},{2,26},{3,27},{4,28},{5,29},{6,30},{7,31},{8,16},{9,... | collective-permute-start | bytes 460808 | tf_op jit(solution)/shard_map/ppermute | solution.py:48
  14.5 13.2 %collective-permute-start.1 = (bf16[24,3200]{1,0:T(8,128)(2,1)}, bf16[24,3200]{1,0:T(8,128)(2,1)S(1)}, u32[]{:S(2)}, u32[]{:S(2)}) collective-permute-start(bf16[24,3200]{1,0:T(8,128)(2,1)} %get-tuple-element.85), channel_id=1, source_target_pairs={{0,8},{1,9},{2,10},{3,11},{4,12},{5,13},{6,14},{7,15},{8,0},{9,1},... | collective-permute-start | bytes 460808 | tf_op jit(solution)/shard_map/ppermute | solution.py:48
  14.5 13.2 %collective-permute-start = (bf16[24,3200]{1,0:T(8,128)(2,1)}, bf16[24,3200]{1,0:T(8,128)(2,1)S(1)}, u32[]{:S(2)}, u32[]{:S(2)}) collective-permute-start(bf16[24,3200]{1,0:T(8,128)(2,1)} %get-tuple-element.85), channel_id=1, source_target_pairs={{0,16},{1,17},{2,18},{3,19},{4,20},{5,21},{6,22},{7,23},{8,24},{9,... | collective-permute-start | bytes 460808 | tf_op jit(solution)/shard_map/ppermute | solution.py:48
  27.8 25.5 %collective-permute-start.4 = (bf16[96,3200]{1,0:T(8,128)(2,1)S(1)}, bf16[96,3200]{1,0:T(8,128)(2,1)S(1)}, u32[]{:S(2)}, u32[]{:S(2)}) collective-permute-start(bf16[96,3200]{1,0:T(8,128)(2,1)S(1)} %constant_dynamic-update-slice_fusion.refs_3_.refs_14_), channel_id=1, source_target_pairs={{0,1},{1,0},{2,6},{3,7},{4,5},{5,4},{6,2},{7,3},{8,9},{9,8},{10,14... | collective-permute-start | bytes 1843208 | tf_op jit(solution)/shard_map/ppermute | solution.py:48
  29.4 13.4 %collective-permute-start.3 = (bf16[96,3200]{1,0:T(8,128)(2,1)S(1)}, bf16[96,3200]{1,0:T(8,128)(2,1)S(1)}, u32[]{:S(2)}, u32[]{:S(2)}) collective-permute-start(bf16[96,3200]{1,0:T(8,128)(2,1)S(1)} %constant_dynamic-update-slice_fusion.refs_3_.refs_14_), channel_id=1, source_target_pairs={{0,4},{1,5},{2,3},{3,2},{4,0},{5,1},{6,7},{7,6},{8,12},{9,13},{10,... | collective-permute-start | bytes 1843208 | tf_op jit(solution)/shard_map/ppermute | solution.py:48
  30.9 10.7 %collective-permute-start.10 = (bf16[24,4352]{1,0:T(8,128)(2,1)S(1)}, bf16[24,4352]{1,0:T(8,128)(2,1)S(1)}, u32[]{:S(2)}, u32[]{:S(2)}) collective-permute-start(bf16[24,4352]{1,0:T(8,128)(2,1)S(1)} %pad_maximum_fusion.8), channel_id=1, source_target_pairs={{0,16},{1,17},{2,18},{3,19},{4,20},{5,21},{6,22},{7,23},{8,24},{9,... | collective-permute-start | bytes 626696 | tf_op jit(solution)/shard_map/ppermute | solution.py:48
  41.6 11.6 %collective-permute-start.11 = (bf16[48,4352]{1,0:T(8,128)(2,1)S(1)}, bf16[48,4352]{1,0:T(8,128)(2,1)S(1)}, u32[]{:S(2)}, u32[]{:S(2)}) collective-permute-start(bf16[48,4352]{1,0:T(8,128)(2,1)S(1)} %pad_maximum_fusion.2), channel_id=1, source_target_pairs={{0,8},{1,9},{2,10},{3,11},{4,12},{5,13},{6,14},{7,15},{8,0},{9,1},... | collective-permute-start | bytes 1253384 | tf_op jit(solution)/shard_map/ppermute | solution.py:48
  42.8 11.6 %collective-permute-start.5 = (bf16[96,3200]{1,0:T(8,128)(2,1)S(1)}, bf16[96,3200]{1,0:T(8,128)(2,1)}, u32[]{:S(2)}, u32[]{:S(2)}) collective-permute-start(bf16[96,3200]{1,0:T(8,128)(2,1)S(1)} %collective-permute-done.3.refs_4_.refs_15_), channel_id=1, source_target_pairs={{0,1},{1,0},{2,6},{3,7},{4,5},{5,4},{6,2},{7,3},{8,9},{9,8},{10,14... | collective-permute-start | bytes 1843208 | tf_op jit(solution)/shard_map/ppermute | solution.py:48
  53.3 19.8 %collective-permute-start.12 = (bf16[96,4352]{1,0:T(8,128)(2,1)S(1)}, bf16[96,4352]{1,0:T(8,128)(2,1)}, u32[]{:S(2)}, u32[]{:S(2)}) collective-permute-start(bf16[96,4352]{1,0:T(8,128)(2,1)S(1)} %constant_dynamic-update-slice_fusion.4.refs_3_.refs_5_.refs_9_), channel_id=1, source_target_pairs={{0,4},{1,5},{2,3},{3,2},{4,0},{5,1},{6,7},{7,6},{8,12},{9,13},{10,... | collective-permute-start | bytes 2506760 | tf_op jit(solution)/shard_map/ppermute | solution.py:48
  53.9 21.0 %collective-permute-start.8 = (bf16[96,3200]{1,0:T(8,128)(2,1)S(1)}, bf16[96,3200]{1,0:T(8,128)(2,1)}, u32[]{:S(2)}, u32[]{:S(2)}) collective-permute-start(bf16[96,3200]{1,0:T(8,128)(2,1)S(1)} %collective-permute-done.4.refs_5_.refs_16_), channel_id=1, source_target_pairs={{0,2},{1,3},{2,0},{3,1},{4,6},{5,7},{6,4},{7,5},{8,10},{9,11},{10,... | collective-permute-start | bytes 1843208 | tf_op jit(solution)/shard_map/ppermute | solution.py:48
  54.4 20.5 %collective-permute-start.7 = (bf16[96,3200]{1,0:T(8,128)(2,1)S(1)}, bf16[96,3200]{1,0:T(8,128)(2,1)}, u32[]{:S(2)}, u32[]{:S(2)}) collective-permute-start(bf16[96,3200]{1,0:T(8,128)(2,1)S(1)} %collective-permute-done.3.refs_4_.refs_15_), channel_id=1, source_target_pairs={{0,2},{1,3},{2,0},{3,1},{4,6},{5,7},{6,4},{7,5},{8,10},{9,11},{10,... | collective-permute-start | bytes 1843208 | tf_op jit(solution)/shard_map/ppermute | solution.py:48
  54.4 21.0 %collective-permute-start.9 = (bf16[96,3200]{1,0:T(8,128)(2,1)}, bf16[96,3200]{1,0:T(8,128)(2,1)}, u32[]{:S(2)}, u32[]{:S(2)}) collective-permute-start(bf16[96,3200]{1,0:T(8,128)(2,1)} %collective-permute-done.5.refs_6_.refs_17_), channel_id=1, source_target_pairs={{0,2},{1,3},{2,0},{3,1},{4,6},{5,7},{6,4},{7,5},{8,10},{9,11},{10,... | collective-permute-start | bytes 1843208 | tf_op jit(solution)/shard_map/ppermute | solution.py:48
  55.0 145.4 %reduce-scatter.3.cloned.1.call-start = ((), (), s32[]{:S(2)}) async-start(), calls=%async_computation.3 | async-start | bytes 1597440 | tf_op jit(solution)/shard_map/reduce_scatter | solution.py:819
  56.1 28.5 %collective-permute-start.13 = (bf16[96,4352]{1,0:T(8,128)(2,1)S(1)}, bf16[96,4352]{1,0:T(8,128)(2,1)}, u32[]{:S(2)}, u32[]{:S(2)}) collective-permute-start(bf16[96,4352]{1,0:T(8,128)(2,1)S(1)} %constant_dynamic-update-slice_fusion.4.refs_3_.refs_5_.refs_9_), channel_id=1, source_target_pairs={{0,1},{1,0},{2,6},{3,7},{4,5},{5,4},{6,2},{7,3},{8,9},{9,8},{10,14... | collective-permute-start | bytes 2506760 | tf_op jit(solution)/shard_map/ppermute | solution.py:48
  73.1 12.8 %collective-permute-start.14 = (bf16[96,4352]{1,0:T(8,128)(2,1)}, bf16[96,4352]{1,0:T(8,128)(2,1)}, u32[]{:S(2)}, u32[]{:S(2)}) collective-permute-start(bf16[96,4352]{1,0:T(8,128)(2,1)} %collective-permute-done.12.refs_4_.refs_6_.refs_10_), channel_id=1, source_target_pairs={{0,1},{1,0},{2,6},{3,7},{4,5},{5,4},{6,2},{7,3},{8,9},{9,8},{10,14... | collective-permute-start | bytes 2506760 | tf_op jit(solution)/shard_map/ppermute | solution.py:48
  74.9 12.4 %collective-permute-start.15 = (bf16[96,4352]{1,0:T(8,128)(2,1)S(1)}, bf16[96,4352]{1,0:T(8,128)(2,1)}, u32[]{:S(2)}, u32[]{:S(2)}) collective-permute-start(bf16[96,4352]{1,0:T(8,128)(2,1)S(1)} %constant_dynamic-update-slice_fusion.4.refs_3_.refs_5_.refs_9_), channel_id=1, source_target_pairs={{0,2},{1,3},{2,0},{3,1},{4,6},{5,7},{6,4},{7,5},{8,10},{9,11},{10,... | collective-permute-start | bytes 2506760 | tf_op jit(solution)/shard_map/ppermute | solution.py:48
  74.9 12.4 %collective-permute-start.16 = (bf16[96,4352]{1,0:T(8,128)(2,1)}, bf16[96,4352]{1,0:T(8,128)(2,1)}, u32[]{:S(2)}, u32[]{:S(2)}) collective-permute-start(bf16[96,4352]{1,0:T(8,128)(2,1)} %collective-permute-done.12.refs_4_.refs_6_.refs_10_), channel_id=1, source_target_pairs={{0,2},{1,3},{2,0},{3,1},{4,6},{5,7},{6,4},{7,5},{8,10},{9,11},{10,... | collective-permute-start | bytes 2506760 | tf_op jit(solution)/shard_map/ppermute | solution.py:48
  87.3 11.6 %collective-permute-start.25 = (bf16[64,768]{1,0:T(8,128)(2,1)S(1)}, bf16[64,768]{1,0:T(8,128)(2,1)S(1)}, u32[]{:S(2)}, u32[]{:S(2)}) collective-permute-start(bf16[64,768]{1,0:T(8,128)(2,1)S(1)} %copy-done.10), channel_id=1, source_target_pairs={{0,4},{1,5},{2,3},{3,2},{4,0},{5,1},{6,7},{7,6},{8,12},{9,13},{10,... | collective-permute-start | bytes 294920 | tf_op jit(solution)/shard_map/ppermute | solution.py:48
  98.9 9.6 %collective-permute-start.26 = (bf16[128,768]{1,0:T(8,128)(2,1)S(1)}, bf16[128,768]{1,0:T(8,128)(2,1)S(1)}, u32[]{:S(2)}, u32[]{:S(2)}) collective-permute-start(bf16[128,768]{1,0:T(8,128)(2,1)S(1)} %pad_maximum_fusion.10), channel_id=1, source_target_pairs={{0,1},{1,0},{2,6},{3,7},{4,5},{5,4},{6,2},{7,3},{8,9},{9,8},{10,14... | collective-permute-start | bytes 589832 | tf_op jit(solution)/shard_map/ppermute | solution.py:48
  108.5 6.5 %collective-permute-start.27 = (bf16[256,768]{1,0:T(8,128)(2,1)S(1)}, bf16[256,768]{1,0:T(8,128)(2,1)S(1)}, u32[]{:S(2)}, u32[]{:S(2)}) collective-permute-start(bf16[256,768]{1,0:T(8,128)(2,1)S(1)} %constant_dynamic-update-slice_fusion.7.refs_0_.refs_2_), channel_id=1, source_target_pairs={{0,2},{1,3},{2,0},{3,1},{4,6},{5,7},{6,4},{7,5},{8,10},{9,11},{10,... | collective-permute-start | bytes 1179656 | tf_op jit(solution)/shard_map/ppermute | solution.py:48
  108.5 4.9 %collective-permute-start.19 = (bf16[64,768]{1,0:T(8,128)(2,1)}, bf16[64,768]{1,0:T(8,128)(2,1)S(1)}, u32[]{:S(2)}, u32[]{:S(2)}) collective-permute-start(bf16[64,768]{1,0:T(8,128)(2,1)} %get-tuple-element.94), channel_id=1, source_target_pairs={{0,4},{1,5},{2,3},{3,2},{4,0},{5,1},{6,7},{7,6},{8,12},{9,13},{10,... | collective-permute-start | bytes 294920 | tf_op jit(solution)/shard_map/ppermute | solution.py:48
  114.4 6.3 %collective-permute-start.20 = (bf16[128,768]{1,0:T(8,128)(2,1)S(1)}, bf16[128,768]{1,0:T(8,128)(2,1)S(1)}, u32[]{:S(2)}, u32[]{:S(2)}) collective-permute-start(bf16[128,768]{1,0:T(8,128)(2,1)S(1)} %pad_maximum_fusion.9), channel_id=1, source_target_pairs={{0,1},{1,0},{2,6},{3,7},{4,5},{5,4},{6,2},{7,3},{8,9},{9,8},{10,14... | collective-permute-start | bytes 589832 | tf_op jit(solution)/shard_map/ppermute | solution.py:48
  123.8 7.2 %collective-permute-start.29 = (bf16[128,768]{1,0:T(8,128)(2,1)S(1)}, bf16[128,768]{1,0:T(8,128)(2,1)S(1)}, u32[]{:S(2)}, u32[]{:S(2)}) collective-permute-start(bf16[128,768]{1,0:T(8,128)(2,1)S(1)} %get-tuple-element.205), channel_id=1, source_target_pairs={{0,1},{1,0},{2,6},{3,7},{4,5},{5,4},{6,2},{7,3},{8,9},{9,8},{10,14... | collective-permute-start | bytes 589832 | tf_op jit(solution)/shard_map/ppermute | solution.py:48
  131.7 4.6 %collective-permute-start.30 = (bf16[64,768]{1,0:T(8,128)(2,1)S(1)}, bf16[64,768]{1,0:T(8,128)(2,1)S(1)}, u32[]{:S(2)}, u32[]{:S(2)}) collective-permute-start(bf16[64,768]{1,0:T(8,128)(2,1)S(1)} %get-tuple-element.220), channel_id=1, source_target_pairs={{0,4},{1,5},{2,3},{3,2},{4,0},{5,1},{6,7},{7,6},{8,12},{9,13},{10,... | collective-permute-start | bytes 294920 | tf_op jit(solution)/shard_map/ppermute | solution.py:48
  134.1 5.7 %collective-permute-start.23 = (bf16[128,768]{1,0:T(8,128)(2,1)S(1)}, bf16[128,768]{1,0:T(8,128)(2,1)S(1)}, u32[]{:S(2)}, u32[]{:S(2)}) collective-permute-start(bf16[128,768]{1,0:T(8,128)(2,1)S(1)} %get-tuple-element.203), channel_id=1, source_target_pairs={{0,1},{1,0},{2,6},{3,7},{4,5},{5,4},{6,2},{7,3},{8,9},{9,8},{10,14... | collective-permute-start | bytes 589832 | tf_op jit(solution)/shard_map/ppermute | solution.py:48
  139.1 4.8 %collective-permute-start.37 = (bf16[64,768]{1,0:T(8,128)(2,1)}, bf16[64,768]{1,0:T(8,128)(2,1)S(1)}, u32[]{:S(2)}, u32[]{:S(2)}) collective-permute-start(bf16[64,768]{1,0:T(8,128)(2,1)} %get-tuple-element.112), channel_id=1, source_target_pairs={{0,4},{1,5},{2,3},{3,2},{4,0},{5,1},{6,7},{7,6},{8,12},{9,13},{10,... | collective-permute-start | bytes 294920 | tf_op jit(solution)/shard_map/ppermute | solution.py:48
  140.5 4.9 %collective-permute-start.24 = (bf16[64,768]{1,0:T(8,128)(2,1)S(1)}, bf16[64,768]{1,0:T(8,128)(2,1)S(1)}, u32[]{:S(2)}, u32[]{:S(2)}) collective-permute-start(bf16[64,768]{1,0:T(8,128)(2,1)S(1)} %get-tuple-element.218), channel_id=1, source_target_pairs={{0,4},{1,5},{2,3},{3,2},{4,0},{5,1},{6,7},{7,6},{8,12},{9,13},{10,... | collective-permute-start | bytes 294920 | tf_op jit(solution)/shard_map/ppermute | solution.py:48
  144.8 8.3 %collective-permute-start.38 = (bf16[128,768]{1,0:T(8,128)(2,1)S(1)}, bf16[128,768]{1,0:T(8,128)(2,1)S(1)}, u32[]{:S(2)}, u32[]{:S(2)}) collective-permute-start(bf16[128,768]{1,0:T(8,128)(2,1)S(1)} %pad_maximum_fusion.13), channel_id=1, source_target_pairs={{0,1},{1,0},{2,6},{3,7},{4,5},{5,4},{6,2},{7,3},{8,9},{9,8},{10,14... | collective-permute-start | bytes 589832 | tf_op jit(solution)/shard_map/ppermute | solution.py:48
  148.3 4.8 %collective-permute-start.31 = (bf16[64,768]{1,0:T(8,128)(2,1)}, bf16[64,768]{1,0:T(8,128)(2,1)S(1)}, u32[]{:S(2)}, u32[]{:S(2)}) collective-permute-start(bf16[64,768]{1,0:T(8,128)(2,1)} %get-tuple-element.107), channel_id=1, source_target_pairs={{0,4},{1,5},{2,3},{3,2},{4,0},{5,1},{6,7},{7,6},{8,12},{9,13},{10,... | collective-permute-start | bytes 294920 | tf_op jit(solution)/shard_map/ppermute | solution.py:48
  153.1 7.8 %collective-permute-start.39 = (bf16[256,768]{1,0:T(8,128)(2,1)S(1)}, bf16[256,768]{1,0:T(8,128)(2,1)S(1)}, u32[]{:S(2)}, u32[]{:S(2)}) collective-permute-start(bf16[256,768]{1,0:T(8,128)(2,1)S(1)} %pad_maximum_fusion.5.refs_0_), channel_id=1, source_target_pairs={{0,2},{1,3},{2,0},{3,1},{4,6},{5,7},{6,4},{7,5},{8,10},{9,11},{10,... | collective-permute-start | bytes 1179656 | tf_op jit(solution)/shard_map/ppermute | solution.py:48
  154.2 5.7 %collective-permute-start.32 = (bf16[128,768]{1,0:T(8,128)(2,1)S(1)}, bf16[128,768]{1,0:T(8,128)(2,1)S(1)}, u32[]{:S(2)}, u32[]{:S(2)}) collective-permute-start(bf16[128,768]{1,0:T(8,128)(2,1)S(1)} %pad_maximum_fusion.12), channel_id=1, source_target_pairs={{0,1},{1,0},{2,6},{3,7},{4,5},{5,4},{6,2},{7,3},{8,9},{9,8},{10,14... | collective-permute-start | bytes 589832 | tf_op jit(solution)/shard_map/ppermute | solution.py:48
  160.8 7.6 %collective-permute-start.33 = (bf16[256,768]{1,0:T(8,128)(2,1)S(1)}, bf16[256,768]{1,0:T(8,128)(2,1)S(1)}, u32[]{:S(2)}, u32[]{:S(2)}) collective-permute-start(bf16[256,768]{1,0:T(8,128)(2,1)S(1)} %pad_maximum_fusion.4.refs_0_), channel_id=1, source_target_pairs={{0,2},{1,3},{2,0},{3,1},{4,6},{5,7},{6,4},{7,5},{8,10},{9,11},{10,... | collective-permute-start | bytes 1179656 | tf_op jit(solution)/shard_map/ppermute | solution.py:48
  167.7 117.3 %reduce-scatter.5.cloned.1.call-start = ((), (), s32[]{:S(2)}) async-start(), calls=%async_computation.4 | async-start | bytes 1597440 | tf_op jit(solution)/shard_map/reduce_scatter | solution.py:819
  167.9 7.6 %collective-permute-start.40 = (bf16[256,768]{1,0:T(8,128)(2,1)}, bf16[256,768]{1,0:T(8,128)(2,1)S(1)}, u32[]{:S(2)}, u32[]{:S(2)}) collective-permute-start(bf16[256,768]{1,0:T(8,128)(2,1)} %get-tuple-element.116), channel_id=1, source_target_pairs={{0,2},{1,3},{2,0},{3,1},{4,6},{5,7},{6,4},{7,5},{8,10},{9,11},{10,... | collective-permute-start | bytes 1179656 | tf_op jit(solution)/shard_map/ppermute | solution.py:48
  175.6 5.7 %collective-permute-start.41 = (bf16[128,768]{1,0:T(8,128)(2,1)S(1)}, bf16[128,768]{1,0:T(8,128)(2,1)S(1)}, u32[]{:S(2)}, u32[]{:S(2)}) collective-permute-start(bf16[128,768]{1,0:T(8,128)(2,1)S(1)} %get-tuple-element.199), channel_id=1, source_target_pairs={{0,1},{1,0},{2,6},{3,7},{4,5},{5,4},{6,2},{7,3},{8,9},{9,8},{10,14... | collective-permute-start | bytes 589832 | tf_op jit(solution)/shard_map/ppermute | solution.py:48
  177.5 5.9 %collective-permute-start.35 = (bf16[128,768]{1,0:T(8,128)(2,1)S(1)}, bf16[128,768]{1,0:T(8,128)(2,1)S(1)}, u32[]{:S(2)}, u32[]{:S(2)}) collective-permute-start(bf16[128,768]{1,0:T(8,128)(2,1)S(1)} %get-tuple-element.201), channel_id=1, source_target_pairs={{0,1},{1,0},{2,6},{3,7},{4,5},{5,4},{6,2},{7,3},{8,9},{9,8},{10,14... | collective-permute-start | bytes 589832 | tf_op jit(solution)/shard_map/ppermute | solution.py:48
  182.0 4.6 %collective-permute-start.42 = (bf16[64,768]{1,0:T(8,128)(2,1)S(1)}, bf16[64,768]{1,0:T(8,128)(2,1)S(1)}, u32[]{:S(2)}, u32[]{:S(2)}) collective-permute-start(bf16[64,768]{1,0:T(8,128)(2,1)S(1)} %get-tuple-element.215), channel_id=1, source_target_pairs={{0,4},{1,5},{2,3},{3,2},{4,0},{5,1},{6,7},{7,6},{8,12},{9,13},{10,... | collective-permute-start | bytes 294920 | tf_op jit(solution)/shard_map/ppermute | solution.py:48
  214.9 10.0 %collective-permute-start.43 = (bf16[384,3200]{1,0:T(8,128)(2,1)}, bf16[384,3200]{1,0:T(8,128)(2,1)S(1)}, u32[]{:S(2)}, u32[]{:S(2)}) collective-permute-start(bf16[384,3200]{1,0:T(8,128)(2,1)} %get-tuple-element.135), channel_id=1, source_target_pairs={{0,2},{1,3},{2,0},{3,1},{4,6},{5,7},{6,4},{7,5},{8,10},{9,11},{10,... | collective-permute-start | bytes 7372808 | tf_op jit(solution)/shard_map/ppermute | solution.py:48
  229.3 16.9 %collective-permute-start.44 = (bf16[192,3200]{1,0:T(8,128)(2,1)S(1)}, bf16[192,3200]{1,0:T(8,128)(2,1)}, u32[]{:S(2)}, u32[]{:S(2)}) collective-permute-start(bf16[192,3200]{1,0:T(8,128)(2,1)S(1)} %get-tuple-element.189), channel_id=1, source_target_pairs={{0,1},{1,0},{2,6},{3,7},{4,5},{5,4},{6,2},{7,3},{8,9},{9,8},{10,14... | collective-permute-start | bytes 3686408 | tf_op jit(solution)/shard_map/ppermute | solution.py:48
  246.2 11.9 %collective-permute-start.47 = (bf16[384,4352]{1,0:T(8,128)(2,1)}, bf16[384,4352]{1,0:T(8,128)(2,1)}, u32[]{:S(2)}, u32[]{:S(2)}) collective-permute-start(bf16[384,4352]{1,0:T(8,128)(2,1)} %get-tuple-element.144), channel_id=1, source_target_pairs={{0,2},{1,3},{2,0},{3,1},{4,6},{5,7},{6,4},{7,5},{8,10},{9,11},{10,... | collective-permute-start | bytes 10027016 | tf_op jit(solution)/shard_map/ppermute | solution.py:48
  247.9 10.2 %collective-permute-start.45 = (bf16[96,3200]{1,0:T(8,128)(2,1)S(1)}, bf16[96,3200]{1,0:T(8,128)(2,1)S(1)}, u32[]{:S(2)}, u32[]{:S(2)}) collective-permute-start(bf16[96,3200]{1,0:T(8,128)(2,1)S(1)} %get-tuple-element.193), channel_id=1, source_target_pairs={{0,4},{1,5},{2,3},{3,2},{4,0},{5,1},{6,7},{7,6},{8,12},{9,13},{10,... | collective-permute-start | bytes 1843208 | tf_op jit(solution)/shard_map/ppermute | solution.py:48
  263.0 22.0 %collective-permute-start.48 = (bf16[192,4352]{1,0:T(8,128)(2,1)}, bf16[192,4352]{1,0:T(8,128)(2,1)}, u32[]{:S(2)}, u32[]{:S(2)}) collective-permute-start(bf16[192,4352]{1,0:T(8,128)(2,1)} %get-tuple-element.186), channel_id=1, source_target_pairs={{0,1},{1,0},{2,6},{3,7},{4,5},{5,4},{6,2},{7,3},{8,9},{9,8},{10,14... | collective-permute-start | bytes 5013512 | tf_op jit(solution)/shard_map/ppermute | solution.py:48
  264.5 22.5 %collective-permute-start.46 = (bf16[48,3200]{1,0:T(8,128)(2,1)S(1)}, bf16[48,3200]{1,0:T(8,128)(2,1)S(1)}, u32[]{:S(2)}, u32[]{:S(2)}) collective-permute-start(bf16[48,3200]{1,0:T(8,128)(2,1)S(1)} %get-tuple-element.196), channel_id=1, source_target_pairs={{0,8},{1,9},{2,10},{3,11},{4,12},{5,13},{6,14},{7,15},{8,0},{9,1},... | collective-permute-start | bytes 921608 | tf_op jit(solution)/shard_map/ppermute | solution.py:48
  287.0 8.4 %collective-permute-start.49 = (bf16[24,3200]{1,0:T(8,128)(2,1)S(1)}, bf16[24,3200]{1,0:T(8,128)(2,1)S(1)}, u32[]{:S(2)}, u32[]{:S(2)}) collective-permute-start(bf16[24,3200]{1,0:T(8,128)(2,1)S(1)} %add_convert_fusion.22), channel_id=1, source_target_pairs={{0,16},{1,17},{2,18},{3,19},{4,20},{5,21},{6,22},{7,23},{8,24},{9,... | collective-permute-start | bytes 460808 | tf_op jit(solution)/shard_map/ppermute | solution.py:48
  291.9 12.5 %collective-permute-start.50 = (bf16[96,4352]{1,0:T(8,128)(2,1)S(1)}, bf16[96,4352]{1,0:T(8,128)(2,1)S(1)}, u32[]{:S(2)}, u32[]{:S(2)}) collective-permute-start(bf16[96,4352]{1,0:T(8,128)(2,1)S(1)} %get-tuple-element.191), channel_id=1, source_target_pairs={{0,4},{1,5},{2,3},{3,2},{4,0},{5,1},{6,7},{7,6},{8,12},{9,13},{10,... | collective-permute-start | bytes 2506760 | tf_op jit(solution)/shard_map/ppermute | solution.py:48
  304.7 10.3 %collective-permute-start.51 = (bf16[48,4352]{1,0:T(8,128)(2,1)S(1)}, bf16[48,4352]{1,0:T(8,128)(2,1)S(1)}, u32[]{:S(2)}, u32[]{:S(2)}) collective-permute-start(bf16[48,4352]{1,0:T(8,128)(2,1)S(1)} %get-tuple-element.195), channel_id=1, source_target_pairs={{0,8},{1,9},{2,10},{3,11},{4,12},{5,13},{6,14},{7,15},{8,0},{9,1},... | collective-permute-start | bytes 1253384 | tf_op jit(solution)/shard_map/ppermute | solution.py:48
  315.0 10.1 %collective-permute-start.52 = (bf16[24,4352]{1,0:T(8,128)(2,1)S(1)}, bf16[24,4352]{1,0:T(8,128)(2,1)S(1)}, u32[]{:S(2)}, u32[]{:S(2)}) collective-permute-start(bf16[24,4352]{1,0:T(8,128)(2,1)S(1)} %add_convert_fusion.12), channel_id=1, source_target_pairs={{0,16},{1,17},{2,18},{3,19},{4,20},{5,21},{6,22},{7,23},{8,24},{9,... | collective-permute-start | bytes 626696 | tf_op jit(solution)/shard_map/ppermute | solution.py:48
  (39 other events, 294.7 us)
Sparse Core Ops, SparseCore 0:
  55.1 52.5 all-gather.1
  167.8 29.0 reduce-scatter.2
  249.3 35.6 reduce-scatter.4

commit v2 on v1

--- a/solution.py
+++ b/solution.py
@@ -4,6 +4,7 @@
 import jax.numpy as jnp
 from jax import lax
 from jax.experimental import pallas as pl
+from jax.experimental.layout import Layout, with_layout_constraint
 from jax.experimental.pallas import tpu as pltpu
 from jax.sharding import Mesh, PartitionSpec as P
 
@@ -671,7 +672,7 @@
         out_specs=jax.tree.map(lambda _: vmem, outs),
         scratch_shapes=scratch,
         cost_estimate=pl.CostEstimate(
-            flops=cost * 900_000_000, bytes_accessed=cost * 3_000_000, transcendentals=0
+            flops=int(cost * 900_000_000), bytes_accessed=int(cost * 3_000_000), transcendentals=0
         ),
     )(*arrays)
 
@@ -842,7 +843,29 @@
         extra=(pltpu.VMEM((query_rows, width), BF),),
         cost=LATE,
     )
-    grad_first = after(grad_first, branches[1][4])
+    packed = shaped(width // 2, cross_start + 2 * width, kind=BF)
+    grad_cross = after(grad_cross, branches[1][4])
+    cross_kept, cross_sent = kernel_call(
+        cross_weights_kernel,
+        "cross_weights",
+        (packed, packed),
+        (grad_cross, grad_ikey, grad_ivalue, two_low, first_query, looked, features, order),
+        cost=LATE,
+    )
+    feature_order = after(order, cross_sent)
+    feature_grad = kernel_call(
+        part(feature_kernel, len(w_cross)),
+        "feature_grad",
+        shaped(items, image_rows, image_width),
+        (grad_ikey, grad_ivalue, feature_order),
+        w_cross,
+        cross_start,
+        cost=LATE,
+    )
+    cross_got = after(swap(cross_sent, step_c), feature_grad)
+    cross_kept, cross_sent = halved(cross_kept, cross_got)
+
+    grad_first = after(grad_first, cross_sent)
     packed = shaped(width // 2, 4 * width + 128, kind=BF)
     grad_qkv, grad_one, kept, sent = kernel_call(
         part(self_backward_kernel, items, len(w_self)),
@@ -868,31 +891,12 @@
         (pltpu.VMEM((128, width), F32), pltpu.VMEM((rows, width), BF)),
         LATE,
     )
-
-    feature_order = after(order, sent)
-    feature_grad = kernel_call(
-        part(feature_kernel, len(w_cross)),
-        "feature_grad",
-        shaped(items, image_rows, image_width),
-        (grad_ikey, grad_ivalue, feature_order),
-        w_cross,
-        cross_start,
-        cost=LATE,
-    )
-    kept, sent = halved(kept, after(swap(sent, step_c), feature_grad))
-    packed = shaped(width // 2, cross_start + 2 * width, kind=BF)
-    grad_cross = after(grad_cross, sent)
-    cross_kept, cross_sent = kernel_call(
-        cross_weights_kernel,
-        "cross_weights",
-        (packed, packed),
-        (grad_cross, grad_ikey, grad_ivalue, two_low, first_query, looked, features, order),
-        cost=LATE,
-    )
-    got = swap(sent, step_b)
-    cross_sent = after(cross_sent, got)
-    kept, sent = halved(kept, got)
-    hidden_order = after(order, cross_sent, sent)
+    feature_grad = with_layout_constraint(feature_grad, Layout((1, 0, 2)))
+    cross_got = after(swap(cross_sent, step_b), feature_grad)
+    sent = after(sent, cross_got, branches[0][4])
+    cross_kept, cross_sent = halved(cross_kept, cross_got)
+    kept, sent = halved(kept, swap(sent, step_c))
+    hidden_order = after(order, sent)
     hidden_grad = kernel_call(
         part(hidden_kernel, len(w_self)),
         "hidden_grad",
@@ -902,24 +906,23 @@
         3 * width,
         cost=LATE,
     )
-    got = swap(sent, step_a)
-    cross_got = after(swap(cross_sent, step_c), hidden_grad, got)
-    cross_kept, cross_sent = halved(cross_kept, cross_got)
+    cross_got = after(swap(cross_sent, step_a), hidden_grad)
+    got = swap(sent, step_b)
     if planes == 4:
+        cross_kept, cross_sent = halved(cross_kept, cross_got)
+        kept, sent = halved(kept, after(got, cross_sent))
+        cross_got = after(swap(cross_sent, step_z1), sent)
+        cross_kept, cross_sent = halved(cross_kept, cross_got)
+        kept, sent = halved(kept, after(swap(sent, step_a), cross_sent))
+        cross_got = after(swap(cross_sent, step_z2), sent)
+        own_cross = cross_kept.astype(F32) + cross_got.astype(F32)
+        kept, sent = halved(kept, swap(sent, step_z1))
+        own_self = kept.astype(F32) + swap(sent, step_z2).astype(F32)
+    else:
+        own_cross = scatter_rest(cross_kept, cross_got)
         kept, sent = halved(kept, got)
-        cross_got = after(swap(cross_sent, step_b), sent, branches[0][4])
-        cross_kept, cross_sent = halved(cross_kept, cross_got)
-        kept, sent = halved(kept, after(swap(sent, step_z1), cross_sent))
-        cross_got = after(swap(cross_sent, step_a), sent)
-        cross_kept, cross_sent = halved(cross_kept, cross_got)
-        own_self = kept.astype(F32) + swap(sent, step_z2).astype(F32)
-        cross_kept, cross_sent = halved(cross_kept, swap(cross_sent, step_z1))
-        own_cross = cross_kept.astype(F32) + swap(cross_sent, step_z2).astype(F32)
-    else:
-        own_self = scatter_rest(kept, got)
-        cross_kept, cross_sent = halved(cross_kept, swap(cross_sent, step_b))
-        own_cross = scatter_rest(cross_kept, swap(cross_sent, step_a))
-    own_ff = [after(branch[4], cross_sent).astype(F32) for branch in branches]
+        own_self = scatter_rest(kept, swap(sent, step_a))
+    own_ff = [after(branch[4], sent).astype(F32) for branch in branches]
     own_sums = own_self[:, 4 * width : 4 * width + n_vectors].T
     own_up = [own[:, :width].T for own in own_ff]
     own_down = [own[:, width : 2 * width] for own in own_ff]

time: 337 us -> 326 us (0.967)
  starting transfers between devices: 40.6 us -> 35.2 us
  waiting for transfers between devices: 123 us -> 118 us
    reduce_scatter x2, waiting for transfers between devices: 20.2 us -> 0.02 us  [shards(): own = lax.psum_scatter(grads, 'z', scatter_dimension=0, tiled=True)]
    ppermute x53, waiting for transfers between devices: 103 us -> 118 us  [swap(): return lax.ppermute(value, AXES, pairs(count, move))]
    ppermute x53, starting transfers between devices: 40.3 us -> 34.9 us  [swap(): return lax.ppermute(value, AXES, pairs(count, move))]
    unnamed x76 -> x79, local copies, waits for them, and re-layouts: 15.1 us -> 12.2 us
  transfers between devices with their start and end apart: 56 -> 56, of which waited for: 29 -> 29; matrix products, arithmetic and copies ran while one was open for 10% -> 10% of each run, Pallas kernels for 28% -> 30%
where the time goes in v2:
time: 326 us; the launch traced here: 322 us
  waiting for transfers between devices  118 us (36%)
  Pallas kernels  111 us (34%)
  starting transfers between devices  35.2 us (11%)
  other arithmetic  25.7 us (8%)
  local copies, waits for them, and re-layouts  17.3 us (5%)
  between operations  15 us (5%)
    ppermute x53, waiting for transfers between devices, swap(): return lax.ppermute(value, AXES, pairs(count, move))  118 us
    pallas_call x15, Pallas kernels, kernel_call(): pl.pallas_call(lambda *refs: body(refs), name=name, out_shape=outs, in_sp...  111 us
    ppermute x53, starting transfers between devices, swap(): return lax.ppermute(value, AXES, pairs(count, move))  34.9 us
    convert_element_type x16, other arithmetic, add_low(): return (left.astype(F32) + right.astype(F32)).astype(BF)  15.8 us
    unnamed x79, local copies, waits for them, and re-layouts  12.2 us
  transfers between devices with their start and end apart: 56, of which 29 were waited for; matrix products, arithmetic and copies ran while one was open for 10% of the time, Pallas kernels for 30%

profile of v2, /device:TPU:0, one launch (start us, length us, event | category | flops | bytes accessed | tf_op | source)
XLA Modules:
  0.0 321.6 jit_solution(1904545480106274289)
XLA Ops:
  7.3 2.2 pack.1
  9.4 5.1 %collective-permute-start.2 = (bf16[24,3200]{1,0:T(8,128)(2,1)}, bf16[24,3200]{1,0:T(8,128)(2,1)S(1)}, u32[]{:S(2)}, u32[]{:S(2)}) collective-permute-start(bf16[24,3200]{1,0:T(8,128)(2,1)} %get-tuple-element.87), channel_id=1, source_target_pairs={{0,24},{1,25},{2,26},{3,27},{4,28},{5,29},{6,30},{7,31},{8,16},{9,... | collective-permute-start | bytes 460808 | tf_op jit(solution)/shard_map/ppermute | solution.py:49
  16.1 11.6 %collective-permute-done = bf16[24,3200]{1,0:T(8,128)(2,1)S(1)} collective-permute-done((bf16[24,3200]{1,0:T(8,128)(2,1)}, bf16[24,3200]{1,0:T(8,128)(2,1)S(1)}, u32[]{:S(2)}, u32[]{:S(2)}) %collective-permute-start) | collective-permute-done | bytes 153632 | tf_op jit(solution)/shard_map/ppermute | solution.py:49
  27.8 1.6 collective-permute-start.4
  29.4 1.5 collective-permute-start.3
  31.2 10.3 %collective-permute-done.10 = bf16[24,4352]{1,0:T(8,128)(2,1)S(1)} collective-permute-done((bf16[24,4352]{1,0:T(8,128)(2,1)S(1)}, bf16[24,4352]{1,0:T(8,128)(2,1)S(1)}, u32[]{:S(2)}, u32[]{:S(2)}) %collective-permute-start.10) | collective-permute-done | bytes 208928 | tf_op jit(solution)/shard_map/ppermute | solution.py:49
  42.8 1.5 collective-permute-start.5
  44.3 8.9 %collective-permute-done.11 = bf16[48,4352]{1,0:T(8,128)(2,1)S(1)} collective-permute-done((bf16[48,4352]{1,0:T(8,128)(2,1)S(1)}, bf16[48,4352]{1,0:T(8,128)(2,1)S(1)}, u32[]{:S(2)}, u32[]{:S(2)}) %collective-permute-start.11) | collective-permute-done | bytes 417824 | tf_op jit(solution)/shard_map/ppermute | solution.py:49
  56.6 16.5 %collective-permute-done.12.refs_4_.refs_6_.refs_10_ = bf16[96,4352]{1,0:T(8,128)(2,1)} collective-permute-done((bf16[96,4352]{1,0:T(8,128)(2,1)S(1)}, bf16[96,4352]{1,0:T(8,128)(2,1)}, u32[]{:S(2)}, u32[]{:S(2)}) %collective-permute-start.12) | collective-permute-done | bytes 835616 | tf_op jit(solution)/shard_map/ppermute | solution.py:49
  73.6 1.3 fusion.refs_2_.refs_1_.refs_3_.refs_7_.refs_9_
  75.5 8.8 %self_forward.1 = (bf16[128,2304]{1,0:T(8,128)(2,1)}, bf16[128,768]{1,0:T(8,128)(2,1)}, f32[128,768]{1,0:T(8,128)}, f32[64,768]{1,0:T(8,128)}, f32[64,768]{1,0:T...) custom-call(s32[2]{0:T(128)} %refs_0_.6, bf16[128,768]{1,0:T(8,128)(2,1)} %bitcast.46, ...), custom_call_target="tpu_custom_call" | custom-call | flops 7200000000 | bytes 24000000 | tf_op jit(solution)/shard_map/self_forward/pallas_call | solution.py:667
  84.4 1.5 collective-permute-done.14.refs_6_.refs_8_.refs_12_
  87.2 1.4 collective-permute-done.18.refs_10_.refs_12_.refs_16_
  88.6 10.2 %image_rows.1 = (bf16[2,257,768]{2,1,0:T(8,128)(2,1)}, bf16[2,257,768]{2,1,0:T(8,128)(2,1)}) custom-call(bf16[2,257,1408]{2,1,0:T(8,128)(2,1)} %copy.41.refs_0_.refs_6_, bf16[768,768]{1,0:T(8,128)(2,1)} %fusion.refs_2_.refs_1_.refs_3_.refs_7_.refs_9_, f32[16,768]{1,0:T(8,128)} %get-tuple-element.89.refs_2_.refs_4_.refs_8_.refs_10_, ...), custom_call_target="tpu_custom_call" | custom-call | flops 7200000000 | bytes 24000000 | tf_op jit(solution)/shard_map/image_rows/pallas_call | solution.py:667
  100.1 8.0 %cross_forward.1 = (bf16[64,768]{1,0:T(8,128)(2,1)}, bf16[64,768]{1,0:T(8,128)(2,1)}, f32[64,768]{1,0:T(8,128)}, f32[64,768]{1,0:T(8,128)}, bf16[64,768]{1,0:T(8,128)(2,1)}) custom-call(f32[64,768]{1,0:T(8,128)} %get-tuple-element.88.refs_0_.refs_4_, bf16[2,257,768]{2,1,0:T(8,128)(2,1)} %get-tuple-element.94.refs_1_.refs_5_, ...), custom_call_target="tpu_custom_call" | custom-call | flops 7200000000 | bytes 24000000 | tf_op jit(solution)/shard_map/cross_forward/pallas_call | solution.py:667
  108.9 4.2 %collective-permute-done.19 = bf16[64,768]{1,0:T(8,128)(2,1)S(1)} collective-permute-done((bf16[64,768]{1,0:T(8,128)(2,1)}, bf16[64,768]{1,0:T(8,128)(2,1)S(1)}, u32[]{:S(2)}, u32[]{:S(2)}) %collective-permute-start.19) | collective-permute-done | bytes 98336 | tf_op jit(solution)/shard_map/ppermute | solution.py:49
  115.7 5.0 %branch_up_1.1 = (f32[512,384]{1,0:T(8,128)}, bf16[512,384]{1,0:T(8,128)(2,1)}, f32[256,768]{1,0:T(8,128)}, bf16[256,768]{1,0:T(8,128)(2,1)}) custom-call(bf16[256,768]{1,0:T(8,128)(2,1)} %copy-done.21, bf16[256,768]{1,0:T(8,128)(2,1)} %copy-done.25, bf16[384,3328]{1,0:T(8,128)(2,1)} %all-gather.2.cloned.1.call-done.refs_2_.refs_6_), custom_call_target="tpu_custom_call" | custom-call | flops 7200000000 | bytes 24000000 | tf_op jit(solution)/shard_map/branch_up_1/pallas_call | solution.py:667
  125.8 4.9 %branch_up_0.1 = (f32[512,384]{1,0:T(8,128)}, bf16[512,384]{1,0:T(8,128)(2,1)}, f32[256,768]{1,0:T(8,128)}, bf16[256,768]{1,0:T(8,128)(2,1)}) custom-call(bf16[256,768]{1,0:T(8,128)(2,1)} %copy-done.6, bf16[256,768]{1,0:T(8,128)(2,1)} %copy-done.26, bf16[384,3328]{1,0:T(8,128)(2,1)} %all-gather.2.cloned.1.call-done.refs_2_.refs_6_), custom_call_target="tpu_custom_call" | custom-call | flops 7200000000 | bytes 24000000 | tf_op jit(solution)/shard_map/branch_up_0/pallas_call | solution.py:667
  136.7 2.2 branch_end_1.1
  141.6 2.1 collective-permute-done.37
  146.2 2.2 branch_end_0.1
  149.4 3.8 %collective-permute-done.31 = bf16[64,768]{1,0:T(8,128)(2,1)S(1)} collective-permute-done((bf16[64,768]{1,0:T(8,128)(2,1)}, bf16[64,768]{1,0:T(8,128)(2,1)S(1)}, u32[]{:S(2)}, u32[]{:S(2)}) %collective-permute-start.31) | collective-permute-done | bytes 98336 | tf_op jit(solution)/shard_map/ppermute | solution.py:49
  155.5 4.5 %collective-permute-done.32 = bf16[128,768]{1,0:T(8,128)(2,1)S(1)} collective-permute-done((bf16[128,768]{1,0:T(8,128)(2,1)S(1)}, bf16[128,768]{1,0:T(8,128)(2,1)S(1)}, u32[]{:S(2)}, u32[]{:S(2)}) %collective-permute-start.32) | collective-permute-done | bytes 196640 | tf_op jit(solution)/shard_map/ppermute | solution.py:49
  161.8 6.0 %branch_down_1.1 = (f32[256,768]{1,0:T(8,128)}, bf16[256,768]{1,0:T(8,128)(2,1)}, bf16[384,1664]{1,0:T(8,128)(2,1)}) custom-call(bf16[256,768]{1,0:T(8,128)(2,1)} %copy-done.8, bf16[256,768]{1,0:T(8,128)(2,1)} %copy-done.28, bf16[256,768]{1,0:T(8,128)(2,1)} %copy-done.21, bf16[256,768]{1,0:T(8,128)(2,1)} %copy-done.25, ...), custom_call_target="tpu_custom_call" | custom-call | flops 7200000000 | bytes 24000000 | tf_op jit(solution)/shard_map/branch_down_1/pallas_call | solution.py:667
  169.4 6.2 %branch_down_0.1 = (f32[256,768]{1,0:T(8,128)}, bf16[256,768]{1,0:T(8,128)(2,1)}, bf16[384,1664]{1,0:T(8,128)(2,1)}) custom-call(bf16[256,768]{1,0:T(8,128)(2,1)} %copy-done.7, bf16[256,768]{1,0:T(8,128)(2,1)} %copy-done.27, bf16[256,768]{1,0:T(8,128)(2,1)} %copy-done.6, bf16[256,768]{1,0:T(8,128)(2,1)} %copy-done.26, ...), custom_call_target="tpu_custom_call" | custom-call | flops 7200000000 | bytes 24000000 | tf_op jit(solution)/shard_map/branch_down_0/pallas_call | solution.py:667
  178.7 2.8 collective-permute-done.41
  185.2 1.6 collective-permute-done.42.refs_3_
  186.8 2.1 collective-permute-done.36.refs_1_
  189.6 10.9 %cross_backward.1 = (bf16[64,768]{1,0:T(8,128)(2,1)}, bf16[2,257,768]{2,1,0:T(8,128)(2,1)}, bf16[2,257,768]{2,1,0:T(8,128)(2,1)}, bf16[64,768]{1,0:T(8,128)(2,1)}, f32[64,768]{1,0:T(8,128)}, /*index=5*/f32[8,768]{1,0:T(8,128)}) custom-call(bf16[64,768]{1,0:T(8,128)(2,1)} %get-tuple-element.221.refs_0_, bf16[64,768]{1,0:T(8,128)(2,1)} %copy-done.31, ...), custom_call_target="tpu_custom_call" | custom-call | flops 3600000000 | bytes 12000000 | tf_op jit(solution)/shard_map/cross_backward/pallas_call | solution.py:667
  200.5 13.3 %cross_weights.1 = (bf16[384,4352]{1,0:T(8,128)(2,1)}, bf16[384,4352]{1,0:T(8,128)(2,1)}) custom-call(bf16[64,768]{1,0:T(8,128)(2,1)} %get-tuple-element.126.refs_0_, bf16[2,257,768]{2,1,0:T(8,128)(2,1)} %get-tuple-element.127.refs_1_.refs_0_, bf16[2,257,768]{2,1,0:T(8,128)(2,1)} %get-tuple-element.128.refs_2_.refs_1_, ...), custom_call_target="tpu_custom_call" | custom-call | flops 3600000000 | bytes 12000000 | tf_op jit(solution)/shard_map/cross_weights/pallas_call | solution.py:667
  213.8 10.0 %feature_grad.1 = f32[2,257,1408]{2,1,0:T(8,128)} custom-call(bf16[2,257,768]{2,1,0:T(8,128)(2,1)} %get-tuple-element.127.refs_1_.refs_0_, bf16[2,257,768]{2,1,0:T(8,128)(2,1)} %get-tuple-element.128.refs_2_.refs_1_, bf16[768,768]{1,0:T(8,128)(2,1)} %fusion.refs_2_.refs_1_.refs_3_.refs_7_.refs_9_, bf16[96,4352]{1,0:T(8,128)(2,1)} %copy-done.17, ...), custom_call_target="tpu_custom_call" | custom-call | flops 3600000000 | bytes 12000000 | tf_op jit(solution)/shard_map/feature_grad/pallas_call | solution.py:667
  223.8 1.7 copy-done
  225.6 3.9 %add_convert_fusion = (bf16[192,4352]{1,0:T(8,128)(2,1)S(1)}, bf16[192,4352]{1,0:T(8,128)(2,1)S(1)}) fusion(bf16[384,4352]{1,0:T(8,128)(2,1)} %copy-done, bf16[384,4352]{1,0:T(8,128)(2,1)} %get-tuple-element.131), kind=kLoop, calls=%fused_computation | loop fusion | flops 6684672 | bytes 10027008 | tf_op jit(solution)/shard_map/convert_element_type | solution.py:93
  230.6 3.1 copy.43
  233.6 14.6 %self_backward.1 = (bf16[128,2304]{1,0:T(8,128)(2,1)}, f32[128,768]{1,0:T(8,128)}, bf16[384,3200]{1,0:T(8,128)(2,1)}, bf16[384,3200]{1,0:T(8,128)(2,1)}) custom-call(s32[2]{0:T(128)} %refs_0_.6, f32[64,768]{1,0:T(8,128)} %get-tuple-element.135.refs_1_, bf16[64,768]{1,0:T(8,128)(2,1)} %get-tuple-element.218.refs_2_, bf16[64,768]{1,0:T(8,128)(2,1)} %copy-done.29, ...), custom_call_target="tpu_custom_call" | custom-call | flops 3600000000 | bytes 12000000 | tf_op jit(solution)/shard_map/self_backward/pallas_call | solution.py:667
  248.2 2.9 collective-permute-done.44
  251.8 1.9 add_convert_fusion.4
  256.0 1.6 add_convert_fusion.2
  258.6 6.4 %hidden_grad.1 = f32[128,768]{1,0:T(8,128)} custom-call(bf16[128,2304]{1,0:T(8,128)(2,1)} %get-tuple-element.143.refs_0_, f32[128,768]{1,0:T(8,128)} %get-tuple-element.144.refs_1_, bf16[768,768]{1,0:T(8,128)(2,1)} %fusion.refs_2_.refs_1_.refs_3_.refs_7_.refs_9_, bf16[96,3200]{1,0:T(8,128)(2,1)} %copy-done.18, bf16[96,3200]{1,0:T(8,128)(2,1)} %copy-done.23, ...), custom_call_target="tpu_custom_call" | custom-call | flops 3600000000 | bytes 12000000 | tf_op jit(solution)/shard_map/hidden_grad/pallas_call | solution.py:667
  265.1 7.1 %collective-permute-done.47 = bf16[96,4352]{1,0:T(8,128)(2,1)} collective-permute-done((bf16[96,4352]{1,0:T(8,128)(2,1)S(1)}, bf16[96,4352]{1,0:T(8,128)(2,1)}, u32[]{:S(2)}, u32[]{:S(2)}) %collective-permute-start.47) | collective-permute-done | bytes 835616 | tf_op jit(solution)/shard_map/ppermute | solution.py:49
  272.2 1.3 add_convert_fusion.8
  273.7 5.4 %collective-permute-done.46 = bf16[192,3200]{1,0:T(8,128)(2,1)} collective-permute-done((bf16[192,3200]{1,0:T(8,128)(2,1)}, bf16[192,3200]{1,0:T(8,128)(2,1)}, u32[]{:S(2)}, u32[]{:S(2)}) %collective-permute-start.46) | collective-permute-done | bytes 1228832 | tf_op jit(solution)/shard_map/ppermute | solution.py:49
  279.1 1.5 add_convert_fusion.6
  281.6 1.9 collective-permute-done.49
  283.7 7.1 %collective-permute-done.48 = bf16[96,3200]{1,0:T(8,128)(2,1)S(1)} collective-permute-done((bf16[96,3200]{1,0:T(8,128)(2,1)S(1)}, bf16[96,3200]{1,0:T(8,128)(2,1)S(1)}, u32[]{:S(2)}, u32[]{:S(2)}) %collective-permute-start.48) | collective-permute-done | bytes 614432 | tf_op jit(solution)/shard_map/ppermute | solution.py:49
  291.2 3.1 collective-permute-done.52
  295.8 5.0 %collective-permute-done.50 = bf16[48,3200]{1,0:T(8,128)(2,1)S(1)} collective-permute-done((bf16[48,3200]{1,0:T(8,128)(2,1)S(1)}, bf16[48,3200]{1,0:T(8,128)(2,1)S(1)}, u32[]{:S(2)}, u32[]{:S(2)}) %collective-permute-start.50) | collective-permute-done | bytes 307232 | tf_op jit(solution)/shard_map/ppermute | solution.py:49
  303.6 6.1 %collective-permute-done.51 = bf16[24,3200]{1,0:T(8,128)(2,1)S(1)} collective-permute-done((bf16[24,3200]{1,0:T(8,128)(2,1)S(1)}, bf16[24,3200]{1,0:T(8,128)(2,1)S(1)}, u32[]{:S(2)}, u32[]{:S(2)}) %collective-permute-start.51) | collective-permute-done | bytes 153632 | tf_op jit(solution)/shard_map/ppermute | solution.py:49
  (215 shorter events, 59.9 us)
Async XLA Ops:
  7.2 107.8 %all-gather.2.cloned.1.call-start = ((), (), s32[]{:S(2)}) async-start(), calls=%async_computation.2 | async-start | bytes 3194880 | tf_op jit(solution)/shard_map/all_gather | solution.py:726
  9.4 18.3 %collective-permute-start.2 = (bf16[24,3200]{1,0:T(8,128)(2,1)}, bf16[24,3200]{1,0:T(8,128)(2,1)S(1)}, u32[]{:S(2)}, u32[]{:S(2)}) collective-permute-start(bf16[24,3200]{1,0:T(8,128)(2,1)} %get-tuple-element.87), channel_id=1, source_target_pairs={{0,24},{1,25},{2,26},{3,27},{4,28},{5,29},{6,30},{7,31},{8,16},{9,... | collective-permute-start | bytes 460808 | tf_op jit(solution)/shard_map/ppermute | solution.py:49
  14.5 13.2 %collective-permute-start.1 = (bf16[24,3200]{1,0:T(8,128)(2,1)}, bf16[24,3200]{1,0:T(8,128)(2,1)S(1)}, u32[]{:S(2)}, u32[]{:S(2)}) collective-permute-start(bf16[24,3200]{1,0:T(8,128)(2,1)} %get-tuple-element.87), channel_id=1, source_target_pairs={{0,8},{1,9},{2,10},{3,11},{4,12},{5,13},{6,14},{7,15},{8,0},{9,1},... | collective-permute-start | bytes 460808 | tf_op jit(solution)/shard_map/ppermute | solution.py:49
  14.5 13.2 %collective-permute-start = (bf16[24,3200]{1,0:T(8,128)(2,1)}, bf16[24,3200]{1,0:T(8,128)(2,1)S(1)}, u32[]{:S(2)}, u32[]{:S(2)}) collective-permute-start(bf16[24,3200]{1,0:T(8,128)(2,1)} %get-tuple-element.87), channel_id=1, source_target_pairs={{0,16},{1,17},{2,18},{3,19},{4,20},{5,21},{6,22},{7,23},{8,24},{9,... | collective-permute-start | bytes 460808 | tf_op jit(solution)/shard_map/ppermute | solution.py:49
  27.8 25.5 %collective-permute-start.4 = (bf16[96,3200]{1,0:T(8,128)(2,1)S(1)}, bf16[96,3200]{1,0:T(8,128)(2,1)S(1)}, u32[]{:S(2)}, u32[]{:S(2)}) collective-permute-start(bf16[96,3200]{1,0:T(8,128)(2,1)S(1)} %constant_dynamic-update-slice_fusion.refs_3_.refs_14_), channel_id=1, source_target_pairs={{0,1},{1,0},{2,6},{3,7},{4,5},{5,4},{6,2},{7,3},{8,9},{9,8},{10,14... | collective-permute-start | bytes 1843208 | tf_op jit(solution)/shard_map/ppermute | solution.py:49
  29.4 13.4 %collective-permute-start.3 = (bf16[96,3200]{1,0:T(8,128)(2,1)S(1)}, bf16[96,3200]{1,0:T(8,128)(2,1)S(1)}, u32[]{:S(2)}, u32[]{:S(2)}) collective-permute-start(bf16[96,3200]{1,0:T(8,128)(2,1)S(1)} %constant_dynamic-update-slice_fusion.refs_3_.refs_14_), channel_id=1, source_target_pairs={{0,4},{1,5},{2,3},{3,2},{4,0},{5,1},{6,7},{7,6},{8,12},{9,13},{10,... | collective-permute-start | bytes 1843208 | tf_op jit(solution)/shard_map/ppermute | solution.py:49
  30.9 10.7 %collective-permute-start.10 = (bf16[24,4352]{1,0:T(8,128)(2,1)S(1)}, bf16[24,4352]{1,0:T(8,128)(2,1)S(1)}, u32[]{:S(2)}, u32[]{:S(2)}) collective-permute-start(bf16[24,4352]{1,0:T(8,128)(2,1)S(1)} %pad_maximum_fusion.8), channel_id=1, source_target_pairs={{0,16},{1,17},{2,18},{3,19},{4,20},{5,21},{6,22},{7,23},{8,24},{9,... | collective-permute-start | bytes 626696 | tf_op jit(solution)/shard_map/ppermute | solution.py:49
  41.6 11.6 %collective-permute-start.11 = (bf16[48,4352]{1,0:T(8,128)(2,1)S(1)}, bf16[48,4352]{1,0:T(8,128)(2,1)S(1)}, u32[]{:S(2)}, u32[]{:S(2)}) collective-permute-start(bf16[48,4352]{1,0:T(8,128)(2,1)S(1)} %pad_maximum_fusion.2), channel_id=1, source_target_pairs={{0,8},{1,9},{2,10},{3,11},{4,12},{5,13},{6,14},{7,15},{8,0},{9,1},... | collective-permute-start | bytes 1253384 | tf_op jit(solution)/shard_map/ppermute | solution.py:49
  42.8 11.6 %collective-permute-start.5 = (bf16[96,3200]{1,0:T(8,128)(2,1)S(1)}, bf16[96,3200]{1,0:T(8,128)(2,1)S(1)}, u32[]{:S(2)}, u32[]{:S(2)}) collective-permute-start(bf16[96,3200]{1,0:T(8,128)(2,1)S(1)} %collective-permute-done.3.refs_4_.refs_15_), channel_id=1, source_target_pairs={{0,1},{1,0},{2,6},{3,7},{4,5},{5,4},{6,2},{7,3},{8,9},{9,8},{10,14... | collective-permute-start | bytes 1843208 | tf_op jit(solution)/shard_map/ppermute | solution.py:49
  53.3 19.8 %collective-permute-start.12 = (bf16[96,4352]{1,0:T(8,128)(2,1)S(1)}, bf16[96,4352]{1,0:T(8,128)(2,1)}, u32[]{:S(2)}, u32[]{:S(2)}) collective-permute-start(bf16[96,4352]{1,0:T(8,128)(2,1)S(1)} %constant_dynamic-update-slice_fusion.4.refs_3_.refs_5_.refs_9_), channel_id=1, source_target_pairs={{0,4},{1,5},{2,3},{3,2},{4,0},{5,1},{6,7},{7,6},{8,12},{9,13},{10,... | collective-permute-start | bytes 2506760 | tf_op jit(solution)/shard_map/ppermute | solution.py:49
  53.9 21.0 %collective-permute-start.8 = (bf16[96,3200]{1,0:T(8,128)(2,1)S(1)}, bf16[96,3200]{1,0:T(8,128)(2,1)}, u32[]{:S(2)}, u32[]{:S(2)}) collective-permute-start(bf16[96,3200]{1,0:T(8,128)(2,1)S(1)} %collective-permute-done.4.refs_5_.refs_16_), channel_id=1, source_target_pairs={{0,2},{1,3},{2,0},{3,1},{4,6},{5,7},{6,4},{7,5},{8,10},{9,11},{10,... | collective-permute-start | bytes 1843208 | tf_op jit(solution)/shard_map/ppermute | solution.py:49
  54.4 20.5 %collective-permute-start.7 = (bf16[96,3200]{1,0:T(8,128)(2,1)S(1)}, bf16[96,3200]{1,0:T(8,128)(2,1)}, u32[]{:S(2)}, u32[]{:S(2)}) collective-permute-start(bf16[96,3200]{1,0:T(8,128)(2,1)S(1)} %collective-permute-done.3.refs_4_.refs_15_), channel_id=1, source_target_pairs={{0,2},{1,3},{2,0},{3,1},{4,6},{5,7},{6,4},{7,5},{8,10},{9,11},{10,... | collective-permute-start | bytes 1843208 | tf_op jit(solution)/shard_map/ppermute | solution.py:49
  54.4 21.0 %collective-permute-start.9 = (bf16[96,3200]{1,0:T(8,128)(2,1)S(1)}, bf16[96,3200]{1,0:T(8,128)(2,1)}, u32[]{:S(2)}, u32[]{:S(2)}) collective-permute-start(bf16[96,3200]{1,0:T(8,128)(2,1)S(1)} %collective-permute-done.5.refs_6_.refs_17_), channel_id=1, source_target_pairs={{0,2},{1,3},{2,0},{3,1},{4,6},{5,7},{6,4},{7,5},{8,10},{9,11},{10,... | collective-permute-start | bytes 1843208 | tf_op jit(solution)/shard_map/ppermute | solution.py:49
  55.0 145.6 %reduce-scatter.3.cloned.1.call-start = ((), (), s32[]{:S(2)}) async-start(), calls=%async_computation.3 | async-start | bytes 1597440 | tf_op jit(solution)/shard_map/reduce_scatter | solution.py:820
  56.1 28.2 %collective-permute-start.13 = (bf16[96,4352]{1,0:T(8,128)(2,1)S(1)}, bf16[96,4352]{1,0:T(8,128)(2,1)}, u32[]{:S(2)}, u32[]{:S(2)}) collective-permute-start(bf16[96,4352]{1,0:T(8,128)(2,1)S(1)} %constant_dynamic-update-slice_fusion.4.refs_3_.refs_5_.refs_9_), channel_id=1, source_target_pairs={{0,1},{1,0},{2,6},{3,7},{4,5},{5,4},{6,2},{7,3},{8,9},{9,8},{10,14... | collective-permute-start | bytes 2506760 | tf_op jit(solution)/shard_map/ppermute | solution.py:49
  73.1 12.8 %collective-permute-start.14 = (bf16[96,4352]{1,0:T(8,128)(2,1)}, bf16[96,4352]{1,0:T(8,128)(2,1)}, u32[]{:S(2)}, u32[]{:S(2)}) collective-permute-start(bf16[96,4352]{1,0:T(8,128)(2,1)} %collective-permute-done.12.refs_4_.refs_6_.refs_10_), channel_id=1, source_target_pairs={{0,1},{1,0},{2,6},{3,7},{4,5},{5,4},{6,2},{7,3},{8,9},{9,8},{10,14... | collective-permute-start | bytes 2506760 | tf_op jit(solution)/shard_map/ppermute | solution.py:49
  74.9 12.3 %collective-permute-start.15 = (bf16[96,4352]{1,0:T(8,128)(2,1)S(1)}, bf16[96,4352]{1,0:T(8,128)(2,1)}, u32[]{:S(2)}, u32[]{:S(2)}) collective-permute-start(bf16[96,4352]{1,0:T(8,128)(2,1)S(1)} %constant_dynamic-update-slice_fusion.4.refs_3_.refs_5_.refs_9_), channel_id=1, source_target_pairs={{0,2},{1,3},{2,0},{3,1},{4,6},{5,7},{6,4},{7,5},{8,10},{9,11},{10,... | collective-permute-start | bytes 2506760 | tf_op jit(solution)/shard_map/ppermute | solution.py:49
  75.0 12.3 %collective-permute-start.16 = (bf16[96,4352]{1,0:T(8,128)(2,1)}, bf16[96,4352]{1,0:T(8,128)(2,1)}, u32[]{:S(2)}, u32[]{:S(2)}) collective-permute-start(bf16[96,4352]{1,0:T(8,128)(2,1)} %collective-permute-done.12.refs_4_.refs_6_.refs_10_), channel_id=1, source_target_pairs={{0,2},{1,3},{2,0},{3,1},{4,6},{5,7},{6,4},{7,5},{8,10},{9,11},{10,... | collective-permute-start | bytes 2506760 | tf_op jit(solution)/shard_map/ppermute | solution.py:49
  87.2 11.6 %collective-permute-start.25 = (bf16[64,768]{1,0:T(8,128)(2,1)S(1)}, bf16[64,768]{1,0:T(8,128)(2,1)S(1)}, u32[]{:S(2)}, u32[]{:S(2)}) collective-permute-start(bf16[64,768]{1,0:T(8,128)(2,1)S(1)} %copy-done.11), channel_id=1, source_target_pairs={{0,4},{1,5},{2,3},{3,2},{4,0},{5,1},{6,7},{7,6},{8,12},{9,13},{10,... | collective-permute-start | bytes 294920 | tf_op jit(solution)/shard_map/ppermute | solution.py:49
  98.8 9.2 %collective-permute-start.26 = (bf16[128,768]{1,0:T(8,128)(2,1)S(1)}, bf16[128,768]{1,0:T(8,128)(2,1)S(1)}, u32[]{:S(2)}, u32[]{:S(2)}) collective-permute-start(bf16[128,768]{1,0:T(8,128)(2,1)S(1)} %pad_maximum_fusion.10), channel_id=1, source_target_pairs={{0,1},{1,0},{2,6},{3,7},{4,5},{5,4},{6,2},{7,3},{8,9},{9,8},{10,14... | collective-permute-start | bytes 589832 | tf_op jit(solution)/shard_map/ppermute | solution.py:49
  108.1 6.8 %collective-permute-start.27 = (bf16[256,768]{1,0:T(8,128)(2,1)S(1)}, bf16[256,768]{1,0:T(8,128)(2,1)S(1)}, u32[]{:S(2)}, u32[]{:S(2)}) collective-permute-start(bf16[256,768]{1,0:T(8,128)(2,1)S(1)} %constant_dynamic-update-slice_fusion.7.refs_0_.refs_2_), channel_id=1, source_target_pairs={{0,2},{1,3},{2,0},{3,1},{4,6},{5,7},{6,4},{7,5},{8,10},{9,11},{10,... | collective-permute-start | bytes 1179656 | tf_op jit(solution)/shard_map/ppermute | solution.py:49
  108.2 4.9 %collective-permute-start.19 = (bf16[64,768]{1,0:T(8,128)(2,1)}, bf16[64,768]{1,0:T(8,128)(2,1)S(1)}, u32[]{:S(2)}, u32[]{:S(2)}) collective-permute-start(bf16[64,768]{1,0:T(8,128)(2,1)} %get-tuple-element.96), channel_id=1, source_target_pairs={{0,4},{1,5},{2,3},{3,2},{4,0},{5,1},{6,7},{7,6},{8,12},{9,13},{10,... | collective-permute-start | bytes 294920 | tf_op jit(solution)/shard_map/ppermute | solution.py:49
  114.0 6.7 %collective-permute-start.20 = (bf16[128,768]{1,0:T(8,128)(2,1)S(1)}, bf16[128,768]{1,0:T(8,128)(2,1)S(1)}, u32[]{:S(2)}, u32[]{:S(2)}) collective-permute-start(bf16[128,768]{1,0:T(8,128)(2,1)S(1)} %pad_maximum_fusion.9), channel_id=1, source_target_pairs={{0,1},{1,0},{2,6},{3,7},{4,5},{5,4},{6,2},{7,3},{8,9},{9,8},{10,14... | collective-permute-start | bytes 589832 | tf_op jit(solution)/shard_map/ppermute | solution.py:49
  123.9 6.9 %collective-permute-start.29 = (bf16[128,768]{1,0:T(8,128)(2,1)S(1)}, bf16[128,768]{1,0:T(8,128)(2,1)S(1)}, u32[]{:S(2)}, u32[]{:S(2)}) collective-permute-start(bf16[128,768]{1,0:T(8,128)(2,1)S(1)} %get-tuple-element.209), channel_id=1, source_target_pairs={{0,1},{1,0},{2,6},{3,7},{4,5},{5,4},{6,2},{7,3},{8,9},{9,8},{10,14... | collective-permute-start | bytes 589832 | tf_op jit(solution)/shard_map/ppermute | solution.py:49
  131.5 4.6 %collective-permute-start.30 = (bf16[64,768]{1,0:T(8,128)(2,1)S(1)}, bf16[64,768]{1,0:T(8,128)(2,1)S(1)}, u32[]{:S(2)}, u32[]{:S(2)}) collective-permute-start(bf16[64,768]{1,0:T(8,128)(2,1)S(1)} %get-tuple-element.224), channel_id=1, source_target_pairs={{0,4},{1,5},{2,3},{3,2},{4,0},{5,1},{6,7},{7,6},{8,12},{9,13},{10,... | collective-permute-start | bytes 294920 | tf_op jit(solution)/shard_map/ppermute | solution.py:49
  133.9 5.7 %collective-permute-start.23 = (bf16[128,768]{1,0:T(8,128)(2,1)S(1)}, bf16[128,768]{1,0:T(8,128)(2,1)S(1)}, u32[]{:S(2)}, u32[]{:S(2)}) collective-permute-start(bf16[128,768]{1,0:T(8,128)(2,1)S(1)} %get-tuple-element.207), channel_id=1, source_target_pairs={{0,1},{1,0},{2,6},{3,7},{4,5},{5,4},{6,2},{7,3},{8,9},{9,8},{10,14... | collective-permute-start | bytes 589832 | tf_op jit(solution)/shard_map/ppermute | solution.py:49
  138.9 4.8 %collective-permute-start.37 = (bf16[64,768]{1,0:T(8,128)(2,1)}, bf16[64,768]{1,0:T(8,128)(2,1)S(1)}, u32[]{:S(2)}, u32[]{:S(2)}) collective-permute-start(bf16[64,768]{1,0:T(8,128)(2,1)} %get-tuple-element.114), channel_id=1, source_target_pairs={{0,4},{1,5},{2,3},{3,2},{4,0},{5,1},{6,7},{7,6},{8,12},{9,13},{10,... | collective-permute-start | bytes 294920 | tf_op jit(solution)/shard_map/ppermute | solution.py:49
  140.3 5.2 %collective-permute-start.24 = (bf16[64,768]{1,0:T(8,128)(2,1)S(1)}, bf16[64,768]{1,0:T(8,128)(2,1)S(1)}, u32[]{:S(2)}, u32[]{:S(2)}) collective-permute-start(bf16[64,768]{1,0:T(8,128)(2,1)S(1)} %get-tuple-element.222), channel_id=1, source_target_pairs={{0,4},{1,5},{2,3},{3,2},{4,0},{5,1},{6,7},{7,6},{8,12},{9,13},{10,... | collective-permute-start | bytes 294920 | tf_op jit(solution)/shard_map/ppermute | solution.py:49
  144.6 8.6 %collective-permute-start.38 = (bf16[128,768]{1,0:T(8,128)(2,1)S(1)}, bf16[128,768]{1,0:T(8,128)(2,1)S(1)}, u32[]{:S(2)}, u32[]{:S(2)}) collective-permute-start(bf16[128,768]{1,0:T(8,128)(2,1)S(1)} %pad_maximum_fusion.13), channel_id=1, source_target_pairs={{0,1},{1,0},{2,6},{3,7},{4,5},{5,4},{6,2},{7,3},{8,9},{9,8},{10,14... | collective-permute-start | bytes 589832 | tf_op jit(solution)/shard_map/ppermute | solution.py:49
  148.4 4.8 %collective-permute-start.31 = (bf16[64,768]{1,0:T(8,128)(2,1)}, bf16[64,768]{1,0:T(8,128)(2,1)S(1)}, u32[]{:S(2)}, u32[]{:S(2)}) collective-permute-start(bf16[64,768]{1,0:T(8,128)(2,1)} %get-tuple-element.109), channel_id=1, source_target_pairs={{0,4},{1,5},{2,3},{3,2},{4,0},{5,1},{6,7},{7,6},{8,12},{9,13},{10,... | collective-permute-start | bytes 294920 | tf_op jit(solution)/shard_map/ppermute | solution.py:49
  153.2 7.8 %collective-permute-start.39 = (bf16[256,768]{1,0:T(8,128)(2,1)S(1)}, bf16[256,768]{1,0:T(8,128)(2,1)S(1)}, u32[]{:S(2)}, u32[]{:S(2)}) collective-permute-start(bf16[256,768]{1,0:T(8,128)(2,1)S(1)} %pad_maximum_fusion.5.refs_0_), channel_id=1, source_target_pairs={{0,2},{1,3},{2,0},{3,1},{4,6},{5,7},{6,4},{7,5},{8,10},{9,11},{10,... | collective-permute-start | bytes 1179656 | tf_op jit(solution)/shard_map/ppermute | solution.py:49
  154.3 5.7 %collective-permute-start.32 = (bf16[128,768]{1,0:T(8,128)(2,1)S(1)}, bf16[128,768]{1,0:T(8,128)(2,1)S(1)}, u32[]{:S(2)}, u32[]{:S(2)}) collective-permute-start(bf16[128,768]{1,0:T(8,128)(2,1)S(1)} %pad_maximum_fusion.12), channel_id=1, source_target_pairs={{0,1},{1,0},{2,6},{3,7},{4,5},{5,4},{6,2},{7,3},{8,9},{9,8},{10,14... | collective-permute-start | bytes 589832 | tf_op jit(solution)/shard_map/ppermute | solution.py:49
  161.0 7.7 %collective-permute-start.33 = (bf16[256,768]{1,0:T(8,128)(2,1)S(1)}, bf16[256,768]{1,0:T(8,128)(2,1)S(1)}, u32[]{:S(2)}, u32[]{:S(2)}) collective-permute-start(bf16[256,768]{1,0:T(8,128)(2,1)S(1)} %pad_maximum_fusion.4.refs_0_), channel_id=1, source_target_pairs={{0,2},{1,3},{2,0},{3,1},{4,6},{5,7},{6,4},{7,5},{8,10},{9,11},{10,... | collective-permute-start | bytes 1179656 | tf_op jit(solution)/shard_map/ppermute | solution.py:49
  167.9 83.2 %reduce-scatter.5.cloned.1.call-start = ((), (), s32[]{:S(2)}) async-start(), calls=%async_computation.4 | async-start | bytes 1597440 | tf_op jit(solution)/shard_map/reduce_scatter | solution.py:820
  168.1 7.6 %collective-permute-start.40 = (bf16[256,768]{1,0:T(8,128)(2,1)}, bf16[256,768]{1,0:T(8,128)(2,1)S(1)}, u32[]{:S(2)}, u32[]{:S(2)}) collective-permute-start(bf16[256,768]{1,0:T(8,128)(2,1)} %get-tuple-element.118), channel_id=1, source_target_pairs={{0,2},{1,3},{2,0},{3,1},{4,6},{5,7},{6,4},{7,5},{8,10},{9,11},{10,... | collective-permute-start | bytes 1179656 | tf_op jit(solution)/shard_map/ppermute | solution.py:49
  175.8 5.7 %collective-permute-start.41 = (bf16[128,768]{1,0:T(8,128)(2,1)S(1)}, bf16[128,768]{1,0:T(8,128)(2,1)S(1)}, u32[]{:S(2)}, u32[]{:S(2)}) collective-permute-start(bf16[128,768]{1,0:T(8,128)(2,1)S(1)} %get-tuple-element.203), channel_id=1, source_target_pairs={{0,1},{1,0},{2,6},{3,7},{4,5},{5,4},{6,2},{7,3},{8,9},{9,8},{10,14... | collective-permute-start | bytes 589832 | tf_op jit(solution)/shard_map/ppermute | solution.py:49
  177.7 5.9 %collective-permute-start.35 = (bf16[128,768]{1,0:T(8,128)(2,1)S(1)}, bf16[128,768]{1,0:T(8,128)(2,1)S(1)}, u32[]{:S(2)}, u32[]{:S(2)}) collective-permute-start(bf16[128,768]{1,0:T(8,128)(2,1)S(1)} %get-tuple-element.205), channel_id=1, source_target_pairs={{0,1},{1,0},{2,6},{3,7},{4,5},{5,4},{6,2},{7,3},{8,9},{9,8},{10,14... | collective-permute-start | bytes 589832 | tf_op jit(solution)/shard_map/ppermute | solution.py:49
  182.2 4.6 %collective-permute-start.42 = (bf16[64,768]{1,0:T(8,128)(2,1)S(1)}, bf16[64,768]{1,0:T(8,128)(2,1)S(1)}, u32[]{:S(2)}, u32[]{:S(2)}) collective-permute-start(bf16[64,768]{1,0:T(8,128)(2,1)S(1)} %get-tuple-element.219), channel_id=1, source_target_pairs={{0,4},{1,5},{2,3},{3,2},{4,0},{5,1},{6,7},{7,6},{8,12},{9,13},{10,... | collective-permute-start | bytes 294920 | tf_op jit(solution)/shard_map/ppermute | solution.py:49
  213.8 10.0 %collective-permute-start.43 = (bf16[384,4352]{1,0:T(8,128)(2,1)}, bf16[384,4352]{1,0:T(8,128)(2,1)S(1)}, u32[]{:S(2)}, u32[]{:S(2)}) collective-permute-start(bf16[384,4352]{1,0:T(8,128)(2,1)} %get-tuple-element.132), channel_id=1, source_target_pairs={{0,2},{1,3},{2,0},{3,1},{4,6},{5,7},{6,4},{7,5},{8,10},{9,11},{10,... | collective-permute-start | bytes 10027016 | tf_op jit(solution)/shard_map/ppermute | solution.py:49
  229.4 21.6 %collective-permute-start.44 = (bf16[192,4352]{1,0:T(8,128)(2,1)S(1)}, bf16[192,4352]{1,0:T(8,128)(2,1)}, u32[]{:S(2)}, u32[]{:S(2)}) collective-permute-start(bf16[192,4352]{1,0:T(8,128)(2,1)S(1)} %get-tuple-element.191), channel_id=1, source_target_pairs={{0,1},{1,0},{2,6},{3,7},{4,5},{5,4},{6,2},{7,3},{8,9},{9,8},{10,14... | collective-permute-start | bytes 5013512 | tf_op jit(solution)/shard_map/ppermute | solution.py:49
  251.1 4.9 %collective-permute-start.45 = (bf16[384,3200]{1,0:T(8,128)(2,1)}, bf16[384,3200]{1,0:T(8,128)(2,1)S(1)}, u32[]{:S(2)}, u32[]{:S(2)}) collective-permute-start(bf16[384,3200]{1,0:T(8,128)(2,1)} %get-tuple-element.149), channel_id=1, source_target_pairs={{0,2},{1,3},{2,0},{3,1},{4,6},{5,7},{6,4},{7,5},{8,10},{9,11},{10,... | collective-permute-start | bytes 7372808 | tf_op jit(solution)/shard_map/ppermute | solution.py:49
  253.7 18.5 %collective-permute-start.47 = (bf16[96,4352]{1,0:T(8,128)(2,1)S(1)}, bf16[96,4352]{1,0:T(8,128)(2,1)}, u32[]{:S(2)}, u32[]{:S(2)}) collective-permute-start(bf16[96,4352]{1,0:T(8,128)(2,1)S(1)} %get-tuple-element.194), channel_id=1, source_target_pairs={{0,4},{1,5},{2,3},{3,2},{4,0},{5,1},{6,7},{7,6},{8,12},{9,13},{10,... | collective-permute-start | bytes 2506760 | tf_op jit(solution)/shard_map/ppermute | solution.py:49
  257.6 21.5 %collective-permute-start.46 = (bf16[192,3200]{1,0:T(8,128)(2,1)}, bf16[192,3200]{1,0:T(8,128)(2,1)}, u32[]{:S(2)}, u32[]{:S(2)}) collective-permute-start(bf16[192,3200]{1,0:T(8,128)(2,1)} %get-tuple-element.193), channel_id=1, source_target_pairs={{0,1},{1,0},{2,6},{3,7},{4,5},{5,4},{6,2},{7,3},{8,9},{9,8},{10,14... | collective-permute-start | bytes 3686408 | tf_op jit(solution)/shard_map/ppermute | solution.py:49
  273.5 9.9 %collective-permute-start.49 = (bf16[48,4352]{1,0:T(8,128)(2,1)S(1)}, bf16[48,4352]{1,0:T(8,128)(2,1)S(1)}, u32[]{:S(2)}, u32[]{:S(2)}) collective-permute-start(bf16[48,4352]{1,0:T(8,128)(2,1)S(1)} %get-tuple-element.199), channel_id=1, source_target_pairs={{0,8},{1,9},{2,10},{3,11},{4,12},{5,13},{6,14},{7,15},{8,0},{9,1},... | collective-permute-start | bytes 1253384 | tf_op jit(solution)/shard_map/ppermute | solution.py:49
  280.7 10.2 %collective-permute-start.48 = (bf16[96,3200]{1,0:T(8,128)(2,1)S(1)}, bf16[96,3200]{1,0:T(8,128)(2,1)S(1)}, u32[]{:S(2)}, u32[]{:S(2)}) collective-permute-start(bf16[96,3200]{1,0:T(8,128)(2,1)S(1)} %get-tuple-element.196), channel_id=1, source_target_pairs={{0,4},{1,5},{2,3},{3,2},{4,0},{5,1},{6,7},{7,6},{8,12},{9,13},{10,... | collective-permute-start | bytes 1843208 | tf_op jit(solution)/shard_map/ppermute | solution.py:49
  283.5 10.8 %collective-permute-start.52 = (bf16[24,4352]{1,0:T(8,128)(2,1)S(1)}, bf16[24,4352]{1,0:T(8,128)(2,1)S(1)}, u32[]{:S(2)}, u32[]{:S(2)}) collective-permute-start(bf16[24,4352]{1,0:T(8,128)(2,1)S(1)} %add_convert_fusion.13), channel_id=1, source_target_pairs={{0,16},{1,17},{2,18},{3,19},{4,20},{5,21},{6,22},{7,23},{8,24},{9,... | collective-permute-start | bytes 626696 | tf_op jit(solution)/shard_map/ppermute | solution.py:49
  291.0 9.8 %collective-permute-start.50 = (bf16[48,3200]{1,0:T(8,128)(2,1)S(1)}, bf16[48,3200]{1,0:T(8,128)(2,1)S(1)}, u32[]{:S(2)}, u32[]{:S(2)}) collective-permute-start(bf16[48,3200]{1,0:T(8,128)(2,1)S(1)} %get-tuple-element.201), channel_id=1, source_target_pairs={{0,8},{1,9},{2,10},{3,11},{4,12},{5,13},{6,14},{7,15},{8,0},{9,1},... | collective-permute-start | bytes 921608 | tf_op jit(solution)/shard_map/ppermute | solution.py:49
  300.9 8.9 %collective-permute-start.51 = (bf16[24,3200]{1,0:T(8,128)(2,1)S(1)}, bf16[24,3200]{1,0:T(8,128)(2,1)S(1)}, u32[]{:S(2)}, u32[]{:S(2)}) collective-permute-start(bf16[24,3200]{1,0:T(8,128)(2,1)S(1)} %add_convert_fusion.22), channel_id=1, source_target_pairs={{0,16},{1,17},{2,18},{3,19},{4,20},{5,21},{6,22},{7,23},{8,24},{9,... | collective-permute-start | bytes 460808 | tf_op jit(solution)/shard_map/ppermute | solution.py:49
  (41 other events, 331.2 us)
Sparse Core Ops, SparseCore 0:
  55.1 52.4 all-gather.1
  168.0 28.8 reduce-scatter.2
  213.9 28.8 reduce-scatter.4

commit v3 on v2

--- a/solution.py
+++ b/solution.py
@@ -651,7 +651,7 @@
 
 
 def kernel_call(
-    body, name, outs, inputs, pieces=(), loaded=None, lengths=None, extra=(), cost=8
+    body, name, outs, inputs, pieces=(), loaded=None, lengths=None, extra=(), cost=12
 ):
     vmem = pl.BlockSpec(memory_space=pltpu.VMEM)
     specs = [vmem] * len(inputs) + [pl.BlockSpec(memory_space=pl.ANY)] * len(pieces)

time: 326 us -> 324 us (level)
  starting transfers between devices: 35.2 us -> 31.9 us
    ppermute x53, starting transfers between devices: 34.9 us -> 31.5 us  [swap(): return lax.ppermute(value, AXES, pairs(count, move))]
  transfers between devices with their start and end apart: 56 -> 56, of which waited for: 29 -> 28; matrix products, arithmetic and copies ran while one was open for 10% -> 10% of each run, Pallas kernels for 30% -> 30%
where the time goes in v3:
time: 324 us; the launch traced here: 320 us
  waiting for transfers between devices  119 us (37%)
  Pallas kernels  111 us (34%)
  starting transfers between devices  31.9 us (10%)
  other arithmetic  25.7 us (8%)
  local copies, waits for them, and re-layouts  17.3 us (5%)
  between operations  15 us (5%)
    ppermute x53, waiting for transfers between devices, swap(): return lax.ppermute(value, AXES, pairs(count, move))  119 us
    pallas_call x15, Pallas kernels, kernel_call(): pl.pallas_call(lambda *refs: body(refs), name=name, out_shape=outs, in_sp...  111 us
    ppermute x53, starting transfers between devices, swap(): return lax.ppermute(value, AXES, pairs(count, move))  31.5 us
    convert_element_type x16, other arithmetic, add_low(): return (left.astype(F32) + right.astype(F32)).astype(BF)  15.8 us
    unnamed x79, local copies, waits for them, and re-layouts  12.2 us
  transfers between devices with their start and end apart: 56, of which 28 were waited for; matrix products, arithmetic and copies ran while one was open for 10% of the time, Pallas kernels for 30%

profile of v3, /device:TPU:0, one launch (start us, length us, event | category | flops | bytes accessed | tf_op | source)
XLA Modules:
  0.0 319.7 jit_solution(7517386636490830364)
XLA Ops:
  7.3 2.2 pack.1
  9.4 5.1 %collective-permute-start.2 = (bf16[24,3200]{1,0:T(8,128)(2,1)}, bf16[24,3200]{1,0:T(8,128)(2,1)S(1)}, u32[]{:S(2)}, u32[]{:S(2)}) collective-permute-start(bf16[24,3200]{1,0:T(8,128)(2,1)} %get-tuple-element.87), channel_id=1, source_target_pairs={{0,24},{1,25},{2,26},{3,27},{4,28},{5,29},{6,30},{7,31},{8,16},{9,... | collective-permute-start | bytes 460808 | tf_op jit(solution)/shard_map/ppermute | solution.py:49
  16.1 11.6 %collective-permute-done = bf16[24,3200]{1,0:T(8,128)(2,1)S(1)} collective-permute-done((bf16[24,3200]{1,0:T(8,128)(2,1)}, bf16[24,3200]{1,0:T(8,128)(2,1)S(1)}, u32[]{:S(2)}, u32[]{:S(2)}) %collective-permute-start) | collective-permute-done | bytes 153632 | tf_op jit(solution)/shard_map/ppermute | solution.py:49
  27.8 1.6 collective-permute-start.4
  29.4 1.5 collective-permute-start.3
  31.2 10.3 %collective-permute-done.10 = bf16[24,4352]{1,0:T(8,128)(2,1)S(1)} collective-permute-done((bf16[24,4352]{1,0:T(8,128)(2,1)S(1)}, bf16[24,4352]{1,0:T(8,128)(2,1)S(1)}, u32[]{:S(2)}, u32[]{:S(2)}) %collective-permute-start.10) | collective-permute-done | bytes 208928 | tf_op jit(solution)/shard_map/ppermute | solution.py:49
  42.8 1.5 collective-permute-start.5
  44.3 8.9 %collective-permute-done.11 = bf16[48,4352]{1,0:T(8,128)(2,1)S(1)} collective-permute-done((bf16[48,4352]{1,0:T(8,128)(2,1)S(1)}, bf16[48,4352]{1,0:T(8,128)(2,1)S(1)}, u32[]{:S(2)}, u32[]{:S(2)}) %collective-permute-start.11) | collective-permute-done | bytes 417824 | tf_op jit(solution)/shard_map/ppermute | solution.py:49
  57.5 14.7 %collective-permute-done.12.refs_4_.refs_6_.refs_10_ = bf16[96,4352]{1,0:T(8,128)(2,1)} collective-permute-done((bf16[96,4352]{1,0:T(8,128)(2,1)S(1)}, bf16[96,4352]{1,0:T(8,128)(2,1)}, u32[]{:S(2)}, u32[]{:S(2)}) %collective-permute-start.12) | collective-permute-done | bytes 835616 | tf_op jit(solution)/shard_map/ppermute | solution.py:49
  72.7 8.8 %self_forward.1 = (bf16[128,2304]{1,0:T(8,128)(2,1)}, bf16[128,768]{1,0:T(8,128)(2,1)}, f32[128,768]{1,0:T(8,128)}, f32[64,768]{1,0:T(8,128)}, f32[64,768]{1,0:T...) custom-call(s32[2]{0:T(128)} %refs_0_.6, bf16[128,768]{1,0:T(8,128)(2,1)} %bitcast.46, ...), custom_call_target="tpu_custom_call" | custom-call | flops 10800000000 | bytes 36000000 | tf_op jit(solution)/shard_map/self_forward/pallas_call | solution.py:667
  81.6 3.4 %collective-permute-done.14.refs_6_.refs_8_.refs_12_ = bf16[96,4352]{1,0:T(8,128)(2,1)} collective-permute-done((bf16[96,4352]{1,0:T(8,128)(2,1)}, bf16[96,4352]{1,0:T(8,128)(2,1)}, u32[]{:S(2)}, u32[]{:S(2)}) %collective-permute-start.14) | collective-permute-done | bytes 835616 | tf_op jit(solution)/shard_map/ppermute | solution.py:49
  87.7 10.2 %image_rows.1 = (bf16[2,257,768]{2,1,0:T(8,128)(2,1)}, bf16[2,257,768]{2,1,0:T(8,128)(2,1)}) custom-call(bf16[2,257,1408]{2,1,0:T(8,128)(2,1)} %copy.41.refs_0_.refs_6_, bf16[768,768]{1,0:T(8,128)(2,1)} %fusion.refs_2_.refs_1_.refs_3_.refs_7_.refs_9_, f32[16,768]{1,0:T(8,128)} %get-tuple-element.89.refs_2_.refs_4_.refs_8_.refs_10_, ...), custom_call_target="tpu_custom_call" | custom-call | flops 10800000000 | bytes 36000000 | tf_op jit(solution)/shard_map/image_rows/pallas_call | solution.py:667
  98.5 8.0 %cross_forward.1 = (bf16[64,768]{1,0:T(8,128)(2,1)}, bf16[64,768]{1,0:T(8,128)(2,1)}, f32[64,768]{1,0:T(8,128)}, f32[64,768]{1,0:T(8,128)}, bf16[64,768]{1,0:T(8,128)(2,1)}) custom-call(f32[64,768]{1,0:T(8,128)} %get-tuple-element.88.refs_0_.refs_4_, bf16[2,257,768]{2,1,0:T(8,128)(2,1)} %get-tuple-element.94.refs_1_.refs_5_, ...), custom_call_target="tpu_custom_call" | custom-call | flops 10800000000 | bytes 36000000 | tf_op jit(solution)/shard_map/cross_forward/pallas_call | solution.py:667
  108.1 3.5 %collective-permute-done.19 = bf16[64,768]{1,0:T(8,128)(2,1)S(1)} collective-permute-done((bf16[64,768]{1,0:T(8,128)(2,1)}, bf16[64,768]{1,0:T(8,128)(2,1)S(1)}, u32[]{:S(2)}, u32[]{:S(2)}) %collective-permute-start.19) | collective-permute-done | bytes 98336 | tf_op jit(solution)/shard_map/ppermute | solution.py:49
  112.5 1.6 collective-permute-start.20
  114.8 5.0 %branch_up_1.1 = (f32[512,384]{1,0:T(8,128)}, bf16[512,384]{1,0:T(8,128)(2,1)}, f32[256,768]{1,0:T(8,128)}, bf16[256,768]{1,0:T(8,128)(2,1)}) custom-call(bf16[256,768]{1,0:T(8,128)(2,1)} %copy-done.21, bf16[256,768]{1,0:T(8,128)(2,1)} %copy-done.25, bf16[384,3328]{1,0:T(8,128)(2,1)} %all-gather.2.cloned.1.call-done.refs_2_.refs_6_), custom_call_target="tpu_custom_call" | custom-call | flops 10800000000 | bytes 36000000 | tf_op jit(solution)/shard_map/branch_up_1/pallas_call | solution.py:667
  124.3 4.9 %branch_up_0.1 = (f32[512,384]{1,0:T(8,128)}, bf16[512,384]{1,0:T(8,128)(2,1)}, f32[256,768]{1,0:T(8,128)}, bf16[256,768]{1,0:T(8,128)(2,1)}) custom-call(bf16[256,768]{1,0:T(8,128)(2,1)} %copy-done.6, bf16[256,768]{1,0:T(8,128)(2,1)} %copy-done.26, bf16[384,3328]{1,0:T(8,128)(2,1)} %all-gather.2.cloned.1.call-done.refs_2_.refs_6_), custom_call_target="tpu_custom_call" | custom-call | flops 10800000000 | bytes 36000000 | tf_op jit(solution)/shard_map/branch_up_0/pallas_call | solution.py:667
  135.2 2.2 branch_end_1.1
  140.1 2.1 collective-permute-done.37
  143.1 1.6 collective-permute-start.38
  145.3 2.2 branch_end_0.1
  148.1 4.2 %collective-permute-done.31 = bf16[64,768]{1,0:T(8,128)(2,1)S(1)} collective-permute-done((bf16[64,768]{1,0:T(8,128)(2,1)}, bf16[64,768]{1,0:T(8,128)(2,1)S(1)}, u32[]{:S(2)}, u32[]{:S(2)}) %collective-permute-start.31) | collective-permute-done | bytes 98336 | tf_op jit(solution)/shard_map/ppermute | solution.py:49
  154.0 5.2 %collective-permute-done.32 = bf16[128,768]{1,0:T(8,128)(2,1)S(1)} collective-permute-done((bf16[128,768]{1,0:T(8,128)(2,1)S(1)}, bf16[128,768]{1,0:T(8,128)(2,1)S(1)}, u32[]{:S(2)}, u32[]{:S(2)}) %collective-permute-start.32) | collective-permute-done | bytes 196640 | tf_op jit(solution)/shard_map/ppermute | solution.py:49
  160.9 6.0 %branch_down_1.1 = (f32[256,768]{1,0:T(8,128)}, bf16[256,768]{1,0:T(8,128)(2,1)}, bf16[384,1664]{1,0:T(8,128)(2,1)}) custom-call(bf16[256,768]{1,0:T(8,128)(2,1)} %copy-done.8, bf16[256,768]{1,0:T(8,128)(2,1)} %copy-done.28, bf16[256,768]{1,0:T(8,128)(2,1)} %copy-done.21, bf16[256,768]{1,0:T(8,128)(2,1)} %copy-done.25, ...), custom_call_target="tpu_custom_call" | custom-call | flops 10800000000 | bytes 36000000 | tf_op jit(solution)/shard_map/branch_down_1/pallas_call | solution.py:667
  168.5 6.2 %branch_down_0.1 = (f32[256,768]{1,0:T(8,128)}, bf16[256,768]{1,0:T(8,128)(2,1)}, bf16[384,1664]{1,0:T(8,128)(2,1)}) custom-call(bf16[256,768]{1,0:T(8,128)(2,1)} %copy-done.7, bf16[256,768]{1,0:T(8,128)(2,1)} %copy-done.27, bf16[256,768]{1,0:T(8,128)(2,1)} %copy-done.6, bf16[256,768]{1,0:T(8,128)(2,1)} %copy-done.26, ...), custom_call_target="tpu_custom_call" | custom-call | flops 10800000000 | bytes 36000000 | tf_op jit(solution)/shard_map/branch_down_0/pallas_call | solution.py:667
  177.2 3.5 %collective-permute-done.41 = bf16[128,768]{1,0:T(8,128)(2,1)S(1)} collective-permute-done((bf16[128,768]{1,0:T(8,128)(2,1)S(1)}, bf16[128,768]{1,0:T(8,128)(2,1)S(1)}, u32[]{:S(2)}, u32[]{:S(2)}) %collective-permute-start.41) | collective-permute-done | bytes 196640 | tf_op jit(solution)/shard_map/ppermute | solution.py:49
  184.1 1.9 collective-permute-done.42.refs_3_
  186.0 2.1 collective-permute-done.36.refs_1_
  188.7 10.9 %cross_backward.1 = (bf16[64,768]{1,0:T(8,128)(2,1)}, bf16[2,257,768]{2,1,0:T(8,128)(2,1)}, bf16[2,257,768]{2,1,0:T(8,128)(2,1)}, bf16[64,768]{1,0:T(8,128)(2,1)}, f32[64,768]{1,0:T(8,128)}, /*index=5*/f32[8,768]{1,0:T(8,128)}) custom-call(bf16[64,768]{1,0:T(8,128)(2,1)} %get-tuple-element.221.refs_0_, bf16[64,768]{1,0:T(8,128)(2,1)} %copy-done.31, ...), custom_call_target="tpu_custom_call" | custom-call | flops 3600000000 | bytes 12000000 | tf_op jit(solution)/shard_map/cross_backward/pallas_call | solution.py:667
  199.7 13.3 %cross_weights.1 = (bf16[384,4352]{1,0:T(8,128)(2,1)}, bf16[384,4352]{1,0:T(8,128)(2,1)}) custom-call(bf16[64,768]{1,0:T(8,128)(2,1)} %get-tuple-element.126.refs_0_, bf16[2,257,768]{2,1,0:T(8,128)(2,1)} %get-tuple-element.127.refs_1_.refs_0_, bf16[2,257,768]{2,1,0:T(8,128)(2,1)} %get-tuple-element.128.refs_2_.refs_1_, ...), custom_call_target="tpu_custom_call" | custom-call | flops 3600000000 | bytes 12000000 | tf_op jit(solution)/shard_map/cross_weights/pallas_call | solution.py:667
  212.9 10.0 %feature_grad.1 = f32[2,257,1408]{2,1,0:T(8,128)} custom-call(bf16[2,257,768]{2,1,0:T(8,128)(2,1)} %get-tuple-element.127.refs_1_.refs_0_, bf16[2,257,768]{2,1,0:T(8,128)(2,1)} %get-tuple-element.128.refs_2_.refs_1_, bf16[768,768]{1,0:T(8,128)(2,1)} %fusion.refs_2_.refs_1_.refs_3_.refs_7_.refs_9_, bf16[96,4352]{1,0:T(8,128)(2,1)} %copy-done.17, ...), custom_call_target="tpu_custom_call" | custom-call | flops 3600000000 | bytes 12000000 | tf_op jit(solution)/shard_map/feature_grad/pallas_call | solution.py:667
  223.0 1.7 copy-done
  224.7 3.9 %add_convert_fusion = (bf16[192,4352]{1,0:T(8,128)(2,1)S(1)}, bf16[192,4352]{1,0:T(8,128)(2,1)S(1)}) fusion(bf16[384,4352]{1,0:T(8,128)(2,1)} %copy-done, bf16[384,4352]{1,0:T(8,128)(2,1)} %get-tuple-element.131), kind=kLoop, calls=%fused_computation | loop fusion | flops 6684672 | bytes 10027008 | tf_op jit(solution)/shard_map/convert_element_type | solution.py:93
  229.0 3.1 copy.43
  232.1 14.6 %self_backward.1 = (bf16[128,2304]{1,0:T(8,128)(2,1)}, f32[128,768]{1,0:T(8,128)}, bf16[384,3200]{1,0:T(8,128)(2,1)}, bf16[384,3200]{1,0:T(8,128)(2,1)}) custom-call(s32[2]{0:T(128)} %refs_0_.6, f32[64,768]{1,0:T(8,128)} %get-tuple-element.135.refs_1_, bf16[64,768]{1,0:T(8,128)(2,1)} %get-tuple-element.218.refs_2_, bf16[64,768]{1,0:T(8,128)(2,1)} %copy-done.29, ...), custom_call_target="tpu_custom_call" | custom-call | flops 3600000000 | bytes 12000000 | tf_op jit(solution)/shard_map/self_backward/pallas_call | solution.py:667
  246.7 3.6 %collective-permute-done.44 = bf16[192,4352]{1,0:T(8,128)(2,1)} collective-permute-done((bf16[192,4352]{1,0:T(8,128)(2,1)S(1)}, bf16[192,4352]{1,0:T(8,128)(2,1)}, u32[]{:S(2)}, u32[]{:S(2)}) %collective-permute-start.44) | collective-permute-done | bytes 1671200 | tf_op jit(solution)/shard_map/ppermute | solution.py:49
  250.9 1.9 add_convert_fusion.4
  253.5 1.6 collective-permute-done.45
  255.1 1.6 add_convert_fusion.2
  257.1 6.4 %hidden_grad.1 = f32[128,768]{1,0:T(8,128)} custom-call(bf16[128,2304]{1,0:T(8,128)(2,1)} %get-tuple-element.143.refs_0_, f32[128,768]{1,0:T(8,128)} %get-tuple-element.144.refs_1_, bf16[768,768]{1,0:T(8,128)(2,1)} %fusion.refs_2_.refs_1_.refs_3_.refs_7_.refs_9_, bf16[96,3200]{1,0:T(8,128)(2,1)} %copy-done.18, bf16[96,3200]{1,0:T(8,128)(2,1)} %copy-done.23, ...), custom_call_target="tpu_custom_call" | custom-call | flops 3600000000 | bytes 12000000 | tf_op jit(solution)/shard_map/hidden_grad/pallas_call | solution.py:667
  263.5 7.8 %collective-permute-done.47 = bf16[96,4352]{1,0:T(8,128)(2,1)} collective-permute-done((bf16[96,4352]{1,0:T(8,128)(2,1)S(1)}, bf16[96,4352]{1,0:T(8,128)(2,1)}, u32[]{:S(2)}, u32[]{:S(2)}) %collective-permute-start.47) | collective-permute-done | bytes 835616 | tf_op jit(solution)/shard_map/ppermute | solution.py:49
  272.9 5.4 %collective-permute-done.46 = bf16[192,3200]{1,0:T(8,128)(2,1)} collective-permute-done((bf16[192,3200]{1,0:T(8,128)(2,1)}, bf16[192,3200]{1,0:T(8,128)(2,1)}, u32[]{:S(2)}, u32[]{:S(2)}) %collective-permute-start.46) | collective-permute-done | bytes 1228832 | tf_op jit(solution)/shard_map/ppermute | solution.py:49
  278.2 1.5 add_convert_fusion.6
  280.5 2.2 collective-permute-done.49
  282.9 7.1 %collective-permute-done.48 = bf16[96,3200]{1,0:T(8,128)(2,1)S(1)} collective-permute-done((bf16[96,3200]{1,0:T(8,128)(2,1)S(1)}, bf16[96,3200]{1,0:T(8,128)(2,1)S(1)}, u32[]{:S(2)}, u32[]{:S(2)}) %collective-permute-start.48) | collective-permute-done | bytes 614432 | tf_op jit(solution)/shard_map/ppermute | solution.py:49
  290.4 2.3 collective-permute-done.52
  294.2 5.1 %collective-permute-done.50 = bf16[48,3200]{1,0:T(8,128)(2,1)S(1)} collective-permute-done((bf16[48,3200]{1,0:T(8,128)(2,1)S(1)}, bf16[48,3200]{1,0:T(8,128)(2,1)S(1)}, u32[]{:S(2)}, u32[]{:S(2)}) %collective-permute-start.50) | collective-permute-done | bytes 307232 | tf_op jit(solution)/shard_map/ppermute | solution.py:49
  302.1 5.7 %collective-permute-done.51 = bf16[24,3200]{1,0:T(8,128)(2,1)S(1)} collective-permute-done((bf16[24,3200]{1,0:T(8,128)(2,1)S(1)}, bf16[24,3200]{1,0:T(8,128)(2,1)S(1)}, u32[]{:S(2)}, u32[]{:S(2)}) %collective-permute-start.51) | collective-permute-done | bytes 153632 | tf_op jit(solution)/shard_map/ppermute | solution.py:49
  (215 shorter events, 55.4 us)
Async XLA Ops:
  7.2 106.9 %all-gather.2.cloned.1.call-start = ((), (), s32[]{:S(2)}) async-start(), calls=%async_computation.2 | async-start | bytes 3194880 | tf_op jit(solution)/shard_map/all_gather | solution.py:726
  9.4 18.3 %collective-permute-start.2 = (bf16[24,3200]{1,0:T(8,128)(2,1)}, bf16[24,3200]{1,0:T(8,128)(2,1)S(1)}, u32[]{:S(2)}, u32[]{:S(2)}) collective-permute-start(bf16[24,3200]{1,0:T(8,128)(2,1)} %get-tuple-element.87), channel_id=1, source_target_pairs={{0,24},{1,25},{2,26},{3,27},{4,28},{5,29},{6,30},{7,31},{8,16},{9,... | collective-permute-start | bytes 460808 | tf_op jit(solution)/shard_map/ppermute | solution.py:49
  14.5 13.2 %collective-permute-start.1 = (bf16[24,3200]{1,0:T(8,128)(2,1)}, bf16[24,3200]{1,0:T(8,128)(2,1)S(1)}, u32[]{:S(2)}, u32[]{:S(2)}) collective-permute-start(bf16[24,3200]{1,0:T(8,128)(2,1)} %get-tuple-element.87), channel_id=1, source_target_pairs={{0,8},{1,9},{2,10},{3,11},{4,12},{5,13},{6,14},{7,15},{8,0},{9,1},... | collective-permute-start | bytes 460808 | tf_op jit(solution)/shard_map/ppermute | solution.py:49
  14.5 13.2 %collective-permute-start = (bf16[24,3200]{1,0:T(8,128)(2,1)}, bf16[24,3200]{1,0:T(8,128)(2,1)S(1)}, u32[]{:S(2)}, u32[]{:S(2)}) collective-permute-start(bf16[24,3200]{1,0:T(8,128)(2,1)} %get-tuple-element.87), channel_id=1, source_target_pairs={{0,16},{1,17},{2,18},{3,19},{4,20},{5,21},{6,22},{7,23},{8,24},{9,... | collective-permute-start | bytes 460808 | tf_op jit(solution)/shard_map/ppermute | solution.py:49
  27.8 25.5 %collective-permute-start.4 = (bf16[96,3200]{1,0:T(8,128)(2,1)S(1)}, bf16[96,3200]{1,0:T(8,128)(2,1)S(1)}, u32[]{:S(2)}, u32[]{:S(2)}) collective-permute-start(bf16[96,3200]{1,0:T(8,128)(2,1)S(1)} %constant_dynamic-update-slice_fusion.refs_3_.refs_14_), channel_id=1, source_target_pairs={{0,1},{1,0},{2,6},{3,7},{4,5},{5,4},{6,2},{7,3},{8,9},{9,8},{10,14... | collective-permute-start | bytes 1843208 | tf_op jit(solution)/shard_map/ppermute | solution.py:49
  29.4 13.4 %collective-permute-start.3 = (bf16[96,3200]{1,0:T(8,128)(2,1)S(1)}, bf16[96,3200]{1,0:T(8,128)(2,1)S(1)}, u32[]{:S(2)}, u32[]{:S(2)}) collective-permute-start(bf16[96,3200]{1,0:T(8,128)(2,1)S(1)} %constant_dynamic-update-slice_fusion.refs_3_.refs_14_), channel_id=1, source_target_pairs={{0,4},{1,5},{2,3},{3,2},{4,0},{5,1},{6,7},{7,6},{8,12},{9,13},{10,... | collective-permute-start | bytes 1843208 | tf_op jit(solution)/shard_map/ppermute | solution.py:49
  30.9 10.7 %collective-permute-start.10 = (bf16[24,4352]{1,0:T(8,128)(2,1)S(1)}, bf16[24,4352]{1,0:T(8,128)(2,1)S(1)}, u32[]{:S(2)}, u32[]{:S(2)}) collective-permute-start(bf16[24,4352]{1,0:T(8,128)(2,1)S(1)} %pad_maximum_fusion.8), channel_id=1, source_target_pairs={{0,16},{1,17},{2,18},{3,19},{4,20},{5,21},{6,22},{7,23},{8,24},{9,... | collective-permute-start | bytes 626696 | tf_op jit(solution)/shard_map/ppermute | solution.py:49
  41.6 11.6 %collective-permute-start.11 = (bf16[48,4352]{1,0:T(8,128)(2,1)S(1)}, bf16[48,4352]{1,0:T(8,128)(2,1)S(1)}, u32[]{:S(2)}, u32[]{:S(2)}) collective-permute-start(bf16[48,4352]{1,0:T(8,128)(2,1)S(1)} %pad_maximum_fusion.2), channel_id=1, source_target_pairs={{0,8},{1,9},{2,10},{3,11},{4,12},{5,13},{6,14},{7,15},{8,0},{9,1},... | collective-permute-start | bytes 1253384 | tf_op jit(solution)/shard_map/ppermute | solution.py:49
  42.8 11.6 %collective-permute-start.5 = (bf16[96,3200]{1,0:T(8,128)(2,1)S(1)}, bf16[96,3200]{1,0:T(8,128)(2,1)S(1)}, u32[]{:S(2)}, u32[]{:S(2)}) collective-permute-start(bf16[96,3200]{1,0:T(8,128)(2,1)S(1)} %collective-permute-done.3.refs_4_.refs_15_), channel_id=1, source_target_pairs={{0,1},{1,0},{2,6},{3,7},{4,5},{5,4},{6,2},{7,3},{8,9},{9,8},{10,14... | collective-permute-start | bytes 1843208 | tf_op jit(solution)/shard_map/ppermute | solution.py:49
  53.3 18.9 %collective-permute-start.12 = (bf16[96,4352]{1,0:T(8,128)(2,1)S(1)}, bf16[96,4352]{1,0:T(8,128)(2,1)}, u32[]{:S(2)}, u32[]{:S(2)}) collective-permute-start(bf16[96,4352]{1,0:T(8,128)(2,1)S(1)} %constant_dynamic-update-slice_fusion.4.refs_3_.refs_5_.refs_9_), channel_id=1, source_target_pairs={{0,4},{1,5},{2,3},{3,2},{4,0},{5,1},{6,7},{7,6},{8,12},{9,13},{10,... | collective-permute-start | bytes 2506760 | tf_op jit(solution)/shard_map/ppermute | solution.py:49
  54.4 17.8 %collective-permute-start.7 = (bf16[96,3200]{1,0:T(8,128)(2,1)S(1)}, bf16[96,3200]{1,0:T(8,128)(2,1)}, u32[]{:S(2)}, u32[]{:S(2)}) collective-permute-start(bf16[96,3200]{1,0:T(8,128)(2,1)S(1)} %collective-permute-done.3.refs_4_.refs_15_), channel_id=1, source_target_pairs={{0,2},{1,3},{2,0},{3,1},{4,6},{5,7},{6,4},{7,5},{8,10},{9,11},{10,... | collective-permute-start | bytes 1843208 | tf_op jit(solution)/shard_map/ppermute | solution.py:49
  54.4 18.3 %collective-permute-start.9 = (bf16[96,3200]{1,0:T(8,128)(2,1)S(1)}, bf16[96,3200]{1,0:T(8,128)(2,1)}, u32[]{:S(2)}, u32[]{:S(2)}) collective-permute-start(bf16[96,3200]{1,0:T(8,128)(2,1)S(1)} %collective-permute-done.5.refs_6_.refs_17_), channel_id=1, source_target_pairs={{0,2},{1,3},{2,0},{3,1},{4,6},{5,7},{6,4},{7,5},{8,10},{9,11},{10,... | collective-permute-start | bytes 1843208 | tf_op jit(solution)/shard_map/ppermute | solution.py:49
  55.0 144.7 %reduce-scatter.3.cloned.1.call-start = ((), (), s32[]{:S(2)}) async-start(), calls=%async_computation.3 | async-start | bytes 1597440 | tf_op jit(solution)/shard_map/reduce_scatter | solution.py:820
  56.6 29.8 %collective-permute-start.15 = (bf16[96,4352]{1,0:T(8,128)(2,1)S(1)}, bf16[96,4352]{1,0:T(8,128)(2,1)}, u32[]{:S(2)}, u32[]{:S(2)}) collective-permute-start(bf16[96,4352]{1,0:T(8,128)(2,1)S(1)} %constant_dynamic-update-slice_fusion.4.refs_3_.refs_5_.refs_9_), channel_id=1, source_target_pairs={{0,2},{1,3},{2,0},{3,1},{4,6},{5,7},{6,4},{7,5},{8,10},{9,11},{10,... | collective-permute-start | bytes 2506760 | tf_op jit(solution)/shard_map/ppermute | solution.py:49
  57.0 24.6 %collective-permute-start.13 = (bf16[96,4352]{1,0:T(8,128)(2,1)S(1)}, bf16[96,4352]{1,0:T(8,128)(2,1)}, u32[]{:S(2)}, u32[]{:S(2)}) collective-permute-start(bf16[96,4352]{1,0:T(8,128)(2,1)S(1)} %constant_dynamic-update-slice_fusion.4.refs_3_.refs_5_.refs_9_), channel_id=1, source_target_pairs={{0,1},{1,0},{2,6},{3,7},{4,5},{5,4},{6,2},{7,3},{8,9},{9,8},{10,14... | collective-permute-start | bytes 2506760 | tf_op jit(solution)/shard_map/ppermute | solution.py:49
  72.2 14.1 %collective-permute-start.16 = (bf16[96,4352]{1,0:T(8,128)(2,1)}, bf16[96,4352]{1,0:T(8,128)(2,1)}, u32[]{:S(2)}, u32[]{:S(2)}) collective-permute-start(bf16[96,4352]{1,0:T(8,128)(2,1)} %collective-permute-done.12.refs_4_.refs_6_.refs_10_), channel_id=1, source_target_pairs={{0,2},{1,3},{2,0},{3,1},{4,6},{5,7},{6,4},{7,5},{8,10},{9,11},{10,... | collective-permute-start | bytes 2506760 | tf_op jit(solution)/shard_map/ppermute | solution.py:49
  72.2 12.8 %collective-permute-start.14 = (bf16[96,4352]{1,0:T(8,128)(2,1)}, bf16[96,4352]{1,0:T(8,128)(2,1)}, u32[]{:S(2)}, u32[]{:S(2)}) collective-permute-start(bf16[96,4352]{1,0:T(8,128)(2,1)} %collective-permute-done.12.refs_4_.refs_6_.refs_10_), channel_id=1, source_target_pairs={{0,1},{1,0},{2,6},{3,7},{4,5},{5,4},{6,2},{7,3},{8,9},{9,8},{10,14... | collective-permute-start | bytes 2506760 | tf_op jit(solution)/shard_map/ppermute | solution.py:49
  81.5 4.8 %collective-permute-start.17 = (bf16[96,4352]{1,0:T(8,128)(2,1)}, bf16[96,4352]{1,0:T(8,128)(2,1)}, u32[]{:S(2)}, u32[]{:S(2)}) collective-permute-start(bf16[96,4352]{1,0:T(8,128)(2,1)} %collective-permute-done.13.refs_5_.refs_7_.refs_11_), channel_id=1, source_target_pairs={{0,2},{1,3},{2,0},{3,1},{4,6},{5,7},{6,4},{7,5},{8,10},{9,11},{10,... | collective-permute-start | bytes 2506760 | tf_op jit(solution)/shard_map/ppermute | solution.py:49
  86.3 11.6 %collective-permute-start.25 = (bf16[64,768]{1,0:T(8,128)(2,1)S(1)}, bf16[64,768]{1,0:T(8,128)(2,1)S(1)}, u32[]{:S(2)}, u32[]{:S(2)}) collective-permute-start(bf16[64,768]{1,0:T(8,128)(2,1)S(1)} %copy-done.11), channel_id=1, source_target_pairs={{0,4},{1,5},{2,3},{3,2},{4,0},{5,1},{6,7},{7,6},{8,12},{9,13},{10,... | collective-permute-start | bytes 294920 | tf_op jit(solution)/shard_map/ppermute | solution.py:49
  98.0 8.6 %collective-permute-start.26 = (bf16[128,768]{1,0:T(8,128)(2,1)S(1)}, bf16[128,768]{1,0:T(8,128)(2,1)S(1)}, u32[]{:S(2)}, u32[]{:S(2)}) collective-permute-start(bf16[128,768]{1,0:T(8,128)(2,1)S(1)} %pad_maximum_fusion.10), channel_id=1, source_target_pairs={{0,1},{1,0},{2,6},{3,7},{4,5},{5,4},{6,2},{7,3},{8,9},{9,8},{10,14... | collective-permute-start | bytes 589832 | tf_op jit(solution)/shard_map/ppermute | solution.py:49
  106.6 7.5 %collective-permute-start.27 = (bf16[256,768]{1,0:T(8,128)(2,1)S(1)}, bf16[256,768]{1,0:T(8,128)(2,1)S(1)}, u32[]{:S(2)}, u32[]{:S(2)}) collective-permute-start(bf16[256,768]{1,0:T(8,128)(2,1)S(1)} %constant_dynamic-update-slice_fusion.7.refs_0_.refs_2_), channel_id=1, source_target_pairs={{0,2},{1,3},{2,0},{3,1},{4,6},{5,7},{6,4},{7,5},{8,10},{9,11},{10,... | collective-permute-start | bytes 1179656 | tf_op jit(solution)/shard_map/ppermute | solution.py:49
  106.7 4.9 %collective-permute-start.19 = (bf16[64,768]{1,0:T(8,128)(2,1)}, bf16[64,768]{1,0:T(8,128)(2,1)S(1)}, u32[]{:S(2)}, u32[]{:S(2)}) collective-permute-start(bf16[64,768]{1,0:T(8,128)(2,1)} %get-tuple-element.96), channel_id=1, source_target_pairs={{0,4},{1,5},{2,3},{3,2},{4,0},{5,1},{6,7},{7,6},{8,12},{9,13},{10,... | collective-permute-start | bytes 294920 | tf_op jit(solution)/shard_map/ppermute | solution.py:49
  112.5 7.4 %collective-permute-start.20 = (bf16[128,768]{1,0:T(8,128)(2,1)S(1)}, bf16[128,768]{1,0:T(8,128)(2,1)S(1)}, u32[]{:S(2)}, u32[]{:S(2)}) collective-permute-start(bf16[128,768]{1,0:T(8,128)(2,1)S(1)} %pad_maximum_fusion.9), channel_id=1, source_target_pairs={{0,1},{1,0},{2,6},{3,7},{4,5},{5,4},{6,2},{7,3},{8,9},{9,8},{10,14... | collective-permute-start | bytes 589832 | tf_op jit(solution)/shard_map/ppermute | solution.py:49
  123.0 6.3 %collective-permute-start.29 = (bf16[128,768]{1,0:T(8,128)(2,1)S(1)}, bf16[128,768]{1,0:T(8,128)(2,1)S(1)}, u32[]{:S(2)}, u32[]{:S(2)}) collective-permute-start(bf16[128,768]{1,0:T(8,128)(2,1)S(1)} %get-tuple-element.209), channel_id=1, source_target_pairs={{0,1},{1,0},{2,6},{3,7},{4,5},{5,4},{6,2},{7,3},{8,9},{9,8},{10,14... | collective-permute-start | bytes 589832 | tf_op jit(solution)/shard_map/ppermute | solution.py:49
  129.9 4.6 %collective-permute-start.30 = (bf16[64,768]{1,0:T(8,128)(2,1)S(1)}, bf16[64,768]{1,0:T(8,128)(2,1)S(1)}, u32[]{:S(2)}, u32[]{:S(2)}) collective-permute-start(bf16[64,768]{1,0:T(8,128)(2,1)S(1)} %get-tuple-element.224), channel_id=1, source_target_pairs={{0,4},{1,5},{2,3},{3,2},{4,0},{5,1},{6,7},{7,6},{8,12},{9,13},{10,... | collective-permute-start | bytes 294920 | tf_op jit(solution)/shard_map/ppermute | solution.py:49
  132.5 6.2 %collective-permute-start.23 = (bf16[128,768]{1,0:T(8,128)(2,1)S(1)}, bf16[128,768]{1,0:T(8,128)(2,1)S(1)}, u32[]{:S(2)}, u32[]{:S(2)}) collective-permute-start(bf16[128,768]{1,0:T(8,128)(2,1)S(1)} %get-tuple-element.207), channel_id=1, source_target_pairs={{0,1},{1,0},{2,6},{3,7},{4,5},{5,4},{6,2},{7,3},{8,9},{9,8},{10,14... | collective-permute-start | bytes 589832 | tf_op jit(solution)/shard_map/ppermute | solution.py:49
  137.3 4.8 %collective-permute-start.37 = (bf16[64,768]{1,0:T(8,128)(2,1)}, bf16[64,768]{1,0:T(8,128)(2,1)S(1)}, u32[]{:S(2)}, u32[]{:S(2)}) collective-permute-start(bf16[64,768]{1,0:T(8,128)(2,1)} %get-tuple-element.114), channel_id=1, source_target_pairs={{0,4},{1,5},{2,3},{3,2},{4,0},{5,1},{6,7},{7,6},{8,12},{9,13},{10,... | collective-permute-start | bytes 294920 | tf_op jit(solution)/shard_map/ppermute | solution.py:49
  139.4 5.3 %collective-permute-start.24 = (bf16[64,768]{1,0:T(8,128)(2,1)S(1)}, bf16[64,768]{1,0:T(8,128)(2,1)S(1)}, u32[]{:S(2)}, u32[]{:S(2)}) collective-permute-start(bf16[64,768]{1,0:T(8,128)(2,1)S(1)} %get-tuple-element.222), channel_id=1, source_target_pairs={{0,4},{1,5},{2,3},{3,2},{4,0},{5,1},{6,7},{7,6},{8,12},{9,13},{10,... | collective-permute-start | bytes 294920 | tf_op jit(solution)/shard_map/ppermute | solution.py:49
  143.1 9.2 %collective-permute-start.38 = (bf16[128,768]{1,0:T(8,128)(2,1)S(1)}, bf16[128,768]{1,0:T(8,128)(2,1)S(1)}, u32[]{:S(2)}, u32[]{:S(2)}) collective-permute-start(bf16[128,768]{1,0:T(8,128)(2,1)S(1)} %pad_maximum_fusion.13), channel_id=1, source_target_pairs={{0,1},{1,0},{2,6},{3,7},{4,5},{5,4},{6,2},{7,3},{8,9},{9,8},{10,14... | collective-permute-start | bytes 589832 | tf_op jit(solution)/shard_map/ppermute | solution.py:49
  147.5 4.8 %collective-permute-start.31 = (bf16[64,768]{1,0:T(8,128)(2,1)}, bf16[64,768]{1,0:T(8,128)(2,1)S(1)}, u32[]{:S(2)}, u32[]{:S(2)}) collective-permute-start(bf16[64,768]{1,0:T(8,128)(2,1)} %get-tuple-element.109), channel_id=1, source_target_pairs={{0,4},{1,5},{2,3},{3,2},{4,0},{5,1},{6,7},{7,6},{8,12},{9,13},{10,... | collective-permute-start | bytes 294920 | tf_op jit(solution)/shard_map/ppermute | solution.py:49
  152.4 7.8 %collective-permute-start.39 = (bf16[256,768]{1,0:T(8,128)(2,1)S(1)}, bf16[256,768]{1,0:T(8,128)(2,1)S(1)}, u32[]{:S(2)}, u32[]{:S(2)}) collective-permute-start(bf16[256,768]{1,0:T(8,128)(2,1)S(1)} %pad_maximum_fusion.5.refs_0_), channel_id=1, source_target_pairs={{0,2},{1,3},{2,0},{3,1},{4,6},{5,7},{6,4},{7,5},{8,10},{9,11},{10,... | collective-permute-start | bytes 1179656 | tf_op jit(solution)/shard_map/ppermute | solution.py:49
  153.4 5.7 %collective-permute-start.32 = (bf16[128,768]{1,0:T(8,128)(2,1)S(1)}, bf16[128,768]{1,0:T(8,128)(2,1)S(1)}, u32[]{:S(2)}, u32[]{:S(2)}) collective-permute-start(bf16[128,768]{1,0:T(8,128)(2,1)S(1)} %pad_maximum_fusion.12), channel_id=1, source_target_pairs={{0,1},{1,0},{2,6},{3,7},{4,5},{5,4},{6,2},{7,3},{8,9},{9,8},{10,14... | collective-permute-start | bytes 589832 | tf_op jit(solution)/shard_map/ppermute | solution.py:49
  160.1 7.7 %collective-permute-start.33 = (bf16[256,768]{1,0:T(8,128)(2,1)S(1)}, bf16[256,768]{1,0:T(8,128)(2,1)S(1)}, u32[]{:S(2)}, u32[]{:S(2)}) collective-permute-start(bf16[256,768]{1,0:T(8,128)(2,1)S(1)} %pad_maximum_fusion.4.refs_0_), channel_id=1, source_target_pairs={{0,2},{1,3},{2,0},{3,1},{4,6},{5,7},{6,4},{7,5},{8,10},{9,11},{10,... | collective-permute-start | bytes 1179656 | tf_op jit(solution)/shard_map/ppermute | solution.py:49
  167.0 83.2 %reduce-scatter.5.cloned.1.call-start = ((), (), s32[]{:S(2)}) async-start(), calls=%async_computation.4 | async-start | bytes 1597440 | tf_op jit(solution)/shard_map/reduce_scatter | solution.py:820
  167.2 7.6 %collective-permute-start.40 = (bf16[256,768]{1,0:T(8,128)(2,1)}, bf16[256,768]{1,0:T(8,128)(2,1)S(1)}, u32[]{:S(2)}, u32[]{:S(2)}) collective-permute-start(bf16[256,768]{1,0:T(8,128)(2,1)} %get-tuple-element.118), channel_id=1, source_target_pairs={{0,2},{1,3},{2,0},{3,1},{4,6},{5,7},{6,4},{7,5},{8,10},{9,11},{10,... | collective-permute-start | bytes 1179656 | tf_op jit(solution)/shard_map/ppermute | solution.py:49
  174.9 5.7 %collective-permute-start.41 = (bf16[128,768]{1,0:T(8,128)(2,1)S(1)}, bf16[128,768]{1,0:T(8,128)(2,1)S(1)}, u32[]{:S(2)}, u32[]{:S(2)}) collective-permute-start(bf16[128,768]{1,0:T(8,128)(2,1)S(1)} %get-tuple-element.203), channel_id=1, source_target_pairs={{0,1},{1,0},{2,6},{3,7},{4,5},{5,4},{6,2},{7,3},{8,9},{9,8},{10,14... | collective-permute-start | bytes 589832 | tf_op jit(solution)/shard_map/ppermute | solution.py:49
  176.8 5.9 %collective-permute-start.35 = (bf16[128,768]{1,0:T(8,128)(2,1)S(1)}, bf16[128,768]{1,0:T(8,128)(2,1)S(1)}, u32[]{:S(2)}, u32[]{:S(2)}) collective-permute-start(bf16[128,768]{1,0:T(8,128)(2,1)S(1)} %get-tuple-element.205), channel_id=1, source_target_pairs={{0,1},{1,0},{2,6},{3,7},{4,5},{5,4},{6,2},{7,3},{8,9},{9,8},{10,14... | collective-permute-start | bytes 589832 | tf_op jit(solution)/shard_map/ppermute | solution.py:49
  181.3 4.6 %collective-permute-start.42 = (bf16[64,768]{1,0:T(8,128)(2,1)S(1)}, bf16[64,768]{1,0:T(8,128)(2,1)S(1)}, u32[]{:S(2)}, u32[]{:S(2)}) collective-permute-start(bf16[64,768]{1,0:T(8,128)(2,1)S(1)} %get-tuple-element.219), channel_id=1, source_target_pairs={{0,4},{1,5},{2,3},{3,2},{4,0},{5,1},{6,7},{7,6},{8,12},{9,13},{10,... | collective-permute-start | bytes 294920 | tf_op jit(solution)/shard_map/ppermute | solution.py:49
  212.9 10.0 %collective-permute-start.43 = (bf16[384,4352]{1,0:T(8,128)(2,1)}, bf16[384,4352]{1,0:T(8,128)(2,1)S(1)}, u32[]{:S(2)}, u32[]{:S(2)}) collective-permute-start(bf16[384,4352]{1,0:T(8,128)(2,1)} %get-tuple-element.132), channel_id=1, source_target_pairs={{0,2},{1,3},{2,0},{3,1},{4,6},{5,7},{6,4},{7,5},{8,10},{9,11},{10,... | collective-permute-start | bytes 10027016 | tf_op jit(solution)/shard_map/ppermute | solution.py:49
  228.6 21.6 %collective-permute-start.44 = (bf16[192,4352]{1,0:T(8,128)(2,1)S(1)}, bf16[192,4352]{1,0:T(8,128)(2,1)}, u32[]{:S(2)}, u32[]{:S(2)}) collective-permute-start(bf16[192,4352]{1,0:T(8,128)(2,1)S(1)} %get-tuple-element.191), channel_id=1, source_target_pairs={{0,1},{1,0},{2,6},{3,7},{4,5},{5,4},{6,2},{7,3},{8,9},{9,8},{10,14... | collective-permute-start | bytes 5013512 | tf_op jit(solution)/shard_map/ppermute | solution.py:49
  250.2 4.9 %collective-permute-start.45 = (bf16[384,3200]{1,0:T(8,128)(2,1)}, bf16[384,3200]{1,0:T(8,128)(2,1)S(1)}, u32[]{:S(2)}, u32[]{:S(2)}) collective-permute-start(bf16[384,3200]{1,0:T(8,128)(2,1)} %get-tuple-element.149), channel_id=1, source_target_pairs={{0,2},{1,3},{2,0},{3,1},{4,6},{5,7},{6,4},{7,5},{8,10},{9,11},{10,... | collective-permute-start | bytes 7372808 | tf_op jit(solution)/shard_map/ppermute | solution.py:49
  252.9 18.5 %collective-permute-start.47 = (bf16[96,4352]{1,0:T(8,128)(2,1)S(1)}, bf16[96,4352]{1,0:T(8,128)(2,1)}, u32[]{:S(2)}, u32[]{:S(2)}) collective-permute-start(bf16[96,4352]{1,0:T(8,128)(2,1)S(1)} %get-tuple-element.194), channel_id=1, source_target_pairs={{0,4},{1,5},{2,3},{3,2},{4,0},{5,1},{6,7},{7,6},{8,12},{9,13},{10,... | collective-permute-start | bytes 2506760 | tf_op jit(solution)/shard_map/ppermute | solution.py:49
  256.7 21.5 %collective-permute-start.46 = (bf16[192,3200]{1,0:T(8,128)(2,1)}, bf16[192,3200]{1,0:T(8,128)(2,1)}, u32[]{:S(2)}, u32[]{:S(2)}) collective-permute-start(bf16[192,3200]{1,0:T(8,128)(2,1)} %get-tuple-element.193), channel_id=1, source_target_pairs={{0,1},{1,0},{2,6},{3,7},{4,5},{5,4},{6,2},{7,3},{8,9},{9,8},{10,14... | collective-permute-start | bytes 3686408 | tf_op jit(solution)/shard_map/ppermute | solution.py:49
  272.7 9.9 %collective-permute-start.49 = (bf16[48,4352]{1,0:T(8,128)(2,1)S(1)}, bf16[48,4352]{1,0:T(8,128)(2,1)S(1)}, u32[]{:S(2)}, u32[]{:S(2)}) collective-permute-start(bf16[48,4352]{1,0:T(8,128)(2,1)S(1)} %get-tuple-element.199), channel_id=1, source_target_pairs={{0,8},{1,9},{2,10},{3,11},{4,12},{5,13},{6,14},{7,15},{8,0},{9,1},... | collective-permute-start | bytes 1253384 | tf_op jit(solution)/shard_map/ppermute | solution.py:49
  279.8 10.2 %collective-permute-start.48 = (bf16[96,3200]{1,0:T(8,128)(2,1)S(1)}, bf16[96,3200]{1,0:T(8,128)(2,1)S(1)}, u32[]{:S(2)}, u32[]{:S(2)}) collective-permute-start(bf16[96,3200]{1,0:T(8,128)(2,1)S(1)} %get-tuple-element.196), channel_id=1, source_target_pairs={{0,4},{1,5},{2,3},{3,2},{4,0},{5,1},{6,7},{7,6},{8,12},{9,13},{10,... | collective-permute-start | bytes 1843208 | tf_op jit(solution)/shard_map/ppermute | solution.py:49
  282.7 10.0 %collective-permute-start.52 = (bf16[24,4352]{1,0:T(8,128)(2,1)S(1)}, bf16[24,4352]{1,0:T(8,128)(2,1)S(1)}, u32[]{:S(2)}, u32[]{:S(2)}) collective-permute-start(bf16[24,4352]{1,0:T(8,128)(2,1)S(1)} %add_convert_fusion.13), channel_id=1, source_target_pairs={{0,16},{1,17},{2,18},{3,19},{4,20},{5,21},{6,22},{7,23},{8,24},{9,... | collective-permute-start | bytes 626696 | tf_op jit(solution)/shard_map/ppermute | solution.py:49
  290.2 9.1 %collective-permute-start.50 = (bf16[48,3200]{1,0:T(8,128)(2,1)S(1)}, bf16[48,3200]{1,0:T(8,128)(2,1)S(1)}, u32[]{:S(2)}, u32[]{:S(2)}) collective-permute-start(bf16[48,3200]{1,0:T(8,128)(2,1)S(1)} %get-tuple-element.201), channel_id=1, source_target_pairs={{0,8},{1,9},{2,10},{3,11},{4,12},{5,13},{6,14},{7,15},{8,0},{9,1},... | collective-permute-start | bytes 921608 | tf_op jit(solution)/shard_map/ppermute | solution.py:49
  299.3 8.5 %collective-permute-start.51 = (bf16[24,3200]{1,0:T(8,128)(2,1)S(1)}, bf16[24,3200]{1,0:T(8,128)(2,1)S(1)}, u32[]{:S(2)}, u32[]{:S(2)}) collective-permute-start(bf16[24,3200]{1,0:T(8,128)(2,1)S(1)} %add_convert_fusion.22), channel_id=1, source_target_pairs={{0,16},{1,17},{2,18},{3,19},{4,20},{5,21},{6,22},{7,23},{8,24},{9,... | collective-permute-start | bytes 460808 | tf_op jit(solution)/shard_map/ppermute | solution.py:49
  (41 other events, 306.4 us)
Sparse Core Ops, SparseCore 0:
  55.1 52.4 all-gather.1
  167.1 28.9 reduce-scatter.2
  213.1 28.8 reduce-scatter.4

commit v4 on v3

--- a/solution.py
+++ b/solution.py
@@ -706,7 +706,8 @@
     query_rows, text_rows = items * NQ, items * (item_rows - NQ)
     ff = planes * ff_each
     order = place_of_slot(width)
-    flat = hidden.reshape(rows, width)
+    features = with_layout_constraint(features, Layout((0, 1, 2)))
+    flat = after(hidden.reshape(rows, width), features)
 
     vectors = (self_bias, norm_gain, norm_bias, cross_bias, reduce_bias)
     n_vectors = sum(v.shape[0] for v in vectors)

time: 324 us -> 325 us (level)
  waiting for transfers between devices: 119 us -> 109 us
  starting transfers between devices: 31.9 us -> 41 us
    ppermute x53, waiting for transfers between devices: 119 us -> 109 us  [swap(): return lax.ppermute(value, AXES, pairs(count, move))]
    ppermute x53, starting transfers between devices: 31.5 us -> 40.7 us  [swap(): return lax.ppermute(value, AXES, pairs(count, move))]
    unnamed x79 -> x83, local copies, waits for them, and re-layouts: 12.2 us -> 14.2 us
  transfers between devices with their start and end apart: 56 -> 56, of which waited for: 28 -> 27; matrix products, arithmetic and copies ran while one was open for 10% -> 10% of each run, Pallas kernels for 30% -> 30%
where the time goes in v4:
time: 325 us; the launch traced here: 321 us
  Pallas kernels  110 us (34%)
  waiting for transfers between devices  109 us (34%)
  starting transfers between devices  41 us (13%)
  other arithmetic  25.7 us (8%)
  local copies, waits for them, and re-layouts  19.3 us (6%)
  between operations  15 us (5%)
    pallas_call x15, Pallas kernels, kernel_call(): pl.pallas_call(lambda *refs: body(refs), name=name, out_shape=outs, in_sp...  110 us
    ppermute x53, waiting for transfers between devices, swap(): return lax.ppermute(value, AXES, pairs(count, move))  109 us
    ppermute x53, starting transfers between devices, swap(): return lax.ppermute(value, AXES, pairs(count, move))  40.7 us
    convert_element_type x16, other arithmetic, add_low(): return (left.astype(F32) + right.astype(F32)).astype(BF)  15.8 us
    unnamed x83, local copies, waits for them, and re-layouts  14.2 us
  transfers between devices with their start and end apart: 56, of which 27 were waited for; matrix products, arithmetic and copies ran while one was open for 10% of the time, Pallas kernels for 30%

profile of v4, /device:TPU:0, one launch (start us, length us, event | category | flops | bytes accessed | tf_op | source)
XLA Modules:
  0.0 320.6 jit_solution(2733699444147220552)
XLA Ops:
  7.3 2.2 pack.1
  9.4 5.1 %collective-permute-start.2 = (bf16[24,3200]{1,0:T(8,128)(2,1)}, bf16[24,3200]{1,0:T(8,128)(2,1)S(1)}, u32[]{:S(2)}, u32[]{:S(2)}) collective-permute-start(bf16[24,3200]{1,0:T(8,128)(2,1)} %get-tuple-element.89), channel_id=1, source_target_pairs={{0,24},{1,25},{2,26},{3,27},{4,28},{5,29},{6,30},{7,31},{8,16},{9,... | collective-permute-start | bytes 460808 | tf_op jit(solution)/shard_map/ppermute | solution.py:49
  16.1 11.6 %collective-permute-done = bf16[24,3200]{1,0:T(8,128)(2,1)S(1)} collective-permute-done((bf16[24,3200]{1,0:T(8,128)(2,1)}, bf16[24,3200]{1,0:T(8,128)(2,1)S(1)}, u32[]{:S(2)}, u32[]{:S(2)}) %collective-permute-start) | collective-permute-done | bytes 153632 | tf_op jit(solution)/shard_map/ppermute | solution.py:49
  27.8 1.6 collective-permute-start.4
  29.4 1.5 collective-permute-start.3
  31.3 10.3 %collective-permute-done.10 = bf16[24,4352]{1,0:T(8,128)(2,1)S(1)} collective-permute-done((bf16[24,4352]{1,0:T(8,128)(2,1)S(1)}, bf16[24,4352]{1,0:T(8,128)(2,1)S(1)}, u32[]{:S(2)}, u32[]{:S(2)}) %collective-permute-start.10) | collective-permute-done | bytes 208928 | tf_op jit(solution)/shard_map/ppermute | solution.py:49
  42.9 1.5 collective-permute-start.5
  44.4 8.8 %collective-permute-done.11 = bf16[48,4352]{1,0:T(8,128)(2,1)S(1)} collective-permute-done((bf16[48,4352]{1,0:T(8,128)(2,1)S(1)}, bf16[48,4352]{1,0:T(8,128)(2,1)S(1)}, u32[]{:S(2)}, u32[]{:S(2)}) %collective-permute-start.11) | collective-permute-done | bytes 417824 | tf_op jit(solution)/shard_map/ppermute | solution.py:49
  58.4 12.5 %collective-permute-done.12.refs_4_.refs_6_.refs_10_ = bf16[96,4352]{1,0:T(8,128)(2,1)} collective-permute-done((bf16[96,4352]{1,0:T(8,128)(2,1)S(1)}, bf16[96,4352]{1,0:T(8,128)(2,1)}, u32[]{:S(2)}, u32[]{:S(2)}) %collective-permute-start.12) | collective-permute-done | bytes 835616 | tf_op jit(solution)/shard_map/ppermute | solution.py:49
  71.5 8.6 %self_forward.1 = (bf16[128,2304]{1,0:T(8,128)(2,1)}, bf16[128,768]{1,0:T(8,128)(2,1)}, f32[128,768]{1,0:T(8,128)}, f32[64,768]{1,0:T(8,128)}, f32[64,768]{1,0:T...) custom-call(s32[2]{0:T(128)} %refs_0_.5, bf16[128,768]{1,0:T(8,128)(2,1)} %bitcast.46, ...), custom_call_target="tpu_custom_call" | custom-call | flops 10800000000 | bytes 36000000 | tf_op jit(solution)/shard_map/self_forward/pallas_call | solution.py:667
  80.2 3.6 %collective-permute-done.14.refs_6_.refs_8_.refs_12_ = bf16[96,4352]{1,0:T(8,128)(2,1)} collective-permute-done((bf16[96,4352]{1,0:T(8,128)(2,1)}, bf16[96,4352]{1,0:T(8,128)(2,1)}, u32[]{:S(2)}, u32[]{:S(2)}) %collective-permute-start.14) | collective-permute-done | bytes 835616 | tf_op jit(solution)/shard_map/ppermute | solution.py:49
  87.4 10.2 %image_rows.1 = (bf16[2,257,768]{2,1,0:T(8,128)(2,1)}, bf16[2,257,768]{2,1,0:T(8,128)(2,1)}) custom-call(bf16[2,257,1408]{2,1,0:T(8,128)(2,1)} %copy.40.refs_0_.refs_6_, bf16[768,768]{1,0:T(8,128)(2,1)} %fusion.refs_2_.refs_1_.refs_3_.refs_7_.refs_9_, f32[16,768]{1,0:T(8,128)} %get-tuple-element.91.refs_2_.refs_4_.refs_8_.refs_10_, ...), custom_call_target="tpu_custom_call" | custom-call | flops 10800000000 | bytes 36000000 | tf_op jit(solution)/shard_map/image_rows/pallas_call | solution.py:667
  98.3 8.0 %cross_forward.1 = (bf16[64,768]{1,0:T(8,128)(2,1)}, bf16[64,768]{1,0:T(8,128)(2,1)}, f32[64,768]{1,0:T(8,128)}, f32[64,768]{1,0:T(8,128)}, bf16[64,768]{1,0:T(8,128)(2,1)}) custom-call(f32[64,768]{1,0:T(8,128)} %get-tuple-element.90.refs_0_.refs_4_, bf16[2,257,768]{2,1,0:T(8,128)(2,1)} %get-tuple-element.96.refs_1_.refs_5_, ...), custom_call_target="tpu_custom_call" | custom-call | flops 10800000000 | bytes 36000000 | tf_op jit(solution)/shard_map/cross_forward/pallas_call | solution.py:667
  106.4 1.6 collective-permute-start.19
  108.0 3.3 %collective-permute-done.19 = bf16[64,768]{1,0:T(8,128)(2,1)S(1)} collective-permute-done((bf16[64,768]{1,0:T(8,128)(2,1)}, bf16[64,768]{1,0:T(8,128)(2,1)S(1)}, u32[]{:S(2)}, u32[]{:S(2)}) %collective-permute-start.19) | collective-permute-done | bytes 98336 | tf_op jit(solution)/shard_map/ppermute | solution.py:49
  112.2 1.6 collective-permute-start.20
  114.5 5.0 %branch_up_1.1 = (f32[512,384]{1,0:T(8,128)}, bf16[512,384]{1,0:T(8,128)(2,1)}, f32[256,768]{1,0:T(8,128)}, bf16[256,768]{1,0:T(8,128)(2,1)}) custom-call(bf16[256,768]{1,0:T(8,128)(2,1)} %copy-done.21, bf16[256,768]{1,0:T(8,128)(2,1)} %copy-done.27, bf16[384,3328]{1,0:T(8,128)(2,1)} %all-gather.2.cloned.1.call-done.refs_2_.refs_6_), custom_call_target="tpu_custom_call" | custom-call | flops 10800000000 | bytes 36000000 | tf_op jit(solution)/shard_map/branch_up_1/pallas_call | solution.py:667
  124.1 4.9 %branch_up_0.1 = (f32[512,384]{1,0:T(8,128)}, bf16[512,384]{1,0:T(8,128)(2,1)}, f32[256,768]{1,0:T(8,128)}, bf16[256,768]{1,0:T(8,128)(2,1)}) custom-call(bf16[256,768]{1,0:T(8,128)(2,1)} %copy-done.6, bf16[256,768]{1,0:T(8,128)(2,1)} %copy-done.28, bf16[384,3328]{1,0:T(8,128)(2,1)} %all-gather.2.cloned.1.call-done.refs_2_.refs_6_), custom_call_target="tpu_custom_call" | custom-call | flops 10800000000 | bytes 36000000 | tf_op jit(solution)/shard_map/branch_up_0/pallas_call | solution.py:667
  135.8 2.2 branch_end_1.1
  140.6 2.1 collective-permute-done.37
  145.0 2.2 branch_end_0.1
  147.2 1.5 collective-permute-start.31
  148.7 3.3 %collective-permute-done.31 = bf16[64,768]{1,0:T(8,128)(2,1)S(1)} collective-permute-done((bf16[64,768]{1,0:T(8,128)(2,1)}, bf16[64,768]{1,0:T(8,128)(2,1)S(1)}, u32[]{:S(2)}, u32[]{:S(2)}) %collective-permute-start.31) | collective-permute-done | bytes 98336 | tf_op jit(solution)/shard_map/ppermute | solution.py:49
  154.5 4.3 %collective-permute-done.32 = bf16[128,768]{1,0:T(8,128)(2,1)S(1)} collective-permute-done((bf16[128,768]{1,0:T(8,128)(2,1)S(1)}, bf16[128,768]{1,0:T(8,128)(2,1)S(1)}, u32[]{:S(2)}, u32[]{:S(2)}) %collective-permute-start.32) | collective-permute-done | bytes 196640 | tf_op jit(solution)/shard_map/ppermute | solution.py:49
  160.7 6.0 %branch_down_1.1 = (f32[256,768]{1,0:T(8,128)}, bf16[256,768]{1,0:T(8,128)(2,1)}, bf16[384,1664]{1,0:T(8,128)(2,1)}) custom-call(bf16[256,768]{1,0:T(8,128)(2,1)} %copy-done.8, bf16[256,768]{1,0:T(8,128)(2,1)} %copy-done.30, bf16[256,768]{1,0:T(8,128)(2,1)} %copy-done.21, bf16[256,768]{1,0:T(8,128)(2,1)} %copy-done.27, ...), custom_call_target="tpu_custom_call" | custom-call | flops 10800000000 | bytes 36000000 | tf_op jit(solution)/shard_map/branch_down_1/pallas_call | solution.py:667
  168.2 6.2 %branch_down_0.1 = (f32[256,768]{1,0:T(8,128)}, bf16[256,768]{1,0:T(8,128)(2,1)}, bf16[384,1664]{1,0:T(8,128)(2,1)}) custom-call(bf16[256,768]{1,0:T(8,128)(2,1)} %copy-done.7, bf16[256,768]{1,0:T(8,128)(2,1)} %copy-done.29, bf16[256,768]{1,0:T(8,128)(2,1)} %copy-done.6, bf16[256,768]{1,0:T(8,128)(2,1)} %copy-done.28, ...), custom_call_target="tpu_custom_call" | custom-call | flops 10800000000 | bytes 36000000 | tf_op jit(solution)/shard_map/branch_down_0/pallas_call | solution.py:667
  177.8 2.5 collective-permute-done.41
  185.6 2.1 collective-permute-done.36.refs_1_
  188.4 10.9 %cross_backward.1 = (bf16[64,768]{1,0:T(8,128)(2,1)}, bf16[2,257,768]{2,1,0:T(8,128)(2,1)}, bf16[2,257,768]{2,1,0:T(8,128)(2,1)}, bf16[64,768]{1,0:T(8,128)(2,1)}, f32[64,768]{1,0:T(8,128)}, /*index=5*/f32[8,768]{1,0:T(8,128)}) custom-call(bf16[64,768]{1,0:T(8,128)(2,1)} %get-tuple-element.223.refs_0_, bf16[64,768]{1,0:T(8,128)(2,1)} %copy-done.33, ...), custom_call_target="tpu_custom_call" | custom-call | flops 3600000000 | bytes 12000000 | tf_op jit(solution)/shard_map/cross_backward/pallas_call | solution.py:667
  199.3 13.2 %cross_weights.1 = (bf16[384,4352]{1,0:T(8,128)(2,1)}, bf16[384,4352]{1,0:T(8,128)(2,1)}) custom-call(bf16[64,768]{1,0:T(8,128)(2,1)} %get-tuple-element.128.refs_0_, bf16[2,257,768]{2,1,0:T(8,128)(2,1)} %get-tuple-element.129.refs_1_.refs_0_, bf16[2,257,768]{2,1,0:T(8,128)(2,1)} %get-tuple-element.130.refs_2_.refs_1_, ...), custom_call_target="tpu_custom_call" | custom-call | flops 3600000000 | bytes 12000000 | tf_op jit(solution)/shard_map/cross_weights/pallas_call | solution.py:667
  212.6 10.0 %feature_grad.1 = f32[2,257,1408]{2,1,0:T(8,128)} custom-call(bf16[2,257,768]{2,1,0:T(8,128)(2,1)} %get-tuple-element.129.refs_1_.refs_0_, bf16[2,257,768]{2,1,0:T(8,128)(2,1)} %get-tuple-element.130.refs_2_.refs_1_, bf16[768,768]{1,0:T(8,128)(2,1)} %fusion.refs_2_.refs_1_.refs_3_.refs_7_.refs_9_, bf16[96,4352]{1,0:T(8,128)(2,1)} %copy-done.17, ...), custom_call_target="tpu_custom_call" | custom-call | flops 3600000000 | bytes 12000000 | tf_op jit(solution)/shard_map/feature_grad/pallas_call | solution.py:667
  222.6 1.7 copy-done
  224.3 3.9 %add_convert_fusion = (bf16[192,4352]{1,0:T(8,128)(2,1)S(1)}, bf16[192,4352]{1,0:T(8,128)(2,1)S(1)}) fusion(bf16[384,4352]{1,0:T(8,128)(2,1)} %copy-done, bf16[384,4352]{1,0:T(8,128)(2,1)} %get-tuple-element.133), kind=kLoop, calls=%fused_computation | loop fusion | flops 6684672 | bytes 10027008 | tf_op jit(solution)/shard_map/convert_element_type | solution.py:93
  229.5 3.1 copy.41
  232.6 14.6 %self_backward.1 = (bf16[128,2304]{1,0:T(8,128)(2,1)}, f32[128,768]{1,0:T(8,128)}, bf16[384,3200]{1,0:T(8,128)(2,1)}, bf16[384,3200]{1,0:T(8,128)(2,1)}) custom-call(s32[2]{0:T(128)} %refs_0_.5, f32[64,768]{1,0:T(8,128)} %get-tuple-element.137.refs_1_, bf16[64,768]{1,0:T(8,128)(2,1)} %get-tuple-element.220.refs_2_, bf16[64,768]{1,0:T(8,128)(2,1)} %copy-done.31, ...), custom_call_target="tpu_custom_call" | custom-call | flops 3600000000 | bytes 12000000 | tf_op jit(solution)/shard_map/self_backward/pallas_call | solution.py:667
  247.2 2.6 collective-permute-done.44
  250.6 1.9 add_convert_fusion.4
  252.5 1.5 collective-permute-start.47
  254.7 1.6 add_convert_fusion.2
  257.6 6.4 %hidden_grad.1 = f32[128,768]{1,0:T(8,128)} custom-call(bf16[128,2304]{1,0:T(8,128)(2,1)} %get-tuple-element.145.refs_0_, f32[128,768]{1,0:T(8,128)} %get-tuple-element.146.refs_1_, bf16[768,768]{1,0:T(8,128)(2,1)} %fusion.refs_2_.refs_1_.refs_3_.refs_7_.refs_9_, bf16[96,3200]{1,0:T(8,128)(2,1)} %copy-done.18, ...), custom_call_target="tpu_custom_call" | custom-call | flops 3600000000 | bytes 12000000 | tf_op jit(solution)/shard_map/hidden_grad/pallas_call | solution.py:667
  264.0 6.9 %collective-permute-done.47 = bf16[96,4352]{1,0:T(8,128)(2,1)} collective-permute-done((bf16[96,4352]{1,0:T(8,128)(2,1)S(1)}, bf16[96,4352]{1,0:T(8,128)(2,1)}, u32[]{:S(2)}, u32[]{:S(2)}) %collective-permute-start.47) | collective-permute-done | bytes 835616 | tf_op jit(solution)/shard_map/ppermute | solution.py:49
  272.6 5.3 %collective-permute-done.46 = bf16[192,3200]{1,0:T(8,128)(2,1)} collective-permute-done((bf16[192,3200]{1,0:T(8,128)(2,1)}, bf16[192,3200]{1,0:T(8,128)(2,1)}, u32[]{:S(2)}, u32[]{:S(2)}) %collective-permute-start.46) | collective-permute-done | bytes 1228832 | tf_op jit(solution)/shard_map/ppermute | solution.py:49
  277.9 1.5 add_convert_fusion.6
  279.4 1.5 collective-permute-start.48
  282.7 7.0 %collective-permute-done.48 = bf16[96,3200]{1,0:T(8,128)(2,1)S(1)} collective-permute-done((bf16[96,3200]{1,0:T(8,128)(2,1)S(1)}, bf16[96,3200]{1,0:T(8,128)(2,1)S(1)}, u32[]{:S(2)}, u32[]{:S(2)}) %collective-permute-start.48) | collective-permute-done | bytes 614432 | tf_op jit(solution)/shard_map/ppermute | solution.py:49
  290.1 3.1 collective-permute-done.52
  294.7 5.0 %collective-permute-done.50 = bf16[48,3200]{1,0:T(8,128)(2,1)S(1)} collective-permute-done((bf16[48,3200]{1,0:T(8,128)(2,1)S(1)}, bf16[48,3200]{1,0:T(8,128)(2,1)S(1)}, u32[]{:S(2)}, u32[]{:S(2)}) %collective-permute-start.50) | collective-permute-done | bytes 307232 | tf_op jit(solution)/shard_map/ppermute | solution.py:49
  302.6 6.2 %collective-permute-done.51 = bf16[24,3200]{1,0:T(8,128)(2,1)S(1)} collective-permute-done((bf16[24,3200]{1,0:T(8,128)(2,1)S(1)}, bf16[24,3200]{1,0:T(8,128)(2,1)S(1)}, u32[]{:S(2)}, u32[]{:S(2)}) %collective-permute-start.51) | collective-permute-done | bytes 153632 | tf_op jit(solution)/shard_map/ppermute | solution.py:49
  (219 shorter events, 63.5 us)
Async XLA Ops:
  7.2 106.6 %all-gather.2.cloned.1.call-start = ((), (), s32[]{:S(2)}) async-start(), calls=%async_computation.2 | async-start | bytes 3194880 | tf_op jit(solution)/shard_map/all_gather | solution.py:727
  9.4 18.3 %collective-permute-start.2 = (bf16[24,3200]{1,0:T(8,128)(2,1)}, bf16[24,3200]{1,0:T(8,128)(2,1)S(1)}, u32[]{:S(2)}, u32[]{:S(2)}) collective-permute-start(bf16[24,3200]{1,0:T(8,128)(2,1)} %get-tuple-element.89), channel_id=1, source_target_pairs={{0,24},{1,25},{2,26},{3,27},{4,28},{5,29},{6,30},{7,31},{8,16},{9,... | collective-permute-start | bytes 460808 | tf_op jit(solution)/shard_map/ppermute | solution.py:49
  14.5 13.2 %collective-permute-start.1 = (bf16[24,3200]{1,0:T(8,128)(2,1)}, bf16[24,3200]{1,0:T(8,128)(2,1)S(1)}, u32[]{:S(2)}, u32[]{:S(2)}) collective-permute-start(bf16[24,3200]{1,0:T(8,128)(2,1)} %get-tuple-element.89), channel_id=1, source_target_pairs={{0,8},{1,9},{2,10},{3,11},{4,12},{5,13},{6,14},{7,15},{8,0},{9,1},... | collective-permute-start | bytes 460808 | tf_op jit(solution)/shard_map/ppermute | solution.py:49
  14.5 13.2 %collective-permute-start = (bf16[24,3200]{1,0:T(8,128)(2,1)}, bf16[24,3200]{1,0:T(8,128)(2,1)S(1)}, u32[]{:S(2)}, u32[]{:S(2)}) collective-permute-start(bf16[24,3200]{1,0:T(8,128)(2,1)} %get-tuple-element.89), channel_id=1, source_target_pairs={{0,16},{1,17},{2,18},{3,19},{4,20},{5,21},{6,22},{7,23},{8,24},{9,... | collective-permute-start | bytes 460808 | tf_op jit(solution)/shard_map/ppermute | solution.py:49
  27.8 25.5 %collective-permute-start.4 = (bf16[96,3200]{1,0:T(8,128)(2,1)S(1)}, bf16[96,3200]{1,0:T(8,128)(2,1)S(1)}, u32[]{:S(2)}, u32[]{:S(2)}) collective-permute-start(bf16[96,3200]{1,0:T(8,128)(2,1)S(1)} %constant_dynamic-update-slice_fusion.refs_3_.refs_14_), channel_id=1, source_target_pairs={{0,1},{1,0},{2,6},{3,7},{4,5},{5,4},{6,2},{7,3},{8,9},{9,8},{10,14... | collective-permute-start | bytes 1843208 | tf_op jit(solution)/shard_map/ppermute | solution.py:49
  29.4 13.5 %collective-permute-start.3 = (bf16[96,3200]{1,0:T(8,128)(2,1)S(1)}, bf16[96,3200]{1,0:T(8,128)(2,1)}, u32[]{:S(2)}, u32[]{:S(2)}) collective-permute-start(bf16[96,3200]{1,0:T(8,128)(2,1)S(1)} %constant_dynamic-update-slice_fusion.refs_3_.refs_14_), channel_id=1, source_target_pairs={{0,4},{1,5},{2,3},{3,2},{4,0},{5,1},{6,7},{7,6},{8,12},{9,13},{10,... | collective-permute-start | bytes 1843208 | tf_op jit(solution)/shard_map/ppermute | solution.py:49
  30.9 10.7 %collective-permute-start.10 = (bf16[24,4352]{1,0:T(8,128)(2,1)S(1)}, bf16[24,4352]{1,0:T(8,128)(2,1)S(1)}, u32[]{:S(2)}, u32[]{:S(2)}) collective-permute-start(bf16[24,4352]{1,0:T(8,128)(2,1)S(1)} %pad_maximum_fusion.8), channel_id=1, source_target_pairs={{0,16},{1,17},{2,18},{3,19},{4,20},{5,21},{6,22},{7,23},{8,24},{9,... | collective-permute-start | bytes 626696 | tf_op jit(solution)/shard_map/ppermute | solution.py:49
  41.6 11.6 %collective-permute-start.11 = (bf16[48,4352]{1,0:T(8,128)(2,1)S(1)}, bf16[48,4352]{1,0:T(8,128)(2,1)S(1)}, u32[]{:S(2)}, u32[]{:S(2)}) collective-permute-start(bf16[48,4352]{1,0:T(8,128)(2,1)S(1)} %pad_maximum_fusion.2), channel_id=1, source_target_pairs={{0,8},{1,9},{2,10},{3,11},{4,12},{5,13},{6,14},{7,15},{8,0},{9,1},... | collective-permute-start | bytes 1253384 | tf_op jit(solution)/shard_map/ppermute | solution.py:49
  42.9 11.5 %collective-permute-start.5 = (bf16[96,3200]{1,0:T(8,128)(2,1)}, bf16[96,3200]{1,0:T(8,128)(2,1)}, u32[]{:S(2)}, u32[]{:S(2)}) collective-permute-start(bf16[96,3200]{1,0:T(8,128)(2,1)} %collective-permute-done.3.refs_4_.refs_15_), channel_id=1, source_target_pairs={{0,1},{1,0},{2,6},{3,7},{4,5},{5,4},{6,2},{7,3},{8,9},{9,8},{10,14... | collective-permute-start | bytes 1843208 | tf_op jit(solution)/shard_map/ppermute | solution.py:49
  53.3 17.6 %collective-permute-start.12 = (bf16[96,4352]{1,0:T(8,128)(2,1)S(1)}, bf16[96,4352]{1,0:T(8,128)(2,1)}, u32[]{:S(2)}, u32[]{:S(2)}) collective-permute-start(bf16[96,4352]{1,0:T(8,128)(2,1)S(1)} %constant_dynamic-update-slice_fusion.4.refs_3_.refs_5_.refs_9_), channel_id=1, source_target_pairs={{0,4},{1,5},{2,3},{3,2},{4,0},{5,1},{6,7},{7,6},{8,12},{9,13},{10,... | collective-permute-start | bytes 2506760 | tf_op jit(solution)/shard_map/ppermute | solution.py:49
  54.4 16.5 %collective-permute-start.7 = (bf16[96,3200]{1,0:T(8,128)(2,1)}, bf16[96,3200]{1,0:T(8,128)(2,1)}, u32[]{:S(2)}, u32[]{:S(2)}) collective-permute-start(bf16[96,3200]{1,0:T(8,128)(2,1)} %collective-permute-done.3.refs_4_.refs_15_), channel_id=1, source_target_pairs={{0,2},{1,3},{2,0},{3,1},{4,6},{5,7},{6,4},{7,5},{8,10},{9,11},{10,... | collective-permute-start | bytes 1843208 | tf_op jit(solution)/shard_map/ppermute | solution.py:49
  54.4 17.0 %collective-permute-start.9 = (bf16[96,3200]{1,0:T(8,128)(2,1)}, bf16[96,3200]{1,0:T(8,128)(2,1)}, u32[]{:S(2)}, u32[]{:S(2)}) collective-permute-start(bf16[96,3200]{1,0:T(8,128)(2,1)} %collective-permute-done.5.refs_6_.refs_17_), channel_id=1, source_target_pairs={{0,2},{1,3},{2,0},{3,1},{4,6},{5,7},{6,4},{7,5},{8,10},{9,11},{10,... | collective-permute-start | bytes 1843208 | tf_op jit(solution)/shard_map/ppermute | solution.py:49
  55.0 144.4 %reduce-scatter.3.cloned.1.call-start = ((), (), s32[]{:S(2)}) async-start(), calls=%async_computation.3 | async-start | bytes 1597440 | tf_op jit(solution)/shard_map/reduce_scatter | solution.py:821
  57.8 27.7 %collective-permute-start.15 = (bf16[96,4352]{1,0:T(8,128)(2,1)S(1)}, bf16[96,4352]{1,0:T(8,128)(2,1)S(1)}, u32[]{:S(2)}, u32[]{:S(2)}) collective-permute-start(bf16[96,4352]{1,0:T(8,128)(2,1)S(1)} %constant_dynamic-update-slice_fusion.4.refs_3_.refs_5_.refs_9_), channel_id=1, source_target_pairs={{0,2},{1,3},{2,0},{3,1},{4,6},{5,7},{6,4},{7,5},{8,10},{9,11},{10,... | collective-permute-start | bytes 2506760 | tf_op jit(solution)/shard_map/ppermute | solution.py:49
  57.9 22.3 %collective-permute-start.13 = (bf16[96,4352]{1,0:T(8,128)(2,1)S(1)}, bf16[96,4352]{1,0:T(8,128)(2,1)S(1)}, u32[]{:S(2)}, u32[]{:S(2)}) collective-permute-start(bf16[96,4352]{1,0:T(8,128)(2,1)S(1)} %constant_dynamic-update-slice_fusion.4.refs_3_.refs_5_.refs_9_), channel_id=1, source_target_pairs={{0,1},{1,0},{2,6},{3,7},{4,5},{5,4},{6,2},{7,3},{8,9},{9,8},{10,14... | collective-permute-start | bytes 2506760 | tf_op jit(solution)/shard_map/ppermute | solution.py:49
  71.0 14.6 %collective-permute-start.16 = (bf16[96,4352]{1,0:T(8,128)(2,1)}, bf16[96,4352]{1,0:T(8,128)(2,1)}, u32[]{:S(2)}, u32[]{:S(2)}) collective-permute-start(bf16[96,4352]{1,0:T(8,128)(2,1)} %collective-permute-done.12.refs_4_.refs_6_.refs_10_), channel_id=1, source_target_pairs={{0,2},{1,3},{2,0},{3,1},{4,6},{5,7},{6,4},{7,5},{8,10},{9,11},{10,... | collective-permute-start | bytes 2506760 | tf_op jit(solution)/shard_map/ppermute | solution.py:49
  71.0 12.8 %collective-permute-start.14 = (bf16[96,4352]{1,0:T(8,128)(2,1)}, bf16[96,4352]{1,0:T(8,128)(2,1)}, u32[]{:S(2)}, u32[]{:S(2)}) collective-permute-start(bf16[96,4352]{1,0:T(8,128)(2,1)} %collective-permute-done.12.refs_4_.refs_6_.refs_10_), channel_id=1, source_target_pairs={{0,1},{1,0},{2,6},{3,7},{4,5},{5,4},{6,2},{7,3},{8,9},{9,8},{10,14... | collective-permute-start | bytes 2506760 | tf_op jit(solution)/shard_map/ppermute | solution.py:49
  80.1 5.4 %collective-permute-start.17 = (bf16[96,4352]{1,0:T(8,128)(2,1)S(1)}, bf16[96,4352]{1,0:T(8,128)(2,1)S(1)}, u32[]{:S(2)}, u32[]{:S(2)}) collective-permute-start(bf16[96,4352]{1,0:T(8,128)(2,1)S(1)} %collective-permute-done.13.refs_5_.refs_7_.refs_11_), channel_id=1, source_target_pairs={{0,2},{1,3},{2,0},{3,1},{4,6},{5,7},{6,4},{7,5},{8,10},{9,11},{10,... | collective-permute-start | bytes 2506760 | tf_op jit(solution)/shard_map/ppermute | solution.py:49
  84.0 13.6 %collective-permute-start.25 = (bf16[64,768]{1,0:T(8,128)(2,1)}, bf16[64,768]{1,0:T(8,128)(2,1)S(1)}, u32[]{:S(2)}, u32[]{:S(2)}) collective-permute-start(bf16[64,768]{1,0:T(8,128)(2,1)} %get-tuple-element.104), channel_id=1, source_target_pairs={{0,4},{1,5},{2,3},{3,2},{4,0},{5,1},{6,7},{7,6},{8,12},{9,13},{10,... | collective-permute-start | bytes 294920 | tf_op jit(solution)/shard_map/ppermute | solution.py:49
  97.7 8.6 %collective-permute-start.26 = (bf16[128,768]{1,0:T(8,128)(2,1)S(1)}, bf16[128,768]{1,0:T(8,128)(2,1)S(1)}, u32[]{:S(2)}, u32[]{:S(2)}) collective-permute-start(bf16[128,768]{1,0:T(8,128)(2,1)S(1)} %pad_maximum_fusion.10), channel_id=1, source_target_pairs={{0,1},{1,0},{2,6},{3,7},{4,5},{5,4},{6,2},{7,3},{8,9},{9,8},{10,14... | collective-permute-start | bytes 589832 | tf_op jit(solution)/shard_map/ppermute | solution.py:49
  106.3 7.4 %collective-permute-start.27 = (bf16[256,768]{1,0:T(8,128)(2,1)S(1)}, bf16[256,768]{1,0:T(8,128)(2,1)S(1)}, u32[]{:S(2)}, u32[]{:S(2)}) collective-permute-start(bf16[256,768]{1,0:T(8,128)(2,1)S(1)} %constant_dynamic-update-slice_fusion.7.refs_0_.refs_2_), channel_id=1, source_target_pairs={{0,2},{1,3},{2,0},{3,1},{4,6},{5,7},{6,4},{7,5},{8,10},{9,11},{10,... | collective-permute-start | bytes 1179656 | tf_op jit(solution)/shard_map/ppermute | solution.py:49
  106.4 4.9 %collective-permute-start.19 = (bf16[64,768]{1,0:T(8,128)(2,1)}, bf16[64,768]{1,0:T(8,128)(2,1)S(1)}, u32[]{:S(2)}, u32[]{:S(2)}) collective-permute-start(bf16[64,768]{1,0:T(8,128)(2,1)} %get-tuple-element.98), channel_id=1, source_target_pairs={{0,4},{1,5},{2,3},{3,2},{4,0},{5,1},{6,7},{7,6},{8,12},{9,13},{10,... | collective-permute-start | bytes 294920 | tf_op jit(solution)/shard_map/ppermute | solution.py:49
  112.2 7.4 %collective-permute-start.20 = (bf16[128,768]{1,0:T(8,128)(2,1)S(1)}, bf16[128,768]{1,0:T(8,128)(2,1)S(1)}, u32[]{:S(2)}, u32[]{:S(2)}) collective-permute-start(bf16[128,768]{1,0:T(8,128)(2,1)S(1)} %pad_maximum_fusion.9), channel_id=1, source_target_pairs={{0,1},{1,0},{2,6},{3,7},{4,5},{5,4},{6,2},{7,3},{8,9},{9,8},{10,14... | collective-permute-start | bytes 589832 | tf_op jit(solution)/shard_map/ppermute | solution.py:49
  122.7 7.1 %collective-permute-start.29 = (bf16[128,768]{1,0:T(8,128)(2,1)S(1)}, bf16[128,768]{1,0:T(8,128)(2,1)S(1)}, u32[]{:S(2)}, u32[]{:S(2)}) collective-permute-start(bf16[128,768]{1,0:T(8,128)(2,1)S(1)} %get-tuple-element.211), channel_id=1, source_target_pairs={{0,1},{1,0},{2,6},{3,7},{4,5},{5,4},{6,2},{7,3},{8,9},{9,8},{10,14... | collective-permute-start | bytes 589832 | tf_op jit(solution)/shard_map/ppermute | solution.py:49
  130.5 4.6 %collective-permute-start.30 = (bf16[64,768]{1,0:T(8,128)(2,1)S(1)}, bf16[64,768]{1,0:T(8,128)(2,1)S(1)}, u32[]{:S(2)}, u32[]{:S(2)}) collective-permute-start(bf16[64,768]{1,0:T(8,128)(2,1)S(1)} %get-tuple-element.226), channel_id=1, source_target_pairs={{0,4},{1,5},{2,3},{3,2},{4,0},{5,1},{6,7},{7,6},{8,12},{9,13},{10,... | collective-permute-start | bytes 294920 | tf_op jit(solution)/shard_map/ppermute | solution.py:49
  132.6 6.0 %collective-permute-start.23 = (bf16[128,768]{1,0:T(8,128)(2,1)S(1)}, bf16[128,768]{1,0:T(8,128)(2,1)S(1)}, u32[]{:S(2)}, u32[]{:S(2)}) collective-permute-start(bf16[128,768]{1,0:T(8,128)(2,1)S(1)} %get-tuple-element.209), channel_id=1, source_target_pairs={{0,1},{1,0},{2,6},{3,7},{4,5},{5,4},{6,2},{7,3},{8,9},{9,8},{10,14... | collective-permute-start | bytes 589832 | tf_op jit(solution)/shard_map/ppermute | solution.py:49
  137.9 4.8 %collective-permute-start.37 = (bf16[64,768]{1,0:T(8,128)(2,1)}, bf16[64,768]{1,0:T(8,128)(2,1)S(1)}, u32[]{:S(2)}, u32[]{:S(2)}) collective-permute-start(bf16[64,768]{1,0:T(8,128)(2,1)} %get-tuple-element.116), channel_id=1, source_target_pairs={{0,4},{1,5},{2,3},{3,2},{4,0},{5,1},{6,7},{7,6},{8,12},{9,13},{10,... | collective-permute-start | bytes 294920 | tf_op jit(solution)/shard_map/ppermute | solution.py:49
  139.3 5.1 %collective-permute-start.24 = (bf16[64,768]{1,0:T(8,128)(2,1)S(1)}, bf16[64,768]{1,0:T(8,128)(2,1)S(1)}, u32[]{:S(2)}, u32[]{:S(2)}) collective-permute-start(bf16[64,768]{1,0:T(8,128)(2,1)S(1)} %get-tuple-element.224), channel_id=1, source_target_pairs={{0,4},{1,5},{2,3},{3,2},{4,0},{5,1},{6,7},{7,6},{8,12},{9,13},{10,... | collective-permute-start | bytes 294920 | tf_op jit(solution)/shard_map/ppermute | solution.py:49
  143.6 8.4 %collective-permute-start.38 = (bf16[128,768]{1,0:T(8,128)(2,1)S(1)}, bf16[128,768]{1,0:T(8,128)(2,1)S(1)}, u32[]{:S(2)}, u32[]{:S(2)}) collective-permute-start(bf16[128,768]{1,0:T(8,128)(2,1)S(1)} %pad_maximum_fusion.13), channel_id=1, source_target_pairs={{0,1},{1,0},{2,6},{3,7},{4,5},{5,4},{6,2},{7,3},{8,9},{9,8},{10,14... | collective-permute-start | bytes 589832 | tf_op jit(solution)/shard_map/ppermute | solution.py:49
  147.2 4.8 %collective-permute-start.31 = (bf16[64,768]{1,0:T(8,128)(2,1)}, bf16[64,768]{1,0:T(8,128)(2,1)S(1)}, u32[]{:S(2)}, u32[]{:S(2)}) collective-permute-start(bf16[64,768]{1,0:T(8,128)(2,1)} %get-tuple-element.111), channel_id=1, source_target_pairs={{0,4},{1,5},{2,3},{3,2},{4,0},{5,1},{6,7},{7,6},{8,12},{9,13},{10,... | collective-permute-start | bytes 294920 | tf_op jit(solution)/shard_map/ppermute | solution.py:49
  152.1 7.8 %collective-permute-start.39 = (bf16[256,768]{1,0:T(8,128)(2,1)S(1)}, bf16[256,768]{1,0:T(8,128)(2,1)S(1)}, u32[]{:S(2)}, u32[]{:S(2)}) collective-permute-start(bf16[256,768]{1,0:T(8,128)(2,1)S(1)} %pad_maximum_fusion.5.refs_0_), channel_id=1, source_target_pairs={{0,2},{1,3},{2,0},{3,1},{4,6},{5,7},{6,4},{7,5},{8,10},{9,11},{10,... | collective-permute-start | bytes 1179656 | tf_op jit(solution)/shard_map/ppermute | solution.py:49
  153.1 5.7 %collective-permute-start.32 = (bf16[128,768]{1,0:T(8,128)(2,1)S(1)}, bf16[128,768]{1,0:T(8,128)(2,1)S(1)}, u32[]{:S(2)}, u32[]{:S(2)}) collective-permute-start(bf16[128,768]{1,0:T(8,128)(2,1)S(1)} %pad_maximum_fusion.12), channel_id=1, source_target_pairs={{0,1},{1,0},{2,6},{3,7},{4,5},{5,4},{6,2},{7,3},{8,9},{9,8},{10,14... | collective-permute-start | bytes 589832 | tf_op jit(solution)/shard_map/ppermute | solution.py:49
  159.8 7.7 %collective-permute-start.33 = (bf16[256,768]{1,0:T(8,128)(2,1)S(1)}, bf16[256,768]{1,0:T(8,128)(2,1)S(1)}, u32[]{:S(2)}, u32[]{:S(2)}) collective-permute-start(bf16[256,768]{1,0:T(8,128)(2,1)S(1)} %pad_maximum_fusion.4.refs_0_), channel_id=1, source_target_pairs={{0,2},{1,3},{2,0},{3,1},{4,6},{5,7},{6,4},{7,5},{8,10},{9,11},{10,... | collective-permute-start | bytes 1179656 | tf_op jit(solution)/shard_map/ppermute | solution.py:49
  166.7 83.2 %reduce-scatter.5.cloned.1.call-start = ((), (), s32[]{:S(2)}) async-start(), calls=%async_computation.4 | async-start | bytes 1597440 | tf_op jit(solution)/shard_map/reduce_scatter | solution.py:821
  167.0 7.5 %collective-permute-start.40 = (bf16[256,768]{1,0:T(8,128)(2,1)}, bf16[256,768]{1,0:T(8,128)(2,1)S(1)}, u32[]{:S(2)}, u32[]{:S(2)}) collective-permute-start(bf16[256,768]{1,0:T(8,128)(2,1)} %get-tuple-element.120), channel_id=1, source_target_pairs={{0,2},{1,3},{2,0},{3,1},{4,6},{5,7},{6,4},{7,5},{8,10},{9,11},{10,... | collective-permute-start | bytes 1179656 | tf_op jit(solution)/shard_map/ppermute | solution.py:49
  174.6 5.7 %collective-permute-start.41 = (bf16[128,768]{1,0:T(8,128)(2,1)S(1)}, bf16[128,768]{1,0:T(8,128)(2,1)S(1)}, u32[]{:S(2)}, u32[]{:S(2)}) collective-permute-start(bf16[128,768]{1,0:T(8,128)(2,1)S(1)} %get-tuple-element.205), channel_id=1, source_target_pairs={{0,1},{1,0},{2,6},{3,7},{4,5},{5,4},{6,2},{7,3},{8,9},{9,8},{10,14... | collective-permute-start | bytes 589832 | tf_op jit(solution)/shard_map/ppermute | solution.py:49
  176.5 5.9 %collective-permute-start.35 = (bf16[128,768]{1,0:T(8,128)(2,1)S(1)}, bf16[128,768]{1,0:T(8,128)(2,1)S(1)}, u32[]{:S(2)}, u32[]{:S(2)}) collective-permute-start(bf16[128,768]{1,0:T(8,128)(2,1)S(1)} %get-tuple-element.207), channel_id=1, source_target_pairs={{0,1},{1,0},{2,6},{3,7},{4,5},{5,4},{6,2},{7,3},{8,9},{9,8},{10,14... | collective-permute-start | bytes 589832 | tf_op jit(solution)/shard_map/ppermute | solution.py:49
  181.0 4.6 %collective-permute-start.42 = (bf16[64,768]{1,0:T(8,128)(2,1)S(1)}, bf16[64,768]{1,0:T(8,128)(2,1)S(1)}, u32[]{:S(2)}, u32[]{:S(2)}) collective-permute-start(bf16[64,768]{1,0:T(8,128)(2,1)S(1)} %get-tuple-element.221), channel_id=1, source_target_pairs={{0,4},{1,5},{2,3},{3,2},{4,0},{5,1},{6,7},{7,6},{8,12},{9,13},{10,... | collective-permute-start | bytes 294920 | tf_op jit(solution)/shard_map/ppermute | solution.py:49
  212.6 10.0 %collective-permute-start.43 = (bf16[384,4352]{1,0:T(8,128)(2,1)}, bf16[384,4352]{1,0:T(8,128)(2,1)S(1)}, u32[]{:S(2)}, u32[]{:S(2)}) collective-permute-start(bf16[384,4352]{1,0:T(8,128)(2,1)} %get-tuple-element.134), channel_id=1, source_target_pairs={{0,2},{1,3},{2,0},{3,1},{4,6},{5,7},{6,4},{7,5},{8,10},{9,11},{10,... | collective-permute-start | bytes 10027016 | tf_op jit(solution)/shard_map/ppermute | solution.py:49
  228.2 21.6 %collective-permute-start.44 = (bf16[192,4352]{1,0:T(8,128)(2,1)S(1)}, bf16[192,4352]{1,0:T(8,128)(2,1)}, u32[]{:S(2)}, u32[]{:S(2)}) collective-permute-start(bf16[192,4352]{1,0:T(8,128)(2,1)S(1)} %get-tuple-element.193), channel_id=1, source_target_pairs={{0,1},{1,0},{2,6},{3,7},{4,5},{5,4},{6,2},{7,3},{8,9},{9,8},{10,14... | collective-permute-start | bytes 5013512 | tf_op jit(solution)/shard_map/ppermute | solution.py:49
  249.9 4.9 %collective-permute-start.45 = (bf16[384,3200]{1,0:T(8,128)(2,1)}, bf16[384,3200]{1,0:T(8,128)(2,1)S(1)}, u32[]{:S(2)}, u32[]{:S(2)}) collective-permute-start(bf16[384,3200]{1,0:T(8,128)(2,1)} %get-tuple-element.151), channel_id=1, source_target_pairs={{0,2},{1,3},{2,0},{3,1},{4,6},{5,7},{6,4},{7,5},{8,10},{9,11},{10,... | collective-permute-start | bytes 7372808 | tf_op jit(solution)/shard_map/ppermute | solution.py:49
  252.5 18.5 %collective-permute-start.47 = (bf16[96,4352]{1,0:T(8,128)(2,1)S(1)}, bf16[96,4352]{1,0:T(8,128)(2,1)}, u32[]{:S(2)}, u32[]{:S(2)}) collective-permute-start(bf16[96,4352]{1,0:T(8,128)(2,1)S(1)} %get-tuple-element.196), channel_id=1, source_target_pairs={{0,4},{1,5},{2,3},{3,2},{4,0},{5,1},{6,7},{7,6},{8,12},{9,13},{10,... | collective-permute-start | bytes 2506760 | tf_op jit(solution)/shard_map/ppermute | solution.py:49
  256.4 21.5 %collective-permute-start.46 = (bf16[192,3200]{1,0:T(8,128)(2,1)}, bf16[192,3200]{1,0:T(8,128)(2,1)}, u32[]{:S(2)}, u32[]{:S(2)}) collective-permute-start(bf16[192,3200]{1,0:T(8,128)(2,1)} %get-tuple-element.195), channel_id=1, source_target_pairs={{0,1},{1,0},{2,6},{3,7},{4,5},{5,4},{6,2},{7,3},{8,9},{9,8},{10,14... | collective-permute-start | bytes 3686408 | tf_op jit(solution)/shard_map/ppermute | solution.py:49
  272.3 9.9 %collective-permute-start.49 = (bf16[48,4352]{1,0:T(8,128)(2,1)S(1)}, bf16[48,4352]{1,0:T(8,128)(2,1)S(1)}, u32[]{:S(2)}, u32[]{:S(2)}) collective-permute-start(bf16[48,4352]{1,0:T(8,128)(2,1)S(1)} %get-tuple-element.201), channel_id=1, source_target_pairs={{0,8},{1,9},{2,10},{3,11},{4,12},{5,13},{6,14},{7,15},{8,0},{9,1},... | collective-permute-start | bytes 1253384 | tf_op jit(solution)/shard_map/ppermute | solution.py:49
  279.4 10.2 %collective-permute-start.48 = (bf16[96,3200]{1,0:T(8,128)(2,1)S(1)}, bf16[96,3200]{1,0:T(8,128)(2,1)S(1)}, u32[]{:S(2)}, u32[]{:S(2)}) collective-permute-start(bf16[96,3200]{1,0:T(8,128)(2,1)S(1)} %get-tuple-element.198), channel_id=1, source_target_pairs={{0,4},{1,5},{2,3},{3,2},{4,0},{5,1},{6,7},{7,6},{8,12},{9,13},{10,... | collective-permute-start | bytes 1843208 | tf_op jit(solution)/shard_map/ppermute | solution.py:49
  282.3 10.9 %collective-permute-start.52 = (bf16[24,4352]{1,0:T(8,128)(2,1)S(1)}, bf16[24,4352]{1,0:T(8,128)(2,1)S(1)}, u32[]{:S(2)}, u32[]{:S(2)}) collective-permute-start(bf16[24,4352]{1,0:T(8,128)(2,1)S(1)} %add_convert_fusion.13), channel_id=1, source_target_pairs={{0,16},{1,17},{2,18},{3,19},{4,20},{5,21},{6,22},{7,23},{8,24},{9,... | collective-permute-start | bytes 626696 | tf_op jit(solution)/shard_map/ppermute | solution.py:49
  289.8 9.9 %collective-permute-start.50 = (bf16[48,3200]{1,0:T(8,128)(2,1)S(1)}, bf16[48,3200]{1,0:T(8,128)(2,1)S(1)}, u32[]{:S(2)}, u32[]{:S(2)}) collective-permute-start(bf16[48,3200]{1,0:T(8,128)(2,1)S(1)} %get-tuple-element.203), channel_id=1, source_target_pairs={{0,8},{1,9},{2,10},{3,11},{4,12},{5,13},{6,14},{7,15},{8,0},{9,1},... | collective-permute-start | bytes 921608 | tf_op jit(solution)/shard_map/ppermute | solution.py:49
  299.8 9.0 %collective-permute-start.51 = (bf16[24,3200]{1,0:T(8,128)(2,1)S(1)}, bf16[24,3200]{1,0:T(8,128)(2,1)S(1)}, u32[]{:S(2)}, u32[]{:S(2)}) collective-permute-start(bf16[24,3200]{1,0:T(8,128)(2,1)S(1)} %add_convert_fusion.22), channel_id=1, source_target_pairs={{0,16},{1,17},{2,18},{3,19},{4,20},{5,21},{6,22},{7,23},{8,24},{9,... | collective-permute-start | bytes 460808 | tf_op jit(solution)/shard_map/ppermute | solution.py:49
  (43 other events, 251.9 us)
Sparse Core Ops, SparseCore 0:
  55.1 53.1 all-gather.1
  166.8 29.1 reduce-scatter.2
  212.7 29.0 reduce-scatter.4
